TPU v7x, 32 devices: a whole 2x2x4 slice. The times are simulated.
32 devices in a mesh: dp: 2 (over core), ctx: 4 (over y, x), tensor: 4 (over z).
Axes of the slice: x: 2, y: 2, z: 4, core: 2. Of those that a mesh axis runs over, the one named last changes fastest.
Arguments:
- tokens: bfloat16 [2, 2, 1024, 2304], P(None, 'dp', 'ctx'), may hold values from -6 to 6
- span_order: int32 [8], replicated, may hold values from 0 to 7, as said below
- w_query: bfloat16 [2304, 2048], P(('dp', 'ctx'), 'tensor'), may hold values from -0.125 to 0.125
- w_key: bfloat16 [2304, 1024], P(('dp', 'ctx'), 'tensor'), may hold values from -0.125 to 0.125
- value_weight: bfloat16 [2304, 1024], P(('dp', 'ctx'), 'tensor'), may hold values from -0.125 to 0.125
- w_out: bfloat16 [2304, 2048], P(('dp', 'ctx'), 'tensor'), may hold values from -1 to 1
- w_gate: bfloat16 [2304, 9216], P(('dp', 'ctx'), 'tensor'), may hold values from -0.125 to 0.125
- w_up: bfloat16 [2304, 9216], P(('dp', 'ctx'), 'tensor'), may hold values from -0.125 to 0.125
- w_down: bfloat16 [2304, 9216], P(('dp', 'ctx'), 'tensor'), may hold values from -0.0625 to 0.0625
- gain_attn_in: bfloat16 [2304], P(('dp', 'ctx')), may hold values from -0.5 to 0.5
- gain_attn_out: bfloat16 [2304], P(('dp', 'ctx')), may hold values from -0.5 to 0.5
- gain_ffn_in: bfloat16 [2304], P(('dp', 'ctx')), may hold values from -0.5 to 0.5
- gain_ffn_out: bfloat16 [2304], P(('dp', 'ctx')), may hold values from -0.5 to 0.5
- cotangent: bfloat16 [2, 2, 1024, 2304], P(None, 'dp', 'ctx'), may hold values from -6 to 6
Outputs:
- block_out: bfloat16 [2, 2, 1024, 2304], P(None, 'dp', 'ctx')
- grad_tokens: bfloat16 [2, 2, 1024, 2304], P(None, 'dp', 'ctx')
- grad_w_query: float32 [2304, 2048], P(('dp', 'ctx'), 'tensor')
- grad_w_key: float32 [2304, 1024], P(('dp', 'ctx'), 'tensor')
- grad_w_value: float32 [2304, 1024], P(('dp', 'ctx'), 'tensor')
- grad_w_out: float32 [2304, 2048], P(('dp', 'ctx'), 'tensor')
- grad_w_gate: float32 [2304, 9216], P(('dp', 'ctx'), 'tensor')
- grad_w_up: float32 [2304, 9216], P(('dp', 'ctx'), 'tensor')
- grad_w_down: float32 [2304, 9216], P(('dp', 'ctx'), 'tensor')
- grad_gain_attn_in: float32 [2304], P(('dp', 'ctx'))
- grad_gain_attn_out: float32 [2304], P(('dp', 'ctx'))
- grad_gain_ffn_in: float32 [2304], P(('dp', 'ctx'))
- grad_gain_ffn_out: float32 [2304], P(('dp', 'ctx'))
Inputs may be any that keep to these rules, and one draw needn't show every extreme that they name: `span_order`: the two slots 2 c and 2 c + 1 hold spans k and 7 - k for some k, in either order; every span appears in exactly one slot.
All inputs are finite; a program needn't handle non-finite values.
Results may differ from a plain program's by a relative error of at most 0.017.
Values may be sent and summed in bfloat16 or wider, within the bound.
No kernel may reach another device: no remote copies, remote signals or barrier semaphores. Data moves between devices by JAX's collectives and lax.ppermute only.
A program may use at most 256 MiB of HBM per device.

v0:
```python
import jax
import jax.numpy as jnp
from jax import lax
from jax.sharding import PartitionSpec as P

MODEL_DIM = 2304
HEAD_SIZE = 256


EPS = 1e-06
CAP = 50.0
BASE = 10000.0


def apply_norm(values):
    factor = lax.rsqrt(jnp.mean(values * values, axis=-1, keepdims=True) + EPS)
    return (values * factor, factor)


def norm_backward(upstream, scaled, factor):
    return factor * (upstream - scaled * jnp.mean(upstream * scaled, axis=-1, keepdims=True))


def rotation(token_positions, width_size):
    half_width = width_size // 2
    inverse = BASE ** (-(jnp.arange(half_width, dtype=jnp.float32) * 2.0) / width_size)
    angles = token_positions.astype(jnp.float32)[:, None] * inverse[None, :]
    return (jnp.cos(angles)[:, None, :], jnp.sin(angles)[:, None, :])


def apply_rotary(values, cosine, sine_table):
    half_width = values.shape[-1] // 2
    leading = values[..., :half_width]
    trailing = values[..., half_width:]
    return jnp.concatenate(
        [leading * cosine - trailing * sine_table, trailing * cosine + leading * sine_table],
        axis=-1,
    )


def capped_weights(query_matrix, key_rows, query_pos, key_pos):
    raw = jnp.einsum(
        "bthgd,bshd->bhgts", query_matrix, key_rows, preferred_element_type=jnp.float32
    ) * query_matrix.shape[-1] ** (-0.5)
    capped = CAP * jnp.tanh(raw / CAP)
    allowed = key_pos[None, :] <= query_pos[:, None]
    return (capped, jnp.where(allowed, jnp.exp(capped), 0.0))


def geglu(gate_lin, up_lin):
    return jax.nn.gelu(gate_lin, approximate=True) * up_lin


def project_out(left, matrix):
    return jnp.einsum("rk,dk->rd", left, matrix, preferred_element_type=jnp.float32)


def weight_grad(left, right):
    return jnp.einsum("rd,rk->dk", left, right, preferred_element_type=jnp.float32)


def local(
    tokens,
    span_order,
    w_query,
    w_key,
    value_weight,
    w_out,
    w_gate,
    w_up,
    w_down,
    gain_attn_in,
    gain_attn_out,
    gain_ffn_in,
    gain_ffn_out,
    cotangent,
):
    micro_count, batch_count, seq_dev, model_width = tokens.shape
    seq_length = seq_dev * lax.axis_size("ctx")
    span_len = seq_length // span_order.shape[0]
    row_index = jnp.arange(seq_length, dtype=jnp.int32)
    key_pos = span_order[row_index // span_len] * span_len + row_index % span_len
    query_pos = lax.dynamic_slice_in_dim(key_pos, lax.axis_index("ctx") * seq_dev, seq_dev)
    head_dim = HEAD_SIZE
    kv_local = w_key.shape[1] // head_dim
    q_local = w_query.shape[1] // head_dim
    group_size = q_local // kv_local
    token_rows = batch_count * seq_dev
    softness = head_dim ** (-0.5)
    cosine, sine_table = rotation(query_pos, head_dim)
    matrices = (w_query, w_key, value_weight, w_out, w_gate, w_up, w_down)
    grad_mats = [jnp.zeros((MODEL_DIM, matrix.shape[1]), jnp.float32) for matrix in matrices]
    gain_gradients = [jnp.zeros((MODEL_DIM,), jnp.float32) for counter in range(4)]
    outputs = []
    input_grads = []
    for micro_step in range(micro_count):
        full_query, full_key, full_value, full_out, gathered_one, gathered_two = (
            lax.all_gather(w_query, ("dp", "ctx"), axis=0, tiled=True),
            lax.all_gather(w_key, ("dp", "ctx"), axis=0, tiled=True),
            lax.all_gather(value_weight, ("dp", "ctx"), axis=0, tiled=True),
            lax.all_gather(w_out, ("dp", "ctx"), axis=0, tiled=True),
            lax.all_gather(gain_attn_in, ("dp", "ctx"), axis=0, tiled=True),
            lax.all_gather(gain_attn_out, ("dp", "ctx"), axis=0, tiled=True),
        )
        input_scale = 1.0 + gathered_one.astype(jnp.float32)
        scale_attn = 1.0 + gathered_two.astype(jnp.float32)
        input_rows = tokens[micro_step].astype(jnp.float32).reshape(token_rows, model_width)
        normalized_input, input_factor = apply_norm(input_rows)
        normed_input = (normalized_input * input_scale).astype(jnp.bfloat16)
        query_lin = jnp.dot(normed_input, full_query, preferred_element_type=jnp.float32)
        key_linear = jnp.dot(normed_input, full_key, preferred_element_type=jnp.float32)
        value_rows = (
            jnp.dot(normed_input, full_value, preferred_element_type=jnp.float32)
            .astype(jnp.bfloat16)
            .reshape(batch_count, seq_dev, kv_local, head_dim)
        )
        query_matrix = (
            apply_rotary(
                query_lin.reshape(batch_count, seq_dev, q_local, head_dim), cosine, sine_table
            )
            .astype(jnp.bfloat16)
            .reshape(batch_count, seq_dev, kv_local, group_size, head_dim)
        )
        key_rows = apply_rotary(
            key_linear.reshape(batch_count, seq_dev, kv_local, head_dim), cosine, sine_table
        ).astype(jnp.bfloat16)
        capped_part, weight_part = capped_weights(
            query_matrix, lax.all_gather(key_rows, "ctx", axis=1, tiled=True), query_pos, key_pos
        )
        added = jnp.einsum(
            "bhgts,bshd->bthgd",
            weight_part.astype(jnp.bfloat16),
            lax.all_gather(value_rows, "ctx", axis=1, tiled=True),
            preferred_element_type=jnp.float32,
        )
        denominator = jnp.sum(weight_part, axis=-1)
        den_rows = jnp.transpose(denominator, (0, 3, 1, 2))[..., None]
        head_output = added / den_rows
        attended = head_output.astype(jnp.bfloat16).reshape(token_rows, q_local * head_dim)
        attn_out = lax.psum(project_out(attended, full_out), "tensor")
        ahat, factor_attn = apply_norm(attn_out)
        hidden_one = input_rows + ahat * scale_attn
        full_gate, full_up, full_down, gathered_three, gathered_four = (
            lax.all_gather(w_gate, ("dp", "ctx"), axis=0, tiled=True),
            lax.all_gather(w_up, ("dp", "ctx"), axis=0, tiled=True),
            lax.all_gather(w_down, ("dp", "ctx"), axis=0, tiled=True),
            lax.all_gather(gain_ffn_in, ("dp", "ctx"), axis=0, tiled=True),
            lax.all_gather(gain_ffn_out, ("dp", "ctx"), axis=0, tiled=True),
        )
        scale_mid = 1.0 + gathered_three.astype(jnp.float32)
        scale_out = 1.0 + gathered_four.astype(jnp.float32)
        h1hat, factor_mid = apply_norm(hidden_one)
        normed_two = (h1hat * scale_mid).astype(jnp.bfloat16)
        gate_lin = jnp.dot(normed_two, full_gate, preferred_element_type=jnp.float32)
        up_lin = jnp.dot(normed_two, full_up, preferred_element_type=jnp.float32)
        hidden, geglu_back = jax.vjp(geglu, gate_lin, up_lin)
        hidden_low = hidden.astype(jnp.bfloat16)
        ffn_out = lax.psum(project_out(hidden_low, full_down), "tensor")
        fhat, factor_out = apply_norm(ffn_out)
        outputs.append(
            (hidden_one + fhat * scale_out)
            .astype(jnp.bfloat16)
            .reshape(batch_count, seq_dev, model_width)
        )
        upstream = cotangent[micro_step].astype(jnp.float32).reshape(token_rows, model_width)
        gain_gradients[3] = gain_gradients[3] + jnp.sum(upstream * fhat, axis=0)
        ffn_grad = norm_backward(upstream * scale_out, fhat, factor_out).astype(jnp.bfloat16)
        back_query, back_key, back_value, back_out, back_gate, back_up, back_down = (
            lax.all_gather(w_query, ("dp", "ctx"), axis=0, tiled=True),
            lax.all_gather(w_key, ("dp", "ctx"), axis=0, tiled=True),
            lax.all_gather(value_weight, ("dp", "ctx"), axis=0, tiled=True),
            lax.all_gather(w_out, ("dp", "ctx"), axis=0, tiled=True),
            lax.all_gather(w_gate, ("dp", "ctx"), axis=0, tiled=True),
            lax.all_gather(w_up, ("dp", "ctx"), axis=0, tiled=True),
            lax.all_gather(w_down, ("dp", "ctx"), axis=0, tiled=True),
        )
        hidden_grad = jnp.dot(ffn_grad, back_down, preferred_element_type=jnp.float32)
        grad_mats[6] = grad_mats[6] + weight_grad(ffn_grad, hidden_low)
        gate_grad, up_grad = geglu_back(hidden_grad)
        gate_grad = gate_grad.astype(jnp.bfloat16)
        up_grad = up_grad.astype(jnp.bfloat16)
        grad_mats[4] = grad_mats[4] + weight_grad(normed_two, gate_grad)
        grad_mats[5] = grad_mats[5] + weight_grad(normed_two, up_grad)
        mid_grad = lax.psum(
            project_out(gate_grad, back_gate) + project_out(up_grad, back_up), "tensor"
        )
        gain_gradients[2] = gain_gradients[2] + jnp.sum(mid_grad * h1hat, axis=0)
        single_gradient = upstream + norm_backward(mid_grad * scale_mid, h1hat, factor_mid)
        gain_gradients[1] = gain_gradients[1] + jnp.sum(single_gradient * ahat, axis=0)
        attn_grad = norm_backward(single_gradient * scale_attn, ahat, factor_attn).astype(
            jnp.bfloat16
        )
        grad_mats[3] = grad_mats[3] + weight_grad(attn_grad, attended)
        heads_grad = jnp.dot(attn_grad, back_out, preferred_element_type=jnp.float32).reshape(
            batch_count, seq_dev, kv_local, group_size, head_dim
        )
        every_key, every_value = (
            lax.all_gather(key_rows, "ctx", axis=1, tiled=True),
            lax.all_gather(value_rows, "ctx", axis=1, tiled=True),
        )
        capped, weight = capped_weights(query_matrix, every_key, query_pos, key_pos)
        scaled_grad = (heads_grad / den_rows).astype(jnp.bfloat16)
        row_dot = jnp.transpose(jnp.sum(heads_grad * head_output, axis=-1), (0, 2, 3, 1))
        prob_grad = jnp.einsum(
            "bthgd,bshd->bhgts", scaled_grad, every_value, preferred_element_type=jnp.float32
        )
        capped_grad = weight * (prob_grad - (row_dot / denominator)[..., None])
        ratio = capped / CAP
        score_grad = (capped_grad * (1.0 - ratio * ratio)).astype(jnp.bfloat16)
        query_grad = (
            jnp.einsum(
                "bhgts,bshd->bthgd", score_grad, every_key, preferred_element_type=jnp.float32
            )
            * softness
        )
        key_terms = (
            jnp.einsum(
                "bhgts,bthgd->bshd", score_grad, query_matrix, preferred_element_type=jnp.float32
            )
            * softness
        )
        value_terms = jnp.einsum(
            "bhgts,bthgd->bshd",
            weight.astype(jnp.bfloat16),
            scaled_grad,
            preferred_element_type=jnp.float32,
        )
        key_grad, value_grad = (
            lax.psum_scatter(key_terms, "ctx", scatter_dimension=1, tiled=True),
            lax.psum_scatter(value_terms, "ctx", scatter_dimension=1, tiled=True),
        )
        query_back = (
            apply_rotary(
                query_grad.reshape(batch_count, seq_dev, q_local, head_dim), cosine, -sine_table
            )
            .astype(jnp.bfloat16)
            .reshape(token_rows, q_local * head_dim)
        )
        key_back = (
            apply_rotary(key_grad, cosine, -sine_table)
            .astype(jnp.bfloat16)
            .reshape(token_rows, kv_local * head_dim)
        )
        value_back = value_grad.astype(jnp.bfloat16).reshape(token_rows, kv_local * head_dim)
        grad_mats[0] = grad_mats[0] + weight_grad(normed_input, query_back)
        grad_mats[1] = grad_mats[1] + weight_grad(normed_input, key_back)
        grad_mats[2] = grad_mats[2] + weight_grad(normed_input, value_back)
        in_terms = (
            project_out(query_back, back_query)
            + project_out(key_back, back_key)
            + project_out(value_back, back_value)
        )
        input_gradient = lax.psum(in_terms, "tensor")
        gain_gradients[0] = gain_gradients[0] + jnp.sum(input_gradient * normalized_input, axis=0)
        input_grads.append(
            (
                single_gradient
                + norm_backward(input_gradient * input_scale, normalized_input, input_factor)
            )
            .astype(jnp.bfloat16)
            .reshape(batch_count, seq_dev, model_width)
        )
    shards = (
        lax.psum_scatter(grad_mats[0], ("dp", "ctx"), scatter_dimension=0, tiled=True),
        lax.psum_scatter(grad_mats[1], ("dp", "ctx"), scatter_dimension=0, tiled=True),
        lax.psum_scatter(grad_mats[2], ("dp", "ctx"), scatter_dimension=0, tiled=True),
        lax.psum_scatter(grad_mats[3], ("dp", "ctx"), scatter_dimension=0, tiled=True),
        lax.psum_scatter(grad_mats[4], ("dp", "ctx"), scatter_dimension=0, tiled=True),
        lax.psum_scatter(grad_mats[5], ("dp", "ctx"), scatter_dimension=0, tiled=True),
        lax.psum_scatter(grad_mats[6], ("dp", "ctx"), scatter_dimension=0, tiled=True),
        lax.psum_scatter(gain_gradients[0], ("dp", "ctx"), scatter_dimension=0, tiled=True),
        lax.psum_scatter(gain_gradients[1], ("dp", "ctx"), scatter_dimension=0, tiled=True),
        lax.psum_scatter(gain_gradients[2], ("dp", "ctx"), scatter_dimension=0, tiled=True),
        lax.psum_scatter(gain_gradients[3], ("dp", "ctx"), scatter_dimension=0, tiled=True),
    )
    return (
        jnp.stack(outputs),
        jnp.stack(input_grads),
        shards[0],
        shards[1],
        shards[2],
        shards[3],
        shards[4],
        shards[5],
        shards[6],
        shards[7],
        shards[8],
        shards[9],
        shards[10],
    )


def solution(mesh):
    return jax.shard_map(
        local,
        mesh=mesh,
        in_specs=(
            P(None, "dp", "ctx", None),
            P(),
            P(("dp", "ctx"), "tensor"),
            P(("dp", "ctx"), "tensor"),
            P(("dp", "ctx"), "tensor"),
            P(("dp", "ctx"), "tensor"),
            P(("dp", "ctx"), "tensor"),
            P(("dp", "ctx"), "tensor"),
            P(("dp", "ctx"), "tensor"),
            P(("dp", "ctx")),
            P(("dp", "ctx")),
            P(("dp", "ctx")),
            P(("dp", "ctx")),
            P(None, "dp", "ctx", None),
        ),
        out_specs=(
            P(None, "dp", "ctx", None),
            P(None, "dp", "ctx", None),
            P(("dp", "ctx"), "tensor"),
            P(("dp", "ctx"), "tensor"),
            P(("dp", "ctx"), "tensor"),
            P(("dp", "ctx"), "tensor"),
            P(("dp", "ctx"), "tensor"),
            P(("dp", "ctx"), "tensor"),
            P(("dp", "ctx"), "tensor"),
            P(("dp", "ctx")),
            P(("dp", "ctx")),
            P(("dp", "ctx")),
            P(("dp", "ctx")),
        ),
        check_vma=False,
    )
```

profile of v0, /device:TPU:0, one launch (start us, length us, event | category | flops | bytes accessed | tf_op | source)
XLA Modules:
  0.0 1874.8 jit_solution(5713118970676231675)
XLA Ops:
  17.2 28.8 %all-reduce.13 = (bf16[2304]{0:T(1024)(128)(2,1)S(1)}, bf16[2304]{0:T(1024)(128)(2,1)}, bf16[2304]{0:T(1024)(128)(2,1)}, bf16[2304]{0:T(1024)(128)(2,1)}) all-reduce(bf16[2304]{0:T(1024)(128)(2,1)S(1)} %dynamic-update-slice, bf16[2304]{0:T(1024)(128)(2,1)S(1)} %dynamic-update-slice.1, ...), channel_id=1, replica_groups=mesh['dp'=2,'ctx'=4,'tensor'=4] {'dp','ctx'}, use_global_device_ids=true, to_apply=%add | all-reduce | flops 9216 | bytes 36864
  48.2 4.5 compare_select_fusion.1
  59.2 12.9 all_gather.88
  72.1 17.3 all_gather.34
  91.5 11.1 all-gather
  103.1 12.1 all-gather.1
  115.2 4.3 copy.73
  137.6 168.4 %all-reduce.25.cloned.1.call-done = (f32[256,2304]{1,0:T(8,128)}, f32[256,2304]{1,0:T(8,128)}) async-done(((f32[256,2304]{1,0:T(8,128)}, f32[256,2304]{1,0:T(8,128)}), (f32[256,2304]{1,0:T(8,128)}, f32[256,2304]{1,0:T(8,128)})) %all-reduce.25.cloned.1.call-update) | async-done | bytes 4718608 | tf_op jit(solution)/shard_map/psum | solution.py:140
  314.6 55.8 %all-gather.18.cloned.1.call-done = bf16[2304,2304]{1,0:T(8,128)(2,1)} async-done(((bf16[288,2304]{1,0:T(8,128)(2,1)}), bf16[2304,2304]{1,0:T(8,128)(2,1)}) %all-gather.18.cloned.1.call-update) | async-done | bytes 10616848 | tf_op jit(solution)/shard_map/all_gather | solution.py:144
  370.5 8.8 fusion.217
  379.3 4.3 fusion.220
  383.6 52.4 %all-gather.20.cloned.1.call-done = bf16[2304,2304]{1,0:T(8,128)(2,1)} async-done(((bf16[288,2304]{1,0:T(8,128)(2,1)}), bf16[2304,2304]{1,0:T(8,128)(2,1)}) %all-gather.20.cloned.1.call-update) | async-done | bytes 10616848 | tf_op jit(solution)/shard_map/all_gather | solution.py:145
  436.1 9.9 multiply_convert_fusion.6
  446.0 4.8 multiply_convert_fusion.4
  450.8 50.9 %all-gather.22.cloned.1.call-done = bf16[2304,2304]{1,0:T(8,128)(2,1)} async-done(((bf16[288,2304]{1,0:T(8,128)(2,1)}), bf16[2304,2304]{1,0:T(8,128)(2,1)}) %all-gather.22.cloned.1.call-update) | async-done | bytes 10616848 | tf_op jit(solution)/shard_map/all_gather | solution.py:146
  501.6 9.1 fusion.218
  510.7 4.4 fusion.221
  515.8 171.4 %all-reduce.23.cloned.1.call-done = (f32[256,2304]{1,0:T(8,128)}, f32[256,2304]{1,0:T(8,128)}) async-done(((f32[256,2304]{1,0:T(8,128)}, f32[256,2304]{1,0:T(8,128)}), (f32[256,2304]{1,0:T(8,128)}, f32[256,2304]{1,0:T(8,128)})) %all-reduce.23.cloned.1.call-update) | async-done | bytes 4718608 | tf_op jit(solution)/shard_map/psum | solution.py:158
  697.0 10.4 multiply_convert_fusion.3
  710.5 9.9 multiply_convert_fusion.1
  720.4 4.3 fusion.224
  724.8 8.6 convolution_add_fusion.12
  733.4 8.4 convolution_add_fusion.11
  743.5 169.4 %all-reduce.21.cloned.1.call-done = (f32[256,2304]{1,0:T(8,128)}, f32[256,2304]{1,0:T(8,128)}) async-done(((f32[256,2304]{1,0:T(8,128)}, f32[256,2304]{1,0:T(8,128)}), (f32[256,2304]{1,0:T(8,128)}, f32[256,2304]{1,0:T(8,128)})) %all-reduce.21.cloned.1.call-update) | async-done | bytes 4718608 | tf_op jit(solution)/shard_map/psum | solution.py:184
  913.0 5.6 multiply_reduce_fusion.1
  919.5 5.6 multiply_reduce_fusion.3
  968.4 4.1 fusion.223
  974.7 22.9 %reduce-scatter.12.cloned.1.call-done = f32[1,256,1,256]{1,3,2,0:T(8,128)} async-done(((f32[1,1024,1,256]{1,3,2,0:T(8,128)}), f32[1,256,1,256]{1,3,2,0:T(8,128)}) %reduce-scatter.12.cloned.1.call-update) | async-done | bytes 262160 | tf_op jit(solution)/shard_map/reduce_scatter | solution.py:229
  999.4 4.1 convolution_add_fusion.10
  1005.5 23.0 %reduce-scatter.14.cloned.1.call-done = f32[1,256,1,256]{1,3,2,0:T(8,128)} async-done(((f32[1,1024,1,256]{1,3,2,0:T(8,128)}), f32[1,256,1,256]{1,3,2,0:T(8,128)}) %reduce-scatter.14.cloned.1.call-update) | async-done | bytes 262160 | tf_op jit(solution)/shard_map/reduce_scatter | solution.py:230
  1032.5 26.7 %reduce-scatter.18.cloned.1.call-done = f32[1,256,1,256]{1,3,2,0:T(8,128)} async-done(((f32[1,1024,1,256]{1,3,2,0:T(8,128)}), f32[1,256,1,256]{1,3,2,0:T(8,128)}) %reduce-scatter.18.cloned.1.call-update) | async-done | bytes 262160 | tf_op jit(solution)/shard_map/reduce_scatter | solution.py:230
  1059.2 4.0 convolution_add_fusion.7
  1081.2 11.9 fusion.229
  1093.1 13.5 convolution_add_fusion
  1106.7 12.0 fusion.228
  1118.7 13.7 convolution_add_fusion.1
  1133.0 11.9 fusion.227
  1144.8 14.5 convolution_add_fusion.2
  1164.4 71.0 %all-reduce.19.cloned.1.call-done = (f32[256,2304]{1,0:T(8,128)}, f32[256,2304]{1,0:T(8,128)}) async-done(((f32[256,2304]{1,0:T(8,128)}, f32[256,2304]{1,0:T(8,128)}), (f32[256,2304]{1,0:T(8,128)}, f32[256,2304]{1,0:T(8,128)})) %all-reduce.19.cloned.1.call-update) | async-done | bytes 4718608 | tf_op jit(solution)/shard_map/psum | solution.py:253
  1239.0 28.9 %all-reduce.8 = (f32[2304]{0:T(1024)S(1)}, f32[2304]{0:T(1024)S(1)}, f32[2304]{0:T(1024)S(1)}, f32[2304]{0:T(1024)S(1)}) all-reduce(f32[2304]{0:T(1024)S(1)} %add.330, f32[2304]{0:T(1024)S(1)} %add.331, f32[2304]{0:T(1024)S(1)} %add.332, f32[2304]{0:T(1024)S(1)} %copy-done.83), channel_id=15, replica_groups=mesh['dp'=2,'ctx'=4,'tensor'=4] {'dp','ctx'}, use_global_device_ids=true, to_apply=%region_41.42.clone | all-reduce | flops 9216 | bytes 73728
  1270.6 4.5 fusion.91
  1276.7 4.2 reduce-scatter.24.cloned.1.call-done
  1280.8 46.2 %reduce-scatter.22.cloned.1.call-done = f32[288,256]{1,0:T(8,128)} async-done(((f32[2304,256]{1,0:T(8,128)}), f32[288,256]{1,0:T(8,128)}) %reduce-scatter.22.cloned.1.call-update) | async-done | bytes 294928 | tf_op jit(solution)/shard_map/reduce_scatter | solution.py:265
  1327.0 57.7 %reduce-scatter.26.cloned.1.call-done = f32[288,512]{1,0:T(8,128)} async-done(((f32[2304,512]{1,0:T(8,128)}), f32[288,512]{1,0:T(8,128)}) %reduce-scatter.26.cloned.1.call-update) | async-done | bytes 589840 | tf_op jit(solution)/shard_map/reduce_scatter | solution.py:267
  1384.7 57.8 %reduce-scatter.20.cloned.1.call-done = f32[288,512]{1,0:T(8,128)} async-done(((f32[2304,512]{1,0:T(8,128)}), f32[288,512]{1,0:T(8,128)}) %reduce-scatter.20.cloned.1.call-update) | async-done | bytes 589840 | tf_op jit(solution)/shard_map/reduce_scatter | solution.py:264
  1442.5 141.7 %reduce-scatter.32.cloned.1.call-done = f32[288,2304]{1,0:T(8,128)} async-done(((f32[2304,2304]{1,0:T(8,128)}), f32[288,2304]{1,0:T(8,128)}) %reduce-scatter.32.cloned.1.call-update) | async-done | bytes 2654224 | tf_op jit(solution)/shard_map/reduce_scatter | solution.py:270
  1584.2 141.8 %reduce-scatter.30.cloned.1.call-done = f32[288,2304]{1,0:T(8,128)} async-done(((f32[2304,2304]{1,0:T(8,128)}), f32[288,2304]{1,0:T(8,128)}) %reduce-scatter.30.cloned.1.call-update) | async-done | bytes 2654224 | tf_op jit(solution)/shard_map/reduce_scatter | solution.py:269
  1726.0 141.8 %reduce-scatter.28.cloned.1.call-done = f32[288,2304]{1,0:T(8,128)} async-done(((f32[2304,2304]{1,0:T(8,128)}), f32[288,2304]{1,0:T(8,128)}) %reduce-scatter.28.cloned.1.call-update) | async-done | bytes 2654224 | tf_op jit(solution)/shard_map/reduce_scatter | solution.py:268
  (396 shorter events, 146.2 us)
Async XLA Ops:
  7.2 48.5 %copy-start = (bf16[2,1,256,2304]{3,2,1,0:T(8,128)(2,1)S(1)}, bf16[2,1,256,2304]{3,2,1,0:T(8,128)(2,1)}, u32[]{:S(2)}) copy-start(bf16[2,1,256,2304]{3,2,1,0:T(8,128)(2,1)} %param.14) | copy-start | bytes 7077892
  7.2 48.5 %all-gather.12.cloned.1.call-start = ((), (), s32[]{:S(2)}) async-start(), calls=%async_computation.12 | async-start | bytes 1327104 | tf_op jit(solution)/shard_map/all_gather | solution.py:99
  7.9 81.5 %all-gather.10.cloned.1.call-start = ((), (), s32[]{:S(2)}) async-start(), calls=%async_computation.11 | async-start | bytes 1327104 | tf_op jit(solution)/shard_map/all_gather | solution.py:100
  8.7 106.5 %all-gather.14.cloned.1.call-start = ((), (), s32[]{:S(2)}) async-start(), calls=%async_computation.13 | async-start | bytes 2654208 | tf_op jit(solution)/shard_map/all_gather | solution.py:98
  9.4 118.9 %all-gather.16.cloned.1.call-start = ((), (), s32[]{:S(2)}) async-start(), calls=%async_computation.14 | async-start | bytes 2654208 | tf_op jit(solution)/shard_map/all_gather | solution.py:101
  10.0 296.1 %all-reduce.25.cloned.1.call-start = ((), (), s32[]{:S(2)}) async-start(), calls=%async_computation.32 | async-start | bytes 9437184 | tf_op jit(solution)/shard_map/psum | solution.py:140
  10.1 48.5 %copy-start.108 = (f32[128]{0:T(128)}, f32[128]{0:T(128)S(1)}, u32[]{:S(2)}) copy-start(f32[128]{0:T(128)S(1)} %multiply_power_fusion) | copy-start | bytes 1540
  48.2 10.4 copy-start.86
  55.7 67.5 %copy-start.42 = (f32[256,128]{0,1:T(8,128)}, f32[256,128]{0,1:T(8,128)S(1)}, u32[]{:S(2)}) copy-start(f32[256,128]{0,1:T(8,128)S(1)} %get-tuple-element.108) | copy-start | bytes 393220
  72.1 51.3 %copy-start.28 = (bf16[1,1024,1,256]{1,3,2,0:T(8,128)(2,1)}, bf16[1,1024,1,256]{1,3,2,0:T(8,128)(2,1)S(1)}, u32[]{:S(2)}) copy-start(bf16[1,1024,1,256]{1,3,2,0:T(8,128)(2,1)S(1)} %all_gather.88) | copy-start | bytes 1572868
  89.4 34.6 %copy-start.40 = (bf16[1,1024,1,256]{1,3,2,0:T(8,128)(2,1)}, bf16[1,1024,1,256]{1,3,2,0:T(8,128)(2,1)S(1)}, u32[]{:S(2)}) copy-start(bf16[1,1024,1,256]{1,3,2,0:T(8,128)(2,1)S(1)} %all_gather.34) | copy-start | bytes 1572868
  89.4 13.2 copy-start.29
  89.4 13.2 copy-start.87
  134.7 235.8 %all-gather.18.cloned.1.call-start = ((), (), s32[]{:S(2)}) async-start(), calls=%async_computation.15 | async-start | bytes 11943936 | tf_op jit(solution)/shard_map/all_gather | solution.py:144
  135.3 300.8 %all-gather.20.cloned.1.call-start = ((), (), s32[]{:S(2)}) async-start(), calls=%async_computation.16 | async-start | bytes 11943936 | tf_op jit(solution)/shard_map/all_gather | solution.py:145
  136.0 365.6 %all-gather.22.cloned.1.call-start = ((), (), s32[]{:S(2)}) async-start(), calls=%async_computation.17 | async-start | bytes 11943936 | tf_op jit(solution)/shard_map/all_gather | solution.py:146
  136.8 550.5 %all-reduce.23.cloned.1.call-start = ((), (), s32[]{:S(2)}) async-start(), calls=%async_computation.31 | async-start | bytes 9437184 | tf_op jit(solution)/shard_map/psum | solution.py:158
  137.0 172.0 %copy-start.77 = (f32[2304]{0:T(1024)}, f32[2304]{0:T(1024)S(1)}, u32[]{:S(2)}) copy-start(f32[2304]{0:T(1024)S(1)} %convert_add_fusion.4) | copy-start | bytes 27652
  314.6 131.3 %copy-start.17 = (bf16[256,2304]{1,0:T(8,128)(2,1)}, bf16[256,2304]{1,0:T(8,128)(2,1)S(1)}, u32[]{:S(2)}) copy-start(bf16[256,2304]{1,0:T(8,128)(2,1)S(1)} %get-tuple-element.103) | copy-start | bytes 3538948
  515.1 397.8 %all-reduce.21.cloned.1.call-start = ((), (), s32[]{:S(2)}) async-start(), calls=%async_computation.30 | async-start | bytes 9437184 | tf_op jit(solution)/shard_map/psum | solution.py:184
  694.1 13.3 slice-start
  694.1 13.4 slice-start.1
  697.0 10.4 copy-start.24
  697.0 13.4 copy-start.22
  697.0 10.5 slice-start.2
  707.5 17.3 copy-start.53
  720.4 13.0 copy-start.54
  741.8 171.1 %copy-start.80 = (f32[2304]{0:T(1024)S(1)}, f32[2304]{0:T(1024)}, u32[]{:S(2)}) copy-start(f32[2304]{0:T(1024)} %convert_add_fusion.3) | copy-start | bytes 27652
  741.8 171.1 %copy-start.98 = (f32[256]{0:T(256)S(1)}, f32[256]{0:T(256)}, u32[]{:S(2)}) copy-start(f32[256]{0:T(256)} %copy-done.97) | copy-start | bytes 3076
  741.8 171.1 %copy-start.100 = (f32[256]{0:T(256)S(1)}, f32[256]{0:T(256)}, u32[]{:S(2)}) copy-start(f32[256]{0:T(256)} %copy-done.99) | copy-start | bytes 3076
  741.9 232.9 %reduce-scatter.16.cloned.1.call-start = ((), (), s32[]{:S(2)}) async-start(), calls=%async_computation.20 | async-start | bytes 1310720 | tf_op jit(solution)/shard_map/reduce_scatter | solution.py:229
  939.9 57.7 %reduce-scatter.12.cloned.1.call-start = ((), (), s32[]{:S(2)}) async-start(), calls=%async_computation.18 | async-start | bytes 1310720 | tf_op jit(solution)/shard_map/reduce_scatter | solution.py:229
  956.2 72.3 %reduce-scatter.14.cloned.1.call-start = ((), (), s32[]{:S(2)}) async-start(), calls=%async_computation.19 | async-start | bytes 1310720 | tf_op jit(solution)/shard_map/reduce_scatter | solution.py:230
  959.7 99.5 %reduce-scatter.18.cloned.1.call-start = ((), (), s32[]{:S(2)}) async-start(), calls=%async_computation.21 | async-start | bytes 1310720 | tf_op jit(solution)/shard_map/reduce_scatter | solution.py:230
  967.1 268.3 %all-reduce.19.cloned.1.call-start = ((), (), s32[]{:S(2)}) async-start(), calls=%async_computation.29 | async-start | bytes 9437184 | tf_op jit(solution)/shard_map/psum | solution.py:253
  1063.2 217.6 %reduce-scatter.24.cloned.1.call-start = ((), (), s32[]{:S(2)}) async-start(), calls=%async_computation.24 | async-start | bytes 2654208 | tf_op jit(solution)/shard_map/reduce_scatter | solution.py:266
  1067.1 260.0 %reduce-scatter.22.cloned.1.call-start = ((), (), s32[]{:S(2)}) async-start(), calls=%async_computation.23 | async-start | bytes 2654208 | tf_op jit(solution)/shard_map/reduce_scatter | solution.py:265
  1070.8 313.8 %reduce-scatter.26.cloned.1.call-start = ((), (), s32[]{:S(2)}) async-start(), calls=%async_computation.25 | async-start | bytes 5308416 | tf_op jit(solution)/shard_map/reduce_scatter | solution.py:267
  1075.9 366.6 %reduce-scatter.20.cloned.1.call-start = ((), (), s32[]{:S(2)}) async-start(), calls=%async_computation.22 | async-start | bytes 5308416 | tf_op jit(solution)/shard_map/reduce_scatter | solution.py:264
  1080.9 12.2 copy-start.23
  1080.9 503.3 %reduce-scatter.32.cloned.1.call-start = ((), (), s32[]{:S(2)}) async-start(), calls=%async_computation.28 | async-start | bytes 23887872 | tf_op jit(solution)/shard_map/reduce_scatter | solution.py:270
  1081.2 11.9 copy-start.49
  1106.6 12.1 copy-start.18
  1106.7 619.3 %reduce-scatter.30.cloned.1.call-start = ((), (), s32[]{:S(2)}) async-start(), calls=%async_computation.27 | async-start | bytes 23887872 | tf_op jit(solution)/shard_map/reduce_scatter | solution.py:269
  1106.7 12.0 copy-start.55
  1132.4 735.4 %reduce-scatter.28.cloned.1.call-start = ((), (), s32[]{:S(2)}) async-start(), calls=%async_computation.26 | async-start | bytes 23887872 | tf_op jit(solution)/shard_map/reduce_scatter | solution.py:268
  1133.0 11.9 copy-start.52
  1235.4 35.2 %copy-start.91 = (f32[256]{0:T(256)S(1)}, f32[256]{0:T(256)}, u32[]{:S(2)}) copy-start(f32[256]{0:T(256)} %copy-done.86) | copy-start | bytes 3076
  (93 other events, 313.8 us)
Sparse Core Ops, SparseCore 0:
  9.9 26.8 all-gather.11
  38.7 23.9 all-gather.9
  64.5 32.0 all-gather.13
  98.4 29.0 all-gather.15
  134.8 171.2 all-reduce.24
  307.8 62.6 all-gather.17
  372.3 63.6 all-gather.19
  437.9 63.6 all-gather.21
  515.2 171.9 all-reduce.22
  742.0 170.9 all-reduce.20
  940.0 26.8 reduce-scatter.15
  969.7 27.9 reduce-scatter.11
  1000.5 27.9 reduce-scatter.13
  1031.2 27.9 reduce-scatter.17
  1063.4 171.9 all-reduce.18
  1239.2 41.6 reduce-scatter.23
  1284.6 42.3 reduce-scatter.21
  1330.9 53.7 reduce-scatter.25
  1388.7 53.7 reduce-scatter.19
  1446.5 137.5 reduce-scatter.31
  1588.4 137.5 reduce-scatter.29
  1730.2 137.5 reduce-scatter.27
where the time goes:
time: 1880 us; the launch traced here: 1870 us
  waiting for transfers between devices  1410 us (75%)
  matrix products  242 us (13%)
  blocking collectives  111 us (6%)
  other arithmetic  59.9 us (3%)
  local copies, waits for them, and re-layouts  34.7 us (2%)
    psum x1, waiting for transfers between devices, local(): ffn_out = lax.psum(project_out(hidden_low, full_down), 'tensor')  171 us
    psum x1, waiting for transfers between devices, local(): lax.psum(project_out(gate_grad, back_gate) + project_out(up_grad, back_up...  169 us
    psum x1, waiting for transfers between devices, local(): attn_out = lax.psum(project_out(attended, full_out), 'tensor')  168 us
    reduce_scatter x1, waiting for transfers between devices, local(): lax.psum_scatter(grad_mats[4], ('dp', 'ctx'), scatter_dimension=0, tiled=...  142 us
    reduce_scatter x1, waiting for transfers between devices, local(): lax.psum_scatter(grad_mats[5], ('dp', 'ctx'), scatter_dimension=0, tiled=...  142 us
    reduce_scatter x1, waiting for transfers between devices, local(): lax.psum_scatter(grad_mats[6], ('dp', 'ctx'), scatter_dimension=0, tiled=...  142 us
    dot_general x14, matrix products, weight_grad(): jnp.einsum('rd,rk->dk', left, right, preferred_element_type=jnp.float32)  93.7 us
    psum x1, waiting for transfers between devices, local(): input_gradient = lax.psum(in_terms, 'tensor')  71 us
  transfers between devices with their start and end apart: 22, of which 17 were waited for; matrix products, arithmetic and copies ran while one was open for 12% of the time, Pallas kernels for 0%

commit v1 on v0

v1 whole, which is shorter than its diff:
```python
import functools

import jax
import jax.numpy as jnp
from jax import lax
from jax.experimental import pallas as pl
from jax.experimental.pallas import tpu as pltpu
from jax.sharding import PartitionSpec as P

HEAD_SIZE = 256
EPS = 1e-06
CAP = 50.0
BASE = 10000.0
BF = jnp.bfloat16
F32 = jnp.float32
PAD = 128
VMEM_LIMIT = 60 * 1024 * 1024
GELU_C = 0.7978845608028654
GELU_A = 0.044715


def apply_norm(values):
    factor = lax.rsqrt(jnp.mean(values * values, axis=-1, keepdims=True) + EPS)
    return values * factor, factor


def norm_backward(upstream, scaled, factor):
    return factor * (upstream - scaled * jnp.mean(upstream * scaled, axis=-1, keepdims=True))


def rotation(token_positions, width_size):
    half_width = width_size // 2
    inverse = BASE ** (-(jnp.arange(half_width, dtype=F32) * 2.0) / width_size)
    angles = token_positions.astype(F32)[:, None] * inverse[None, :]
    return jnp.cos(angles), jnp.sin(angles)


def mm(a, b):
    return jnp.dot(a, b, preferred_element_type=F32)


def mm_t(a, b):
    return lax.dot_general(a, b, (((1,), (1,)), ((), ())), preferred_element_type=F32)


def tmm(a, b):
    return lax.dot_general(a, b, (((0,), (0,)), ((), ())), preferred_element_type=F32)


def low(values):
    return lax.reduce_precision(values, 8, 7).astype(BF)


def call(body, out_shape, grid, in_specs, out_specs, scratch=(), flops=0, moved=0):
    return pl.pallas_call(
        body,
        out_shape=out_shape,
        grid_spec=pltpu.PrefetchScalarGridSpec(
            num_scalar_prefetch=0,
            grid=grid,
            in_specs=in_specs,
            out_specs=out_specs,
            scratch_shapes=list(scratch),
        ),
        compiler_params=pltpu.CompilerParams(
            dimension_semantics=("arbitrary",) * len(grid), vmem_limit_bytes=VMEM_LIMIT
        ),
        cost_estimate=pl.CostEstimate(flops=flops, bytes_accessed=moved, transcendentals=0),
    )


def shape(dims, dtype):
    return jax.ShapeDtypeStruct(dims, dtype)


def whole(dims):
    return pl.BlockSpec(dims, lambda *_: (0,) * len(dims))


def project_body(n_rot, x_ref, w_ref, cos_ref, sin_ref, out_ref):
    half = HEAD_SIZE // 2
    y = mm(x_ref[...], w_ref[...])
    rotate = pl.program_id(0) < n_rot
    cos = jnp.where(rotate, cos_ref[...], 1.0)
    sin = jnp.where(rotate, sin_ref[...], 0.0)
    a, b = y[:, :half], y[:, half:]
    out_ref[:, :half] = (a * cos - b * sin).astype(BF)
    out_ref[:, half:] = (b * cos + a * sin).astype(BF)


def project(normed, weights, columns, n_rot, cos, sin):
    rows, width = normed.shape
    return call(
        functools.partial(project_body, n_rot),
        shape((rows, columns), BF),
        (columns // HEAD_SIZE,),
        [
            whole((rows, width)),
            pl.BlockSpec((width, HEAD_SIZE), lambda j: (0, j)),
            whole(cos.shape),
            whole(sin.shape),
        ],
        pl.BlockSpec((rows, HEAD_SIZE), lambda j: (0, j)),
        flops=2 * rows * width * columns,
        moved=2 * (rows * width + width * columns + rows * columns),
    )(normed, weights, cos, sin)


def scores(q, k, allowed):
    soft = HEAD_SIZE ** (-0.5)
    bend = jnp.tanh(mm_t(q, k) * (soft / CAP))
    return bend, jnp.where(allowed, jnp.exp(CAP * bend), 0.0)


def attend_body(n_q, n_kv, n_pieces, *refs):
    hd = HEAD_SIZE
    q_ref, qpos_ref, kpos_ref = refs[:3]
    pieces = refs[3 : 3 + n_pieces]
    heads_ref, attended_ref, den_ref = refs[3 + n_pieces :]
    qpos = qpos_ref[...]
    for h in range(n_q):
        kv = h // (n_q // n_kv)
        q = q_ref[:, h * hd : (h + 1) * hd]
        num, den = 0.0, 0.0
        for j, piece in enumerate(pieces):
            size = piece.shape[0]
            allowed = kpos_ref[:, j * size : (j + 1) * size] <= qpos
            _, weight = scores(q, piece[:, kv * hd : (kv + 1) * hd], allowed)
            den = den + jnp.sum(weight, axis=-1, keepdims=True)
            v = piece[:, (n_kv + kv) * hd : (n_kv + kv + 1) * hd]
            num = num + mm(weight.astype(BF), v)
        heads = num / den
        heads_ref[:, h * hd : (h + 1) * hd] = heads
        attended_ref[:, h * hd : (h + 1) * hd] = heads.astype(BF)
        den_ref[:, h * PAD : (h + 1) * PAD] = jnp.broadcast_to(den, (den.shape[0], PAD))


def attend(q, q_block, pieces, qpos, kpos, n_q, n_kv):
    hd = HEAD_SIZE
    seq_dev = qpos.shape[0]
    specs = [pl.BlockSpec((seq_dev, n_q * hd), lambda i: (q_block, 0))]
    specs += [whole(qpos.shape), whole(kpos.shape)]
    arrays = [q, qpos, kpos]
    for array, size, row, col in pieces:
        specs.append(pl.BlockSpec((size, 2 * n_kv * hd), lambda i, row=row, col=col: (row, col)))
        arrays.append(array)
    seq = kpos.shape[1]
    return call(
        functools.partial(attend_body, n_q, n_kv, len(pieces)),
        (
            shape((seq_dev, n_q * hd), F32),
            shape((seq_dev, n_q * hd), BF),
            shape((seq_dev, n_q * PAD), F32),
        ),
        (1,),
        specs,
        (whole((seq_dev, n_q * hd)), whole((seq_dev, n_q * hd)), whole((seq_dev, n_q * PAD))),
        flops=4 * n_q * seq_dev * seq * hd,
        moved=2 * (2 * n_kv * hd * seq + 4 * seq_dev * n_q * hd),
    )(*arrays)


def attend_back_body(n_q, n_kv, n_pieces, *refs):
    hd = HEAD_SIZE
    half = hd // 2
    soft = hd ** (-0.5)
    q_ref, qpos_ref, kpos_ref, grad_ref, heads_ref, den_ref, cos_ref, sin_ref = refs[:8]
    pieces = refs[8 : 8 + n_pieces]
    q_back_ref = refs[8 + n_pieces]
    outs = refs[9 + n_pieces :]
    qpos = qpos_ref[...]
    group = n_q // n_kv
    for h in range(n_q):
        kv = h // group
        cols = slice(h * hd, (h + 1) * hd)
        k_cols = slice(kv * hd, (kv + 1) * hd)
        v_cols = slice((n_kv + kv) * hd, (n_kv + kv + 1) * hd)
        q = q_ref[:, cols]
        grad = grad_ref[:, cols]
        inverse = 1.0 / den_ref[:, h * PAD : h * PAD + 1]
        scaled = (grad * inverse).astype(BF)
        row_dot = jnp.sum(grad * heads_ref[:, cols], axis=-1, keepdims=True) * inverse
        q_grad = 0.0
        for j, piece in enumerate(pieces):
            size = piece.shape[0]
            allowed = kpos_ref[:, j * size : (j + 1) * size] <= qpos
            k, v = piece[:, k_cols], piece[:, v_cols]
            bend, weight = scores(q, k, allowed)
            prob = mm_t(scaled, v)
            score = (weight * (prob - row_dot) * (1.0 - bend * bend)).astype(BF)
            q_grad = q_grad + mm(score, k)
            k_term = tmm(score, q) * soft
            v_term = tmm(weight.astype(BF), scaled)
            if h % group == 0:
                outs[j][:, k_cols] = k_term
                outs[j][:, v_cols] = v_term
            else:
                outs[j][:, k_cols] += k_term
                outs[j][:, v_cols] += v_term
        q_grad = q_grad * soft
        a, b = q_grad[:, :half], q_grad[:, half:]
        q_back_ref[:, h * hd : h * hd + half] = (a * cos_ref[...] + b * sin_ref[...]).astype(BF)
        q_back_ref[:, h * hd + half : (h + 1) * hd] = (
            b * cos_ref[...] - a * sin_ref[...]
        ).astype(BF)


def attend_back(q, q_block, pieces, qpos, kpos, grad, heads, den, cos, sin, n_q, n_kv):
    hd = HEAD_SIZE
    seq_dev = qpos.shape[0]
    specs = [pl.BlockSpec((seq_dev, n_q * hd), lambda i: (q_block, 0))]
    arrays = [q, qpos, kpos, grad, heads, den, cos, sin]
    specs += [whole(a.shape) for a in arrays[1:]]
    out_shapes, out_specs = [shape((seq_dev, n_q * hd), BF)], [whole((seq_dev, n_q * hd))]
    for array, size, row, col in pieces:
        specs.append(pl.BlockSpec((size, 2 * n_kv * hd), lambda i, row=row, col=col: (row, col)))
        arrays.append(array)
        out_shapes.append(shape((size, 2 * n_kv * hd), F32))
        out_specs.append(whole((size, 2 * n_kv * hd)))
    seq = kpos.shape[1]
    return call(
        functools.partial(attend_back_body, n_q, n_kv, len(pieces)),
        tuple(out_shapes),
        (1,),
        specs,
        tuple(out_specs),
        flops=10 * n_q * seq_dev * seq * hd,
        moved=2 * (6 * n_kv * hd * seq + 8 * seq_dev * n_q * hd),
    )(*arrays)


def ffn_body(n_out, x_ref, wg_ref, wu_ref, wd_ref, gate_ref, up_ref, hid_ref, *rest):
    outs, acc = rest[:n_out], rest[n_out]
    j = pl.program_id(0)
    x = x_ref[...]
    gate = mm(x, wg_ref[...])
    up = mm(x, wu_ref[...])
    bend = jnp.tanh(GELU_C * (gate + GELU_A * gate * gate * gate))
    hidden = (0.5 * gate * (1.0 + bend) * up).astype(BF)
    gate_ref[...] = gate
    up_ref[...] = up
    hid_ref[...] = hidden
    term = mm_t(hidden, wd_ref[...])

    @pl.when(j == 0)
    def _():
        acc[...] = term

    @pl.when(j > 0)
    def _():
        acc[...] += term

    @pl.when(j == pl.num_programs(0) - 1)
    def _():
        size = acc.shape[0] // n_out
        for i, out in enumerate(outs):
            out[...] = acc[i * size : (i + 1) * size, :].astype(BF)


def ffn(x, weights, ff, n_out):
    rows, width = x.shape
    tile = 256
    steps = ff // tile
    col = lambda part: pl.BlockSpec((width, tile), lambda j: (0, part * steps + j))
    act = pl.BlockSpec((rows, tile), lambda j: (0, j))
    piece = (rows // n_out, width)
    return call(
        functools.partial(ffn_body, n_out),
        (shape((rows, ff), F32), shape((rows, ff), F32), shape((rows, ff), BF))
        + (shape(piece, BF),) * n_out,
        (steps,),
        [whole((rows, width)), col(0), col(1), col(2)],
        (act, act, act) + (whole(piece),) * n_out,
        [pltpu.VMEM((rows, width), F32)],
        flops=6 * rows * width * ff,
        moved=6 * width * ff + 4 * rows * width + 10 * rows * ff,
    )(x, weights, weights, weights)


def ffn_back_body(n_out, y_ref, wg_ref, wu_ref, wd_ref, gate_ref, up_ref, dg_ref, du_ref, *rest):
    outs, acc = rest[:n_out], rest[n_out]
    j = pl.program_id(0)
    grad = mm(y_ref[...], wd_ref[...])
    gate, up = gate_ref[...], up_ref[...]
    square = gate * gate
    bend = jnp.tanh(GELU_C * gate * (1.0 + GELU_A * square))
    rise = 0.5 * (1.0 + bend)
    slope = rise + 0.5 * gate * (1.0 - bend * bend) * (GELU_C * (1.0 + 3.0 * GELU_A * square))
    d_gate = (grad * up * slope).astype(BF)
    d_up = (grad * (gate * rise)).astype(BF)
    dg_ref[...] = d_gate
    du_ref[...] = d_up
    term = mm_t(d_gate, wg_ref[...]) + mm_t(d_up, wu_ref[...])

    @pl.when(j == 0)
    def _():
        acc[...] = term

    @pl.when(j > 0)
    def _():
        acc[...] += term

    @pl.when(j == pl.num_programs(0) - 1)
    def _():
        size = acc.shape[0] // n_out
        for i, out in enumerate(outs):
            out[...] = acc[i * size : (i + 1) * size, :].astype(BF)


def ffn_back(y, weights, gate, up, ff, n_out):
    rows, width = y.shape
    tile = 256
    steps = ff // tile
    col = lambda part: pl.BlockSpec((width, tile), lambda j: (0, part * steps + j))
    act = pl.BlockSpec((rows, tile), lambda j: (0, j))
    piece = (rows // n_out, width)
    return call(
        functools.partial(ffn_back_body, n_out),
        (shape((rows, ff), BF), shape((rows, ff), BF)) + (shape(piece, BF),) * n_out,
        (steps,),
        [whole((rows, width)), col(0), col(1), col(2), act, act],
        (act, act) + (whole(piece),) * n_out,
        [pltpu.VMEM((rows, width), F32)],
        flops=6 * rows * width * ff,
        moved=6 * width * ff + 4 * rows * width + 12 * rows * ff,
    )(y, weights, weights, weights, gate, up)


class Chain:
    def __init__(self):
        self.token = None

    def after(self, *values):
        if self.token is None:
            return values
        return lax.optimization_barrier((*values, self.token))[:-1]

    def mark(self, value):
        self.token = value
        return value


class Reduce:
    def __init__(self, chain):
        self.chain, self.piece, self.first = chain, {}, {}
        self.sums, self.second, self.total, self.third = {}, {}, {}, {}
        self.line = lax.axis_size("tensor") == 4

    def send(self, k, piece):
        self.piece[k] = piece
        if self.line:
            self.first[k] = lax.ppermute(piece, "tensor", [(0, 1), (3, 2)])
        else:
            self.total[k] = lax.psum(piece.astype(F32), "tensor")

    def add(self, k):
        if self.line:
            piece, first = self.chain.after(self.piece[k], self.first[k])
            total = low(piece.astype(F32) + first.astype(F32))
            self.sums[k] = self.chain.mark(total)
            self.second[k] = lax.ppermute(total, "tensor", [(1, 2), (2, 1)])

    def join(self, k):
        if self.line:
            sums, second = self.chain.after(self.sums[k], self.second[k])
            total = low(sums.astype(F32) + second.astype(F32))
            self.total[k] = self.chain.mark(total)
            self.third[k] = lax.ppermute(total, "tensor", [(1, 0), (2, 3)])

    def take(self, *ks):
        totals = [self.total[k] for k in ks]
        if self.line:
            zi = lax.axis_index("tensor")
            inner = (zi == 1) | (zi == 2)
            got = self.chain.after(*totals, *[self.third[k] for k in ks])
            n = len(ks)
            totals = [jnp.where(inner, got[i], got[n + i]) for i in range(n)]
        else:
            totals = list(self.chain.after(*totals))
        return jnp.concatenate(totals, axis=0).astype(F32)


def local(
    tokens,
    span_order,
    w_query,
    w_key,
    value_weight,
    w_out,
    w_gate,
    w_up,
    w_down,
    gain_attn_in,
    gain_attn_out,
    gain_ffn_in,
    gain_ffn_out,
    cotangent,
):
    micros, batch, seq_dev, width = tokens.shape
    n_dp, n_ctx, n_t = lax.axis_size("dp"), lax.axis_size("ctx"), lax.axis_size("tensor")
    dpi, ctx, zi = lax.axis_index("dp"), lax.axis_index("ctx"), lax.axis_index("tensor")
    seq = seq_dev * n_ctx
    span_len = seq // span_order.shape[0]
    hd = HEAD_SIZE
    n_kv = w_key.shape[1] // hd
    n_q = w_query.shape[1] // hd
    ff = w_gate.shape[1]
    qc, kc, oc = w_query.shape[1], w_key.shape[1], w_out.shape[1]
    n_seqs, chunks = micros * batch, 2
    swap = n_ctx == 4
    pair = n_dp == 2

    row_index = jnp.arange(seq, dtype=jnp.int32)
    all_pos = span_order[row_index // span_len] * span_len + row_index % span_len
    by_dev = all_pos.reshape(n_ctx, seq_dev)
    query_pos = lax.dynamic_index_in_dim(by_dev, ctx, 0, keepdims=False)
    if swap:
        key_pos = jnp.concatenate(
            [lax.dynamic_index_in_dim(by_dev, ctx ^ j, 0, keepdims=False) for j in range(n_ctx)]
        )
    else:
        key_pos = all_pos
    qpos, kpos = query_pos[:, None], key_pos[None, :]
    cos, sin = rotation(query_pos, hd)

    gains = jnp.stack([gain_attn_in, gain_attn_out, gain_ffn_in, gain_ffn_out], axis=1)
    gains = jnp.pad(gains, ((0, 0), (0, PAD - gains.shape[1])))
    pack_attn = jnp.concatenate([w_query, w_key, value_weight, w_out, gains], axis=1)
    pack_ffn = jnp.concatenate([w_gate, w_up, w_down], axis=1)
    full_attn = lax.all_gather(pack_attn, ("dp", "ctx"), axis=0, tiled=True)
    full_ffn = lax.all_gather(pack_ffn, ("dp", "ctx"), axis=0, tiled=True)
    at_out = qc + 2 * kc
    full_qkv = full_attn[:, :at_out]
    full_out = full_attn[:, at_out : at_out + oc]
    pick = jnp.eye(8, PAD, dtype=BF)
    gain_rows = mm_t(pick, full_attn[:, at_out + oc :])
    scale_in, scale_attn, scale_mid, scale_fin = (1.0 + gain_rows[i : i + 1] for i in range(4))

    flips = [[(i, i ^ j) for i in range(n_ctx)] for j in range(n_ctx)]

    def half(full, owner):
        return lax.dynamic_slice_in_dim(full, owner * (width // 2), width // 2, 1)

    def swap_core(value):
        return lax.ppermute(value, "dp", [(0, 1), (1, 0)])

    def grad_operands(lefts, rights):
        left, right = jnp.concatenate(lefts, axis=0), jnp.concatenate(rights, axis=0)
        if not pair:
            return left, right
        other_left = [swap_core(half(v, 1 - dpi)) for v in lefts]
        other_right = [swap_core(v) for v in rights]
        return (
            jnp.concatenate([half(v, dpi) for v in lefts] + other_left, axis=0),
            jnp.concatenate(list(rights) + other_right, axis=0),
        )

    def scatter(grad):
        axes = "ctx" if pair else ("dp", "ctx")
        return lax.psum_scatter(grad, axes, scatter_dimension=0, tiled=True)

    def mine(full):
        size = full.shape[0] // n_t
        return lax.dynamic_slice_in_dim(full, zi * size, size, 0)

    xs = tokens.astype(F32).reshape(n_seqs * seq_dev, width)
    xhats, fac_in = apply_norm(xs)
    normed = (xhats * scale_in).astype(BF)
    cos_all, sin_all = jnp.tile(cos, (n_seqs, 1)), jnp.tile(sin, (n_seqs, 1))
    qkv = project(normed, full_attn, qc + 2 * kc, n_q + n_kv, cos_all, sin_all)
    kv = qkv[:, qc:]
    if swap:
        others = [lax.ppermute(kv, "ctx", flips[j]) for j in range(1, n_ctx)]
        pieces = [[(a, seq_dev, m, 0) for a in [kv] + others] for m in range(n_seqs)]
    else:
        every = lax.all_gather(kv.reshape(n_seqs, seq_dev, 2 * kc), "ctx", axis=1, tiled=True)
        every = every.reshape(n_seqs * seq, 2 * kc)
        pieces = [[(every, seq, m, 0)] for m in range(n_seqs)]

    def rows_of(value, m):
        return value[m * seq_dev : (m + 1) * seq_dev]

    def split(value):
        size = value.shape[0] // 2
        return value[:size], value[size:]

    chain = Chain()
    st = [{}, {}]
    assert n_seqs == 2
    red = Reduce(chain)
    for m in (0, 1):
        s = st[m]
        (first, *rest) = chain.after(*[p[0] for p in pieces[m]])
        tied = [(v,) + p[1:] for v, p in zip([first, *rest], pieces[m])]
        s["pieces"] = tied
        s["heads"], s["attended"], s["den"] = attend(qkv, m, tied, qpos, kpos, n_q, n_kv)
        for i, rows in enumerate(split(s["attended"])):
            red.send(2 * m + i, chain.mark(mm_t(rows, full_out).astype(BF)))

    def drain(red):
        red.add(0), red.add(1), red.join(0), red.add(2)
        red.join(1), red.add(3), red.join(2)

    def post_attend(m, red):
        s = st[m]
        s["ahat"], s["fac_attn"] = apply_norm(red.take(2 * m, 2 * m + 1))
        s["hidden_one"] = rows_of(xs, m) + s["ahat"] * scale_attn
        s["h1hat"], s["fac_mid"] = apply_norm(s["hidden_one"])
        s["normed_two"] = chain.mark((s["h1hat"] * scale_mid).astype(BF))

    drain(red)
    red.join(3)
    post_attend(0, red)
    post_attend(1, red)

    red = Reduce(chain)
    for m in (0, 1):
        s = st[m]
        (value,) = chain.after(s["normed_two"])
        s["gate"], s["up"], s["hidden"], *part = ffn(value, full_ffn, ff, chunks)
        chain.mark(part[0])
        for i in range(2):
            red.send(2 * m + i, part[i])
    outputs = []
    dys = cotangent.astype(F32).reshape(n_seqs * seq_dev, width)
    gain_sums = [0.0] * 4

    def post_ffn(m, red):
        s = st[m]
        fhat, fac_out = apply_norm(red.take(2 * m, 2 * m + 1))
        outputs.append((s["hidden_one"] + fhat * scale_fin).astype(BF))
        dy = rows_of(dys, m)
        gain_sums[3] = gain_sums[3] + jnp.sum(mine(dy * fhat), axis=0)
        s["ffn_grad"] = chain.mark(norm_backward(dy * scale_fin, fhat, fac_out).astype(BF))

    def run_ffn_back(m, red):
        s = st[m]
        (value,) = chain.after(s["ffn_grad"])
        s["gate_grad"], s["up_grad"], *part = ffn_back(
            value, full_ffn, s["gate"], s["up"], ff, chunks
        )
        chain.mark(part[0])
        for i in range(2):
            red.send(2 * m + i, part[i])

    def every(name):
        return [s[name] for s in st]

    def chained_grad(lefts, rights):
        left, right = chain.after(*grad_operands(lefts, rights))
        return chain.mark(tmm(left, right).astype(BF))

    drain(red)
    post_ffn(0, red)
    red.join(3)
    back = Reduce(chain)
    run_ffn_back(0, back)
    post_ffn(1, red)
    run_ffn_back(1, back)
    red = back

    red.add(0), red.add(1)
    g_down = scatter(chained_grad(every("ffn_grad"), every("hidden")))
    red.join(0), red.add(2), red.join(1), red.add(3)
    both = [jnp.concatenate([s["gate_grad"], s["up_grad"]], axis=1) for s in st]
    g_gate_up = scatter(chained_grad(every("normed_two"), both))
    red.join(2)

    def post_mid(m, red):
        s = st[m]
        mid = red.take(2 * m, 2 * m + 1)
        gain_sums[2] = gain_sums[2] + jnp.sum(mine(mid * s["h1hat"]), axis=0)
        s["one_grad"] = rows_of(dys, m) + norm_backward(mid * scale_mid, s["h1hat"], s["fac_mid"])
        gain_sums[1] = gain_sums[1] + jnp.sum(mine(s["one_grad"] * s["ahat"]), axis=0)
        s["attn_grad"] = chain.mark(
            norm_backward(s["one_grad"] * scale_attn, s["ahat"], s["fac_attn"]).astype(BF)
        )

    def attention_back(m):
        s = st[m]
        (value,) = chain.after(s["attn_grad"])
        heads_grad = mm(value, full_out)
        s["q_back"], *s["terms"] = attend_back(
            qkv, m, s["pieces"], qpos, kpos, heads_grad, s["heads"], s["den"], cos, sin, n_q, n_kv
        )
        chain.mark(s["q_back"])
        if swap:
            s["moved"] = [
                lax.ppermute(s["terms"][j].astype(BF), "ctx", flips[j]) for j in range(1, n_ctx)
            ]
        else:
            s["moved"] = [lax.psum_scatter(s["terms"][0], "ctx", scatter_dimension=0, tiled=True)]

    def input_back(m, red):
        s = st[m]
        moved = chain.after(*s["moved"])
        kv_grad = s["terms"][0] if swap else 0.0
        for value in moved:
            kv_grad = kv_grad + value.astype(F32)
        backs = [s["q_back"]]
        for h in range(n_kv):
            a = kv_grad[:, h * hd : h * hd + hd // 2]
            b = kv_grad[:, h * hd + hd // 2 : (h + 1) * hd]
            backs += [(a * cos + b * sin).astype(BF), (b * cos - a * sin).astype(BF)]
        backs.append(kv_grad[:, kc:].astype(BF))
        s["qkv_back"] = jnp.concatenate(backs, axis=1)
        terms = mm_t(s["qkv_back"], full_qkv)
        gain_sums[0] = gain_sums[0] + jnp.sum(terms * rows_of(xhats, m), axis=0)
        for i, rows in enumerate(split(terms.astype(BF))):
            red.send(2 * m + i, chain.mark(rows))

    post_mid(0, red)
    attention_back(0)
    red.join(3)
    post_mid(1, red)
    attention_back(1)
    red = Reduce(chain)
    (g_down,) = chain.after(g_down)
    chain.mark(g_down)
    input_back(0, red)
    input_back(1, red)
    normed_list = [rows_of(normed, m) for m in range(n_seqs)]
    d_qkv = chained_grad(normed_list, every("qkv_back"))
    red.add(0), red.add(1)
    d_out = chained_grad(every("attn_grad"), every("attended"))
    gain_cols = jnp.stack(gain_sums, axis=1)
    if pair:
        keep = lax.dynamic_slice_in_dim(gain_cols, dpi * (width // 2), width // 2, 0)
        give = lax.dynamic_slice_in_dim(gain_cols, (1 - dpi) * (width // 2), width // 2, 0)
        gain_cols = keep + swap_core(give)
    gain_cols = jnp.pad(gain_cols.astype(BF), ((0, 0), (0, PAD - gain_cols.shape[1])))
    tail = jnp.concatenate([d_qkv, d_out, gain_cols], axis=1)
    if pair:
        tail = tail.reshape(n_ctx, tail.shape[0] // n_ctx, tail.shape[1])
        g_tail = lax.all_to_all(tail, "ctx", 0, 0)
    else:
        g_tail = scatter(tail)[None]
    red.join(0), red.add(2), red.join(1), red.add(3), red.join(2)

    input_grads = []

    def post_in(m, red):
        s = st[m]
        in_grad = red.take(2 * m, 2 * m + 1)
        grad = norm_backward(in_grad * scale_in, rows_of(xhats, m), rows_of(fac_in, m))
        input_grads.append(chain.mark((s["one_grad"] + grad).astype(BF)))

    post_in(0, red)
    red.join(3)
    (g_tail,) = chain.after(g_tail)
    g_tail = chain.mark(jnp.sum(g_tail.astype(F32), axis=0))
    g_gains = mm_t(pick.astype(F32), g_tail[:, at_out + oc :])
    g_gains = lax.all_to_all(
        jnp.broadcast_to(g_gains[None], (n_t,) + g_gains.shape), "tensor", 0, 0
    )
    post_in(1, red)
    g_gains = jnp.sum(g_gains, axis=0)
    g_gate_up = g_gate_up.astype(F32)
    return (
        jnp.concatenate(outputs, axis=0).reshape(tokens.shape),
        jnp.concatenate(input_grads, axis=0).reshape(tokens.shape),
        g_tail[:, :qc],
        g_tail[:, qc : qc + kc],
        g_tail[:, qc + kc : qc + 2 * kc],
        g_tail[:, at_out : at_out + oc],
        g_gate_up[:, :ff],
        g_gate_up[:, ff:],
        g_down.astype(F32),
        g_gains[0],
        g_gains[1],
        g_gains[2],
        g_gains[3],
    )


def solution(mesh):
    act = P(None, "dp", "ctx", None)
    mat = P(("dp", "ctx"), "tensor")
    vec = P(("dp", "ctx"))
    return jax.shard_map(
        local,
        mesh=mesh,
        in_specs=(act, P()) + (mat,) * 7 + (vec,) * 4 + (act,),
        out_specs=(act, act) + (mat,) * 7 + (vec,) * 4,
        check_vma=False,
    )
```

time: 1880 us -> 775 us (0.41)
  waiting for transfers between devices: 1410 us -> 273 us
  matrix products: 242 us -> 50.5 us
  Pallas kernels: 0 us -> 115 us
  blocking collectives: 111 us -> 0 us
  starting transfers between devices: 1.99 us -> 103 us
  other arithmetic: 59.9 us -> 153 us
    reduce_scatter x11 -> x2, waiting for transfers between devices: 664 us -> 0.02 us  [scatter(): return lax.psum_scatter(grad, axes, scatter_dimension=0, tiled=True)]
    psum x4 -> x0, waiting for transfers between devices: 580 us -> none  [the longest x1 171 us: local(): ffn_out = lax.psum(project_out(hidden_low, full_down), 'tensor')]
    ppermute x0 -> x74, waiting for transfers between devices: none -> 207 us  [the longest x16 89.9 us: join(): self.third[k] = lax.ppermute(total, 'tensor', [(1, 0), (2, 3)])]
    dot_general x54 -> x14, matrix products: 242 us -> 50.5 us  [the longest x4 26 us: tmm(): lax.dot_general(a, b, (((0,), (0,)), ((), ())), preferred_element_type=F32)]
    all_gather x7 -> x2, waiting for transfers between devices: 159 us -> 34.3 us  [the longest x1 34.3 us: local(): full_attn = lax.all_gather(pack_attn, ('dp', 'ctx'), axis=0, tiled=True)]
    pallas_call x0 -> x9, Pallas kernels: none -> 115 us  [the longest x2 47.9 us: ffn_back(): call(functools.partial(ffn_back_body, n_out), (shape((rows, ff), BF), sha...]
    ppermute x0 -> x74, starting transfers between devices: none -> 95.1 us  [the longest x16 43.9 us: send(): self.first[k] = lax.ppermute(piece, 'tensor', [(0, 1), (3, 2)])]
    unnamed x2 -> x0, blocking collectives: 57.7 us -> none
  transfers between devices with their start and end apart: 22 -> 80, of which waited for: 17 -> 22; matrix products, arithmetic and copies ran while one was open for 12% -> 31% of each run, Pallas kernels for 0% -> 12%
where the time goes in v1:
time: 775 us; the launch traced here: 762 us
  waiting for transfers between devices  273 us (35%)
  other arithmetic  153 us (20%)
  Pallas kernels  115 us (15%)
  starting transfers between devices  103 us (13%)
  local copies, waits for them, and re-layouts  51.4 us (7%)
  matrix products  50.5 us (7%)
  between operations  16.1 us (2%)
    ppermute x16, waiting for transfers between devices, join(): self.third[k] = lax.ppermute(total, 'tensor', [(1, 0), (2, 3)])  89.9 us
    ppermute x16, waiting for transfers between devices, send(): self.first[k] = lax.ppermute(piece, 'tensor', [(0, 1), (3, 2)])  62 us
    pallas_call x2, Pallas kernels, ffn_back(): call(functools.partial(ffn_back_body, n_out), (shape((rows, ff), BF), sha...  47.9 us
    ppermute x16, starting transfers between devices, send(): self.first[k] = lax.ppermute(piece, 'tensor', [(0, 1), (3, 2)])  43.9 us
    ppermute x3, waiting for transfers between devices, local(): others = [lax.ppermute(kv, 'ctx', flips[j]) for j in range(1, n_ctx)]  42.3 us
    pallas_call x2, Pallas kernels, ffn(): call(functools.partial(ffn_body, n_out), (shape((rows, ff), F32), shape((...  41.2 us
    all_gather x1, waiting for transfers between devices, local(): full_attn = lax.all_gather(pack_attn, ('dp', 'ctx'), axis=0, tiled=True)  34.3 us
    all_to_all x1, waiting for transfers between devices, local(): g_tail = lax.all_to_all(tail, 'ctx', 0, 0)  31.9 us
  transfers between devices with their start and end apart: 80, of which 22 were waited for; matrix products, arithmetic and copies ran while one was open for 31% of the time, Pallas kernels for 12%

profile of v1, /device:TPU:0, one launch (start us, length us, event | category | flops | bytes accessed | tf_op | source)
XLA Modules:
  0.0 762.5 jit_solution(4119715051095586026)
XLA Ops:
  15.1 3.3 pad_maximum_fusion.2
  19.7 4.5 compare_select_fusion.1
  29.5 4.1 convert_element_type.514
  34.8 34.3 %all-gather.3.cloned.1.call-done.w_ref = bf16[2304,1664]{1,0:T(8,128)(2,1)} async-done(((bf16[288,1664]{1,0:T(8,128)(2,1)}), bf16[2304,1664]{1,0:T(8,128)(2,1)}) %all-gather.3.cloned.1.call-update) | async-done | bytes 7667728 | tf_op jit(solution)/shard_map/all_gather | solution.py:430
  70.6 3.6 bitcast_multiply_fusion
  75.7 7.7 %shard_map.237.refs_0_ = bf16[512,1024]{1,0:T(8,128)(2,1)} custom-call(bf16[512,2304]{1,0:T(8,128)(2,1)} %get-tuple-element.403.x_ref, bf16[2304,1664]{1,0:T(8,128)(2,1)} %all-gather.3.cloned.1.call-done.w_ref, f32[512,128]{1,0:T(8,128)} %bitcast.104, f32[512,128]{1,0:T(8,128)} %bitcast.105), custom_call_target="tpu_custom_call" | custom-call | flops 2415919104 | bytes 8126464 | tf_op jit(solution)/shard_map/pallas_call | solution.py:93
  90.8 19.8 %collective-permute-done.refs_4_.refs_9_ = bf16[512,512]{1,0:T(8,128)(2,1)S(1)} collective-permute-done((bf16[512,512]{1,0:T(8,128)(2,1)S(1)}, bf16[512,512]{1,0:T(8,128)(2,1)S(1)}, u32[]{:S(2)}, u32[]{:S(2)}) %collective-permute-start) | collective-permute-done | bytes 524320 | tf_op jit(solution)/shard_map/ppermute | solution.py:473
  112.5 20.5 %collective-permute-done.2.refs_6_.refs_11_ = bf16[512,512]{1,0:T(8,128)(2,1)S(1)} collective-permute-done((bf16[512,512]{1,0:T(8,128)(2,1)S(1)}, bf16[512,512]{1,0:T(8,128)(2,1)S(1)}, u32[]{:S(2)}, u32[]{:S(2)}) %collective-permute-start.2) | collective-permute-done | bytes 524320 | tf_op jit(solution)/shard_map/ppermute | solution.py:473
  133.9 3.4 shard_map.238
  139.9 3.4 collective-permute-start.5
  147.2 3.4 shard_map.239
  157.3 12.3 %collective-permute-done.3 = bf16[128,2304]{1,0:T(8,128)(2,1)S(1)} collective-permute-done((bf16[128,2304]{1,0:T(8,128)(2,1)S(1)}, bf16[128,2304]{1,0:T(8,128)(2,1)S(1)}, u32[]{:S(2)}, u32[]{:S(2)}) %collective-permute-start.3) | collective-permute-done | bytes 589856 | tf_op jit(solution)/shard_map/ppermute | solution.py:352
  169.6 4.4 collective-permute-start.10
  175.9 6.3 collective-permute-done.7
  184.7 8.7 %collective-permute-done.10 = bf16[128,2304]{1,0:T(8,128)(2,1)S(1)} collective-permute-done((bf16[128,2304]{1,0:T(8,128)(2,1)S(1)}, bf16[128,2304]{1,0:T(8,128)(2,1)S(1)}, u32[]{:S(2)}, u32[]{:S(2)}) %collective-permute-start.10) | collective-permute-done | bytes 589856 | tf_op jit(solution)/shard_map/ppermute | solution.py:352
  197.3 17.8 %collective-permute-done.9 = bf16[128,2304]{1,0:T(8,128)(2,1)S(1)} collective-permute-done((bf16[128,2304]{1,0:T(8,128)(2,1)S(1)}, bf16[128,2304]{1,0:T(8,128)(2,1)S(1)}, u32[]{:S(2)}, u32[]{:S(2)}) %collective-permute-start.9) | collective-permute-done | bytes 589856 | tf_op jit(solution)/shard_map/ppermute | solution.py:368
  222.1 26.4 %collective-permute-done.14 = bf16[128,2304]{1,0:T(8,128)(2,1)S(1)} collective-permute-done((bf16[128,2304]{1,0:T(8,128)(2,1)S(1)}, bf16[128,2304]{1,0:T(8,128)(2,1)S(1)}, u32[]{:S(2)}, u32[]{:S(2)}) %collective-permute-start.14) | collective-permute-done | bytes 589856 | tf_op jit(solution)/shard_map/ppermute | solution.py:368
  262.2 4.5 pad_maximum_fusion.5
  266.7 20.6 %shard_map.240 = (f32[256,2304]{1,0:T(8,128)}, f32[256,2304]{1,0:T(8,128)}, bf16[256,2304]{1,0:T(8,128)(2,1)}, bf16[128,2304]{1,0:T(8,128)(2,1)}, bf16[128,2304]{1,0:T(8,128)(2,1)}) custom-call(bf16[256,2304]{1,0:T(8,128)(2,1)} %copy-done.8, bf16[2304,6912]{1,0:T(8,128)(2,1)} %all-gather.5.cloned.1.call-done.wg_ref.wu_ref.wd_ref, ...), custom_call_target="tpu_custom_call" | custom-call | flops 8153726976 | bytes 40108032 | tf_op jit(solution)/shard_map/pallas_call | solution.py:267
  291.8 20.6 %shard_map.241 = (f32[256,2304]{1,0:T(8,128)}, f32[256,2304]{1,0:T(8,128)}, bf16[256,2304]{1,0:T(8,128)(2,1)}, bf16[128,2304]{1,0:T(8,128)(2,1)}, bf16[128,2304]{1,0:T(8,128)(2,1)}) custom-call(bf16[256,2304]{1,0:T(8,128)(2,1)} %copy-done.9, bf16[2304,6912]{1,0:T(8,128)(2,1)} %all-gather.5.cloned.1.call-done.wg_ref.wu_ref.wd_ref, ...), custom_call_target="tpu_custom_call" | custom-call | flops 8153726976 | bytes 40108032 | tf_op jit(solution)/shard_map/pallas_call | solution.py:267
  324.3 3.6 collective-permute-done.19
  330.2 10.0 %collective-permute-done.23 = bf16[128,2304]{1,0:T(8,128)(2,1)S(1)} collective-permute-done((bf16[128,2304]{1,0:T(8,128)(2,1)}, bf16[128,2304]{1,0:T(8,128)(2,1)S(1)}, u32[]{:S(2)}, u32[]{:S(2)}) %collective-permute-start.23) | collective-permute-done | bytes 589856 | tf_op jit(solution)/shard_map/ppermute | solution.py:352
  342.6 18.1 %collective-permute-done.21 = bf16[128,2304]{1,0:T(8,128)(2,1)S(1)} collective-permute-done((bf16[128,2304]{1,0:T(8,128)(2,1)S(1)}, bf16[128,2304]{1,0:T(8,128)(2,1)S(1)}, u32[]{:S(2)}, u32[]{:S(2)}) %collective-permute-start.21) | collective-permute-done | bytes 589856 | tf_op jit(solution)/shard_map/ppermute | solution.py:368
  368.7 23.9 %shard_map.242 = (bf16[256,2304]{1,0:T(8,128)(2,1)}, bf16[256,2304]{1,0:T(8,128)(2,1)}, bf16[128,2304]{1,0:T(8,128)(2,1)}, bf16[128,2304]{1,0:T(8,128)(2,1)}) custom-call(bf16[256,2304]{1,0:T(8,128)(2,1)} %copy-done.11, bf16[2304,6912]{1,0:T(8,128)(2,1)} %all-gather.5.cloned.1.call-done.wg_ref.wu_ref.wd_ref, ...), custom_call_target="tpu_custom_call" | custom-call | flops 8153726976 | bytes 41287680 | tf_op jit(solution)/shard_map/pallas_call | solution.py:317
  392.6 12.7 %collective-permute-start.27 = (bf16[128,2304]{1,0:T(8,128)(2,1)}, bf16[128,2304]{1,0:T(8,128)(2,1)}, u32[]{:S(2)}, u32[]{:S(2)}) collective-permute-start(bf16[128,2304]{1,0:T(8,128)(2,1)} %get-tuple-element.237), channel_id=1, source_target_pairs={{0,1},{3,2},{4,5},{7,6},{8,9},{11,10},{12,13},{15,14},{16,17},{19,... | collective-permute-start | bytes 1769480 | tf_op jit(solution)/shard_map/ppermute | solution.py:352
  415.5 6.7 add_convert_fusion.3
  424.6 24.0 %shard_map.243 = (bf16[256,2304]{1,0:T(8,128)(2,1)}, bf16[256,2304]{1,0:T(8,128)(2,1)}, bf16[128,2304]{1,0:T(8,128)(2,1)}, bf16[128,2304]{1,0:T(8,128)(2,1)}) custom-call(bf16[256,2304]{1,0:T(8,128)(2,1)} %get-tuple-element.233.y_ref, bf16[2304,6912]{1,0:T(8,128)(2,1)} %all-gather.5.cloned.1.call-done.wg_ref.wu_ref.wd_ref, ...), custom_call_target="tpu_custom_call" | custom-call | flops 8153726976 | bytes 41287680 | tf_op jit(solution)/shard_map/pallas_call | solution.py:317
  464.8 4.0 pad_maximum_fusion.4
  468.9 7.5 convolution_convert_fusion.1
  490.4 4.0 pad_maximum_fusion
  494.5 13.7 %convolution_convert_fusion = bf16[1152,4608]{1,0:T(8,128)(2,1)} fusion(bf16[1024,1152]{1,0:T(8,128)(2,1)S(1)} %copy-done.24, bf16[1024,4608]{1,0:T(8,128)(2,1)S(1)} %pad_maximum_fusion), kind=kOutput, calls=%fused_computation | convolution fusion | flops 10876944384 | bytes 22413312 | tf_op jit(solution)/shard_map/dot_general | solution.py:47
  518.7 3.9 fusion.14.refs_3_
  522.6 5.7 shard_map.244
  544.3 8.4 %collective-permute-done.49 = bf16[128,2304]{1,0:T(8,128)(2,1)} collective-permute-done((bf16[128,2304]{1,0:T(8,128)(2,1)S(1)}, bf16[128,2304]{1,0:T(8,128)(2,1)}, u32[]{:S(2)}, u32[]{:S(2)}) %collective-permute-start.49) | collective-permute-done | bytes 589856 | tf_op jit(solution)/shard_map/ppermute | solution.py:368
  562.0 5.7 shard_map.245
  580.7 3.4 pad_maximum_fusion.7
  586.7 3.9 fusion.65
  594.5 9.7 %collective-permute-done.55 = bf16[256,512]{1,0:T(8,128)(2,1)S(1)} collective-permute-done((bf16[256,512]{1,0:T(8,128)(2,1)}, bf16[256,512]{1,0:T(8,128)(2,1)S(1)}, u32[]{:S(2)}, u32[]{:S(2)}) %collective-permute-start.55) | collective-permute-done | bytes 262176 | tf_op jit(solution)/shard_map/ppermute | solution.py:589
  626.0 7.7 %collective-permute-done.65 = bf16[128,2304]{1,0:T(8,128)(2,1)S(1)} collective-permute-done((bf16[128,2304]{1,0:T(8,128)(2,1)S(1)}, bf16[128,2304]{1,0:T(8,128)(2,1)S(1)}, u32[]{:S(2)}, u32[]{:S(2)}) %collective-permute-start.65) | collective-permute-done | bytes 589856 | tf_op jit(solution)/shard_map/ppermute | solution.py:352
  636.2 10.0 %collective-permute-done.69 = bf16[128,2304]{1,0:T(8,128)(2,1)S(1)} collective-permute-done((bf16[128,2304]{1,0:T(8,128)(2,1)S(1)}, bf16[128,2304]{1,0:T(8,128)(2,1)S(1)}, u32[]{:S(2)}, u32[]{:S(2)}) %collective-permute-start.69) | collective-permute-done | bytes 589856 | tf_op jit(solution)/shard_map/ppermute | solution.py:352
  648.1 19.1 %collective-permute-done.67 = bf16[128,2304]{1,0:T(8,128)(2,1)S(1)} collective-permute-done((bf16[128,2304]{1,0:T(8,128)(2,1)S(1)}, bf16[128,2304]{1,0:T(8,128)(2,1)S(1)}, u32[]{:S(2)}, u32[]{:S(2)}) %collective-permute-start.67) | collective-permute-done | bytes 589856 | tf_op jit(solution)/shard_map/ppermute | solution.py:368
  670.3 8.0 %fusion.5 = bf16[1152,1664]{0,1:T(8,128)(2,1)} fusion(bf16[1152,4]{0,1:T(4,128)(2,1)S(1)} %add_convert_fusion.4, bf16[1152,512]{0,1:T(8,128)(2,1)S(1)} %convolution_convert_fusion.7, bf16[1152,1024]{0,1:T(8,128)(2,1)S(1)} %convolution_convert_fusion.2), kind=kLoop, calls=%fused_computation.15 | loop fusion | flops 15335424 | bytes 7382016 | tf_op jit(solution)/shard_map/concatenate | solution.py:632
  678.3 6.4 copy.53
  684.7 4.9 all-to-all-start
  692.8 3.4 add_convert_fusion.1
  702.1 31.9 %all-to-all-done = bf16[4,288,1664]{2,1,0:T(8,128)(2,1)} async-done(((bf16[4,288,1664]{2,1,0:T(8,128)(2,1)}), bf16[4,288,1664]{2,1,0:T(8,128)(2,1)}, u32[]{:S(2)}, u32[]{:S(2)}) %all-to-all-start) | async-done | bytes 3833888 | tf_op jit(solution)/shard_map/all_to_all | solution.py:635
  737.6 3.3 all-to-all-start.1
  751.3 4.5 fusion.57
  (523 shorter events, 248.2 us)
Async XLA Ops:
  7.2 62.0 %all-gather.3.cloned.1.call-start = ((), (), s32[]{:S(2)}) async-start(), calls=%async_computation.4 | async-start | bytes 8626176 | tf_op jit(solution)/shard_map/all_gather | solution.py:430
  15.1 251.6 %all-gather.5.cloned.1.call-start = ((), (), s32[]{:S(2)}) async-start(), calls=%async_computation.5 | async-start | bytes 35831808 | tf_op jit(solution)/shard_map/all_gather | solution.py:431
  18.5 565.7 %reduce-scatter.3.cloned.1.call-start = ((), (), s32[]{:S(2)}) async-start(), calls=%async_computation.6 | async-start | bytes 6635520 | tf_op jit(solution)/shard_map/reduce_scatter | solution.py:460
  84.5 26.1 %collective-permute-start = (bf16[512,512]{1,0:T(8,128)(2,1)S(1)}, bf16[512,512]{1,0:T(8,128)(2,1)S(1)}, u32[]{:S(2)}, u32[]{:S(2)}) collective-permute-start(bf16[512,512]{1,0:T(8,128)(2,1)S(1)} %slice.208.refs_3_.refs_8_), channel_id=1, source_target_pairs={{0,4},{4,0},{8,12},{12,8},{1,5},{5,1},{9,13},{13,9},{2,6},{6,2},{1... | collective-permute-start | bytes 1572872 | tf_op jit(solution)/shard_map/ppermute | solution.py:473
  85.7 26.8 %collective-permute-start.1 = (bf16[512,512]{1,0:T(8,128)(2,1)S(1)}, bf16[512,512]{1,0:T(8,128)(2,1)S(1)}, u32[]{:S(2)}, u32[]{:S(2)}) collective-permute-start(bf16[512,512]{1,0:T(8,128)(2,1)S(1)} %slice.208.refs_3_.refs_8_), channel_id=1, source_target_pairs={{0,8},{4,12},{8,0},{12,4},{1,9},{5,13},{9,1},{13,5},{2,10},{6,14},... | collective-permute-start | bytes 1572872 | tf_op jit(solution)/shard_map/ppermute | solution.py:473
  86.1 46.9 %collective-permute-start.2 = (bf16[512,512]{1,0:T(8,128)(2,1)S(1)}, bf16[512,512]{1,0:T(8,128)(2,1)S(1)}, u32[]{:S(2)}, u32[]{:S(2)}) collective-permute-start(bf16[512,512]{1,0:T(8,128)(2,1)S(1)} %slice.208.refs_3_.refs_8_), channel_id=1, source_target_pairs={{0,12},{4,8},{8,4},{12,0},{1,13},{5,9},{9,5},{13,1},{2,14},{6,10},... | collective-permute-start | bytes 1572872 | tf_op jit(solution)/shard_map/ppermute | solution.py:473
  89.2 168.8 %collective-permute-start.51 = (bf16[256,1152]{1,0:T(8,128)(2,1)}, bf16[256,1152]{1,0:T(8,128)(2,1)}, u32[]{:S(2)}, u32[]{:S(2)}) collective-permute-start(bf16[256,1152]{1,0:T(8,128)(2,1)} %get-tuple-element.424), channel_id=1, source_target_pairs={{0,16},{16,0},{1,17},{17,1},{2,18},{18,2},{3,19},{19,3},{4,20},{20... | collective-permute-start | bytes 1769480 | tf_op jit(solution)/shard_map/ppermute | solution.py:445
  90.3 167.7 %collective-permute-start.52 = (bf16[256,1152]{1,0:T(8,128)(2,1)}, bf16[256,1152]{1,0:T(8,128)(2,1)}, u32[]{:S(2)}, u32[]{:S(2)}) collective-permute-start(bf16[256,1152]{1,0:T(8,128)(2,1)} %get-tuple-element.426), channel_id=1, source_target_pairs={{0,16},{16,0},{1,17},{17,1},{2,18},{18,2},{3,19},{19,3},{4,20},{20... | collective-permute-start | bytes 1769480 | tf_op jit(solution)/shard_map/ppermute | solution.py:445
  139.9 34.3 %collective-permute-start.5 = (bf16[128,2304]{1,0:T(8,128)(2,1)S(1)}, bf16[128,2304]{1,0:T(8,128)(2,1)S(1)}, u32[]{:S(2)}, u32[]{:S(2)}) collective-permute-start(bf16[128,2304]{1,0:T(8,128)(2,1)S(1)} %convolution_convert_fusion.5), channel_id=1, source_target_pairs={{0,1},{3,2},{4,5},{7,6},{8,9},{11,10},{12,13},{15,14},{16,17},{19,... | collective-permute-start | bytes 1769480 | tf_op jit(solution)/shard_map/ppermute | solution.py:352
  145.9 23.7 %collective-permute-start.3 = (bf16[128,2304]{1,0:T(8,128)(2,1)S(1)}, bf16[128,2304]{1,0:T(8,128)(2,1)S(1)}, u32[]{:S(2)}, u32[]{:S(2)}) collective-permute-start(bf16[128,2304]{1,0:T(8,128)(2,1)S(1)} %convolution_convert_fusion.6), channel_id=1, source_target_pairs={{0,1},{3,2},{4,5},{7,6},{8,9},{11,10},{12,13},{15,14},{16,17},{19,... | collective-permute-start | bytes 1769480 | tf_op jit(solution)/shard_map/ppermute | solution.py:352
  153.3 29.0 %collective-permute-start.7 = (bf16[128,2304]{1,0:T(8,128)(2,1)S(1)}, bf16[128,2304]{1,0:T(8,128)(2,1)S(1)}, u32[]{:S(2)}, u32[]{:S(2)}) collective-permute-start(bf16[128,2304]{1,0:T(8,128)(2,1)S(1)} %convolution_convert_fusion.3), channel_id=1, source_target_pairs={{0,1},{3,2},{4,5},{7,6},{8,9},{11,10},{12,13},{15,14},{16,17},{19,... | collective-permute-start | bytes 1769480 | tf_op jit(solution)/shard_map/ppermute | solution.py:352
  169.6 23.8 %collective-permute-start.10 = (bf16[128,2304]{1,0:T(8,128)(2,1)S(1)}, bf16[128,2304]{1,0:T(8,128)(2,1)S(1)}, u32[]{:S(2)}, u32[]{:S(2)}) collective-permute-start(bf16[128,2304]{1,0:T(8,128)(2,1)S(1)} %convolution_convert_fusion.4), channel_id=1, source_target_pairs={{0,1},{3,2},{4,5},{7,6},{8,9},{11,10},{12,13},{15,14},{16,17},{19,... | collective-permute-start | bytes 1769480 | tf_op jit(solution)/shard_map/ppermute | solution.py:352
  182.3 34.4 %collective-permute-start.8 = (bf16[128,2304]{1,0:T(8,128)(2,1)S(1)}, bf16[128,2304]{1,0:T(8,128)(2,1)S(1)}, u32[]{:S(2)}, u32[]{:S(2)}) collective-permute-start(bf16[128,2304]{1,0:T(8,128)(2,1)S(1)} %reduce-precision_convert_fusion.29), channel_id=1, source_target_pairs={{1,0},{2,3},{5,4},{6,7},{9,8},{10,11},{13,12},{14,15},{17,16},{18,... | collective-permute-start | bytes 1769480 | tf_op jit(solution)/shard_map/ppermute | solution.py:368
  195.9 52.6 %collective-permute-start.13 = (bf16[128,2304]{1,0:T(8,128)(2,1)S(1)}, bf16[128,2304]{1,0:T(8,128)(2,1)S(1)}, u32[]{:S(2)}, u32[]{:S(2)}) collective-permute-start(bf16[128,2304]{1,0:T(8,128)(2,1)S(1)} %reduce-precision_convert_fusion.25), channel_id=1, source_target_pairs={{1,0},{2,3},{5,4},{6,7},{9,8},{10,11},{13,12},{14,15},{17,16},{18,... | collective-permute-start | bytes 1769480 | tf_op jit(solution)/shard_map/ppermute | solution.py:368
  215.2 33.3 %collective-permute-start.14 = (bf16[128,2304]{1,0:T(8,128)(2,1)S(1)}, bf16[128,2304]{1,0:T(8,128)(2,1)S(1)}, u32[]{:S(2)}, u32[]{:S(2)}) collective-permute-start(bf16[128,2304]{1,0:T(8,128)(2,1)S(1)} %reduce-precision_convert_fusion.24), channel_id=1, source_target_pairs={{1,0},{2,3},{5,4},{6,7},{9,8},{10,11},{13,12},{14,15},{17,16},{18,... | collective-permute-start | bytes 1769480 | tf_op jit(solution)/shard_map/ppermute | solution.py:368
  222.1 40.1 %collective-permute-start.39 = (bf16[256,1152]{1,0:T(8,128)(2,1)}, bf16[256,1152]{1,0:T(8,128)(2,1)}, u32[]{:S(2)}, u32[]{:S(2)}) collective-permute-start(bf16[256,1152]{1,0:T(8,128)(2,1)} %get-tuple-element.430), channel_id=1, source_target_pairs={{0,16},{16,0},{1,17},{17,1},{2,18},{18,2},{3,19},{19,3},{4,20},{20... | collective-permute-start | bytes 1769480 | tf_op jit(solution)/shard_map/ppermute | solution.py:445
  287.3 28.3 %collective-permute-start.15 = (bf16[128,2304]{1,0:T(8,128)(2,1)}, bf16[128,2304]{1,0:T(8,128)(2,1)}, u32[]{:S(2)}, u32[]{:S(2)}) collective-permute-start(bf16[128,2304]{1,0:T(8,128)(2,1)} %get-tuple-element.203), channel_id=1, source_target_pairs={{0,1},{3,2},{4,5},{7,6},{8,9},{11,10},{12,13},{15,14},{16,17},{19,... | collective-permute-start | bytes 1769480 | tf_op jit(solution)/shard_map/ppermute | solution.py:352
  289.6 27.5 %collective-permute-start.17 = (bf16[128,2304]{1,0:T(8,128)(2,1)}, bf16[128,2304]{1,0:T(8,128)(2,1)}, u32[]{:S(2)}, u32[]{:S(2)}) collective-permute-start(bf16[128,2304]{1,0:T(8,128)(2,1)} %get-tuple-element.206), channel_id=1, source_target_pairs={{0,1},{3,2},{4,5},{7,6},{8,9},{11,10},{12,13},{15,14},{16,17},{19,... | collective-permute-start | bytes 1769480 | tf_op jit(solution)/shard_map/ppermute | solution.py:352
  313.9 26.3 %collective-permute-start.23 = (bf16[128,2304]{1,0:T(8,128)(2,1)}, bf16[128,2304]{1,0:T(8,128)(2,1)S(1)}, u32[]{:S(2)}, u32[]{:S(2)}) collective-permute-start(bf16[128,2304]{1,0:T(8,128)(2,1)} %get-tuple-element.215), channel_id=1, source_target_pairs={{0,1},{3,2},{4,5},{7,6},{8,9},{11,10},{12,13},{15,14},{16,17},{19,... | collective-permute-start | bytes 1769480 | tf_op jit(solution)/shard_map/ppermute | solution.py:352
  322.8 37.8 %collective-permute-start.20 = (bf16[128,2304]{1,0:T(8,128)(2,1)S(1)}, bf16[128,2304]{1,0:T(8,128)(2,1)S(1)}, u32[]{:S(2)}, u32[]{:S(2)}) collective-permute-start(bf16[128,2304]{1,0:T(8,128)(2,1)S(1)} %reduce-precision_convert_fusion.21), channel_id=1, source_target_pairs={{1,0},{2,3},{5,4},{6,7},{9,8},{10,11},{13,12},{14,15},{17,16},{18,... | collective-permute-start | bytes 1769480 | tf_op jit(solution)/shard_map/ppermute | solution.py:368
  328.9 31.7 %collective-permute-start.21 = (bf16[128,2304]{1,0:T(8,128)(2,1)S(1)}, bf16[128,2304]{1,0:T(8,128)(2,1)S(1)}, u32[]{:S(2)}, u32[]{:S(2)}) collective-permute-start(bf16[128,2304]{1,0:T(8,128)(2,1)S(1)} %reduce-precision_convert_fusion.19), channel_id=1, source_target_pairs={{1,0},{2,3},{5,4},{6,7},{9,8},{10,11},{13,12},{14,15},{17,16},{18,... | collective-permute-start | bytes 1769480 | tf_op jit(solution)/shard_map/ppermute | solution.py:368
  364.8 47.4 %collective-permute-start.26 = (bf16[128,2304]{1,0:T(8,128)(2,1)}, bf16[128,2304]{1,0:T(8,128)(2,1)}, u32[]{:S(2)}, u32[]{:S(2)}) collective-permute-start(bf16[128,2304]{1,0:T(8,128)(2,1)} %reduce-precision_convert_fusion.16), channel_id=1, source_target_pairs={{1,0},{2,3},{5,4},{6,7},{9,8},{10,11},{13,12},{14,15},{17,16},{18,... | collective-permute-start | bytes 1769480 | tf_op jit(solution)/shard_map/ppermute | solution.py:368
  366.1 46.6 %collective-permute-start.25 = (bf16[128,2304]{1,0:T(8,128)(2,1)}, bf16[128,2304]{1,0:T(8,128)(2,1)}, u32[]{:S(2)}, u32[]{:S(2)}) collective-permute-start(bf16[128,2304]{1,0:T(8,128)(2,1)} %reduce-precision_convert_fusion.17), channel_id=1, source_target_pairs={{1,0},{2,3},{5,4},{6,7},{9,8},{10,11},{13,12},{14,15},{17,16},{18,... | collective-permute-start | bytes 1769480 | tf_op jit(solution)/shard_map/ppermute | solution.py:368
  392.6 58.3 %collective-permute-start.27 = (bf16[128,2304]{1,0:T(8,128)(2,1)}, bf16[128,2304]{1,0:T(8,128)(2,1)}, u32[]{:S(2)}, u32[]{:S(2)}) collective-permute-start(bf16[128,2304]{1,0:T(8,128)(2,1)} %get-tuple-element.237), channel_id=1, source_target_pairs={{0,1},{3,2},{4,5},{7,6},{8,9},{11,10},{12,13},{15,14},{16,17},{19,... | collective-permute-start | bytes 1769480 | tf_op jit(solution)/shard_map/ppermute | solution.py:352
  405.4 48.7 %collective-permute-start.33 = (bf16[128,2304]{1,0:T(8,128)(2,1)}, bf16[128,2304]{1,0:T(8,128)(2,1)}, u32[]{:S(2)}, u32[]{:S(2)}) collective-permute-start(bf16[128,2304]{1,0:T(8,128)(2,1)} %get-tuple-element.242), channel_id=1, source_target_pairs={{0,1},{3,2},{4,5},{7,6},{8,9},{11,10},{12,13},{15,14},{16,17},{19,... | collective-permute-start | bytes 1769480 | tf_op jit(solution)/shard_map/ppermute | solution.py:352
  407.5 53.4 %collective-permute-start.29 = (bf16[256,1152]{1,0:T(8,128)(2,1)}, bf16[256,1152]{1,0:T(8,128)(2,1)}, u32[]{:S(2)}, u32[]{:S(2)}) collective-permute-start(bf16[256,1152]{1,0:T(8,128)(2,1)} %get-tuple-element.434), channel_id=1, source_target_pairs={{0,16},{16,0},{1,17},{17,1},{2,18},{18,2},{3,19},{19,3},{4,20},{20... | collective-permute-start | bytes 1769480 | tf_op jit(solution)/shard_map/ppermute | solution.py:445
  412.3 76.6 %collective-permute-start.41 = (bf16[256,4608]{1,0:T(8,128)(2,1)}, bf16[256,4608]{1,0:T(8,128)(2,1)}, u32[]{:S(2)}, u32[]{:S(2)}) collective-permute-start(bf16[256,4608]{1,0:T(8,128)(2,1)} %constant_dynamic-update-slice_fusion.4), channel_id=1, source_target_pairs={{0,16},{16,0},{1,17},{17,1},{2,18},{18,2},{3,19},{19,3},{4,20},{20... | collective-permute-start | bytes 7077896 | tf_op jit(solution)/shard_map/ppermute | solution.py:445
  448.6 30.0 %collective-permute-start.35 = (bf16[128,2304]{1,0:T(8,128)(2,1)}, bf16[128,2304]{1,0:T(8,128)(2,1)}, u32[]{:S(2)}, u32[]{:S(2)}) collective-permute-start(bf16[128,2304]{1,0:T(8,128)(2,1)} %get-tuple-element.248), channel_id=1, source_target_pairs={{0,1},{3,2},{4,5},{7,6},{8,9},{11,10},{12,13},{15,14},{16,17},{19,... | collective-permute-start | bytes 1769480 | tf_op jit(solution)/shard_map/ppermute | solution.py:352
  452.2 24.3 %collective-permute-start.28 = (bf16[128,2304]{1,0:T(8,128)(2,1)S(1)}, bf16[128,2304]{1,0:T(8,128)(2,1)}, u32[]{:S(2)}, u32[]{:S(2)}) collective-permute-start(bf16[128,2304]{1,0:T(8,128)(2,1)S(1)} %reduce-precision_convert_fusion.15), channel_id=1, source_target_pairs={{1,2},{2,1},{5,6},{6,5},{9,10},{10,9},{13,14},{14,13},{17,18},{18,... | collective-permute-start | bytes 1769480 | tf_op jit(solution)/shard_map/ppermute | solution.py:361
  476.4 274.8 %reduce-scatter.5.cloned.1.call-start = ((), (), s32[]{:S(2)}) async-start(), calls=%async_computation.7 | async-start | bytes 13271040 | tf_op jit(solution)/shard_map/reduce_scatter | solution.py:460
  478.6 33.1 %collective-permute-start.36 = (bf16[128,2304]{1,0:T(8,128)(2,1)}, bf16[128,2304]{1,0:T(8,128)(2,1)}, u32[]{:S(2)}, u32[]{:S(2)}) collective-permute-start(bf16[128,2304]{1,0:T(8,128)(2,1)} %reduce-precision_convert_fusion.13), channel_id=1, source_target_pairs={{1,0},{2,3},{5,4},{6,7},{9,8},{10,11},{13,12},{14,15},{17,16},{18,... | collective-permute-start | bytes 1769480 | tf_op jit(solution)/shard_map/ppermute | solution.py:368
  481.3 26.9 %collective-permute-start.38 = (bf16[128,2304]{1,0:T(8,128)(2,1)S(1)}, bf16[128,2304]{1,0:T(8,128)(2,1)}, u32[]{:S(2)}, u32[]{:S(2)}) collective-permute-start(bf16[128,2304]{1,0:T(8,128)(2,1)S(1)} %reduce-precision_convert_fusion.12), channel_id=1, source_target_pairs={{1,2},{2,1},{5,6},{6,5},{9,10},{10,9},{13,14},{14,13},{17,18},{18,... | collective-permute-start | bytes 1769480 | tf_op jit(solution)/shard_map/ppermute | solution.py:361
  485.3 26.3 %collective-permute-start.37 = (bf16[128,2304]{1,0:T(8,128)(2,1)}, bf16[128,2304]{1,0:T(8,128)(2,1)}, u32[]{:S(2)}, u32[]{:S(2)}) collective-permute-start(bf16[128,2304]{1,0:T(8,128)(2,1)} %reduce-precision_convert_fusion.11), channel_id=1, source_target_pairs={{1,0},{2,3},{5,4},{6,7},{9,8},{10,11},{13,12},{14,15},{17,16},{18,... | collective-permute-start | bytes 1769480 | tf_op jit(solution)/shard_map/ppermute | solution.py:368
  488.8 39.5 %collective-permute-start.47 = (bf16[128,2304]{1,0:T(8,128)(2,1)}, bf16[128,2304]{1,0:T(8,128)(2,1)}, u32[]{:S(2)}, u32[]{:S(2)}) collective-permute-start(bf16[128,2304]{1,0:T(8,128)(2,1)} %reduce-precision_convert_fusion.10), channel_id=1, source_target_pairs={{1,2},{2,1},{5,6},{6,5},{9,10},{10,9},{13,14},{14,13},{17,18},{18,... | collective-permute-start | bytes 1769480 | tf_op jit(solution)/shard_map/ppermute | solution.py:361
  510.4 42.3 %collective-permute-start.48 = (bf16[128,2304]{1,0:T(8,128)(2,1)}, bf16[128,2304]{1,0:T(8,128)(2,1)}, u32[]{:S(2)}, u32[]{:S(2)}) collective-permute-start(bf16[128,2304]{1,0:T(8,128)(2,1)} %reduce-precision_convert_fusion.9), channel_id=1, source_target_pairs={{1,0},{2,3},{5,4},{6,7},{9,8},{10,11},{13,12},{14,15},{17,16},{18,... | collective-permute-start | bytes 1769480 | tf_op jit(solution)/shard_map/ppermute | solution.py:368
  533.2 51.0 %collective-permute-start.44 = (bf16[256,512]{1,0:T(8,128)(2,1)}, bf16[256,512]{1,0:T(8,128)(2,1)}, u32[]{:S(2)}, u32[]{:S(2)}) collective-permute-start(bf16[256,512]{1,0:T(8,128)(2,1)} %convert_element_type.547), channel_id=1, source_target_pairs={{0,4},{4,0},{8,12},{12,8},{1,5},{5,1},{9,13},{13,9},{2,6},{6,2},{1... | collective-permute-start | bytes 786440 | tf_op jit(solution)/shard_map/ppermute | solution.py:589
  535.2 49.3 %collective-permute-start.45 = (bf16[256,512]{1,0:T(8,128)(2,1)}, bf16[256,512]{1,0:T(8,128)(2,1)}, u32[]{:S(2)}, u32[]{:S(2)}) collective-permute-start(bf16[256,512]{1,0:T(8,128)(2,1)} %convert_element_type.548), channel_id=1, source_target_pairs={{0,8},{4,12},{8,0},{12,4},{1,9},{5,13},{9,1},{13,5},{2,10},{6,14},... | collective-permute-start | bytes 786440 | tf_op jit(solution)/shard_map/ppermute | solution.py:589
  537.5 47.0 %collective-permute-start.46 = (bf16[256,512]{1,0:T(8,128)(2,1)}, bf16[256,512]{1,0:T(8,128)(2,1)}, u32[]{:S(2)}, u32[]{:S(2)}) collective-permute-start(bf16[256,512]{1,0:T(8,128)(2,1)} %convert_element_type.549), channel_id=1, source_target_pairs={{0,12},{4,8},{8,4},{12,0},{1,13},{5,9},{9,5},{13,1},{2,14},{6,10},... | collective-permute-start | bytes 786440 | tf_op jit(solution)/shard_map/ppermute | solution.py:589
  552.6 24.4 %collective-permute-start.59 = (bf16[256,1152]{1,0:T(8,128)(2,1)}, bf16[256,1152]{1,0:T(8,128)(2,1)}, u32[]{:S(2)}, u32[]{:S(2)}) collective-permute-start(bf16[256,1152]{1,0:T(8,128)(2,1)} %get-tuple-element.418), channel_id=1, source_target_pairs={{0,16},{16,0},{1,17},{17,1},{2,18},{18,2},{3,19},{19,3},{4,20},{20... | collective-permute-start | bytes 1769480 | tf_op jit(solution)/shard_map/ppermute | solution.py:445
  586.6 23.9 %collective-permute-start.56 = (bf16[256,1024]{1,0:T(8,128)(2,1)S(1)}, bf16[256,1024]{1,0:T(8,128)(2,1)S(1)}, u32[]{:S(2)}, u32[]{:S(2)}) collective-permute-start(bf16[256,1024]{1,0:T(8,128)(2,1)S(1)} %pad_maximum_fusion.17), channel_id=1, source_target_pairs={{0,16},{16,0},{1,17},{17,1},{2,18},{18,2},{3,19},{19,3},{4,20},{20... | collective-permute-start | bytes 1572872 | tf_op jit(solution)/shard_map/ppermute | solution.py:445
  590.7 31.2 %collective-permute-start.63 = (bf16[128,2304]{1,0:T(8,128)(2,1)S(1)}, bf16[128,2304]{1,0:T(8,128)(2,1)S(1)}, u32[]{:S(2)}, u32[]{:S(2)}) collective-permute-start(bf16[128,2304]{1,0:T(8,128)(2,1)S(1)} %get-tuple-element.300), channel_id=1, source_target_pairs={{0,1},{3,2},{4,5},{7,6},{8,9},{11,10},{12,13},{15,14},{16,17},{19,... | collective-permute-start | bytes 1769480 | tf_op jit(solution)/shard_map/ppermute | solution.py:352
  609.1 24.7 %collective-permute-start.65 = (bf16[128,2304]{1,0:T(8,128)(2,1)S(1)}, bf16[128,2304]{1,0:T(8,128)(2,1)S(1)}, u32[]{:S(2)}, u32[]{:S(2)}) collective-permute-start(bf16[128,2304]{1,0:T(8,128)(2,1)S(1)} %get-tuple-element.306), channel_id=1, source_target_pairs={{0,1},{3,2},{4,5},{7,6},{8,9},{11,10},{12,13},{15,14},{16,17},{19,... | collective-permute-start | bytes 1769480 | tf_op jit(solution)/shard_map/ppermute | solution.py:352
  610.5 35.6 %collective-permute-start.69 = (bf16[128,2304]{1,0:T(8,128)(2,1)S(1)}, bf16[128,2304]{1,0:T(8,128)(2,1)S(1)}, u32[]{:S(2)}, u32[]{:S(2)}) collective-permute-start(bf16[128,2304]{1,0:T(8,128)(2,1)S(1)} %get-tuple-element.310), channel_id=1, source_target_pairs={{0,1},{3,2},{4,5},{7,6},{8,9},{11,10},{12,13},{15,14},{16,17},{19,... | collective-permute-start | bytes 1769480 | tf_op jit(solution)/shard_map/ppermute | solution.py:352
  624.6 42.7 %collective-permute-start.66 = (bf16[128,2304]{1,0:T(8,128)(2,1)S(1)}, bf16[128,2304]{1,0:T(8,128)(2,1)S(1)}, u32[]{:S(2)}, u32[]{:S(2)}) collective-permute-start(bf16[128,2304]{1,0:T(8,128)(2,1)S(1)} %reduce-precision_convert_fusion.5), channel_id=1, source_target_pairs={{1,0},{2,3},{5,4},{6,7},{9,8},{10,11},{13,12},{14,15},{17,16},{18,... | collective-permute-start | bytes 1769480 | tf_op jit(solution)/shard_map/ppermute | solution.py:368
  634.7 32.5 %collective-permute-start.67 = (bf16[128,2304]{1,0:T(8,128)(2,1)S(1)}, bf16[128,2304]{1,0:T(8,128)(2,1)S(1)}, u32[]{:S(2)}, u32[]{:S(2)}) collective-permute-start(bf16[128,2304]{1,0:T(8,128)(2,1)S(1)} %reduce-precision_convert_fusion.3), channel_id=1, source_target_pairs={{1,0},{2,3},{5,4},{6,7},{9,8},{10,11},{13,12},{14,15},{17,16},{18,... | collective-permute-start | bytes 1769480 | tf_op jit(solution)/shard_map/ppermute | solution.py:368
  684.7 49.3 %all-to-all-start = ((bf16[4,288,1664]{2,1,0:T(8,128)(2,1)}), bf16[4,288,1664]{2,1,0:T(8,128)(2,1)}, u32[]{:S(2)}, u32[]{:S(2)}) async-start(bf16[4,288,1664]{2,1,0:T(8,128)(2,1)} %bitcast.97), calls=%async_computation.1 | async-start | bytes 7667712 | tf_op jit(solution)/shard_map/all_to_all | solution.py:635
  690.9 46.0 %collective-permute-start.71 = (bf16[128,2304]{1,0:T(8,128)(2,1)}, bf16[128,2304]{1,0:T(8,128)(2,1)}, u32[]{:S(2)}, u32[]{:S(2)}) collective-permute-start(bf16[128,2304]{1,0:T(8,128)(2,1)} %reduce-precision_convert_fusion.1), channel_id=1, source_target_pairs={{1,0},{2,3},{5,4},{6,7},{9,8},{10,11},{13,12},{14,15},{17,16},{18,... | collective-permute-start | bytes 1769480 | tf_op jit(solution)/shard_map/ppermute | solution.py:368
  697.2 39.6 %collective-permute-start.72 = (bf16[128,2304]{1,0:T(8,128)(2,1)}, bf16[128,2304]{1,0:T(8,128)(2,1)}, u32[]{:S(2)}, u32[]{:S(2)}) collective-permute-start(bf16[128,2304]{1,0:T(8,128)(2,1)} %reduce-precision_convert_fusion), channel_id=1, source_target_pairs={{1,0},{2,3},{5,4},{6,7},{9,8},{10,11},{13,12},{14,15},{17,16},{18,... | collective-permute-start | bytes 1769480 | tf_op jit(solution)/shard_map/ppermute | solution.py:368
  (126 other events, 1580.4 us)
Sparse Core Ops, SparseCore 0:
  15.2 53.9 all-gather.2
  71.0 175.9 all-gather.4
  476.6 61.9 reduce-scatter.2
  541.5 121.2 reduce-scatter.4

commit v2 on v1

v2 whole, which is shorter than its diff:
```python
import functools

import jax
import jax.numpy as jnp
from jax import lax
from jax.experimental import pallas as pl
from jax.experimental.pallas import tpu as pltpu
from jax.sharding import PartitionSpec as P

HEAD_SIZE = 256
EPS = 1e-06
CAP = 50.0
BASE = 10000.0
BF = jnp.bfloat16
F32 = jnp.float32
PAD = 128
VMEM_LIMIT = 60 * 1024 * 1024
GELU_C = 0.7978845608028654
GELU_A = 0.044715


def apply_norm(values):
    factor = lax.rsqrt(jnp.mean(values * values, axis=-1, keepdims=True) + EPS)
    return values * factor, factor


def norm_backward(upstream, scaled, factor):
    return factor * (upstream - scaled * jnp.mean(upstream * scaled, axis=-1, keepdims=True))


def rotation(token_positions, width_size):
    half_width = width_size // 2
    inverse = BASE ** (-(jnp.arange(half_width, dtype=F32) * 2.0) / width_size)
    angles = token_positions.astype(F32)[:, None] * inverse[None, :]
    return jnp.cos(angles), jnp.sin(angles)


def mm(a, b):
    return jnp.dot(a, b, preferred_element_type=F32)


def mm_t(a, b):
    return lax.dot_general(a, b, (((1,), (1,)), ((), ())), preferred_element_type=F32)


def tmm(a, b):
    return lax.dot_general(a, b, (((0,), (0,)), ((), ())), preferred_element_type=F32)


def low(values):
    return lax.reduce_precision(values, 8, 7).astype(BF)


def call(body, out_shape, grid, in_specs, out_specs, scratch=(), flops=0, moved=0):
    return pl.pallas_call(
        body,
        out_shape=out_shape,
        grid_spec=pltpu.PrefetchScalarGridSpec(
            num_scalar_prefetch=0,
            grid=grid,
            in_specs=in_specs,
            out_specs=out_specs,
            scratch_shapes=list(scratch),
        ),
        compiler_params=pltpu.CompilerParams(
            dimension_semantics=("arbitrary",) * len(grid), vmem_limit_bytes=VMEM_LIMIT
        ),
        cost_estimate=pl.CostEstimate(flops=flops, bytes_accessed=moved, transcendentals=0),
    )


def shape(dims, dtype):
    return jax.ShapeDtypeStruct(dims, dtype)


def whole(dims):
    return pl.BlockSpec(dims, lambda *_: (0,) * len(dims))


def project_body(n_rot, x_ref, w_ref, cos_ref, sin_ref, out_ref):
    half = HEAD_SIZE // 2
    y = mm(x_ref[...], w_ref[...])
    rotate = pl.program_id(0) < n_rot
    cos = jnp.where(rotate, cos_ref[...], 1.0)
    sin = jnp.where(rotate, sin_ref[...], 0.0)
    a, b = y[:, :half], y[:, half:]
    out_ref[:, :half] = (a * cos - b * sin).astype(BF)
    out_ref[:, half:] = (b * cos + a * sin).astype(BF)


def project(normed, weights, columns, n_rot, cos, sin):
    rows, width = normed.shape
    return call(
        functools.partial(project_body, n_rot),
        shape((rows, columns), BF),
        (columns // HEAD_SIZE,),
        [
            whole((rows, width)),
            pl.BlockSpec((width, HEAD_SIZE), lambda j: (0, j)),
            whole(cos.shape),
            whole(sin.shape),
        ],
        pl.BlockSpec((rows, HEAD_SIZE), lambda j: (0, j)),
        flops=2 * rows * width * columns,
        moved=2 * (rows * width + width * columns + rows * columns),
    )(normed, weights, cos, sin)


def scores(q, k, allowed):
    soft = HEAD_SIZE ** (-0.5)
    bend = jnp.tanh(mm_t(q, k) * (soft / CAP))
    return bend, jnp.where(allowed, jnp.exp(CAP * bend), 0.0)


def attend_body(n_q, n_kv, n_pieces, chunks, *refs):
    hd = HEAD_SIZE
    q_ref, qpos_ref, kpos_ref, w_ref = refs[:4]
    pieces = refs[4 : 4 + n_pieces]
    heads_ref, attended_ref, den_ref = refs[4 + n_pieces : 7 + n_pieces]
    outs = refs[7 + n_pieces :]
    qpos = qpos_ref[...]
    for h in range(n_q):
        kv = h // (n_q // n_kv)
        q = q_ref[:, h * hd : (h + 1) * hd]
        num, den = 0.0, 0.0
        for j, piece in enumerate(pieces):
            size = piece.shape[0]
            allowed = kpos_ref[:, j * size : (j + 1) * size] <= qpos
            _, weight = scores(q, piece[:, kv * hd : (kv + 1) * hd], allowed)
            den = den + jnp.sum(weight, axis=-1, keepdims=True)
            v = piece[:, (n_kv + kv) * hd : (n_kv + kv + 1) * hd]
            num = num + mm(weight.astype(BF), v)
        heads = num / den
        heads_ref[:, h * hd : (h + 1) * hd] = heads
        attended_ref[:, h * hd : (h + 1) * hd] = heads.astype(BF)
        den_ref[:, h * PAD : (h + 1) * PAD] = jnp.broadcast_to(den, (den.shape[0], PAD))
    put_chunks(mm_t(attended_ref[...], w_ref[...]), outs)


def put_chunks(value, outs):
    size = value.shape[0] // len(outs)
    for i, out in enumerate(outs):
        out[...] = value[i * size : (i + 1) * size].astype(BF)


def attend(q, q_block, pieces, qpos, kpos, n_q, n_kv, weights, out_block, chunks):
    hd = HEAD_SIZE
    seq_dev = qpos.shape[0]
    width = weights.shape[0]
    specs = [pl.BlockSpec((seq_dev, n_q * hd), lambda i: (q_block, 0))]
    specs += [whole(qpos.shape), whole(kpos.shape)]
    specs.append(pl.BlockSpec((width, n_q * hd), lambda i: (0, out_block)))
    arrays = [q, qpos, kpos, weights]
    for array, size, row, col in pieces:
        specs.append(pl.BlockSpec((size, 2 * n_kv * hd), lambda i, row=row, col=col: (row, col)))
        arrays.append(array)
    seq = kpos.shape[1]
    part = (seq_dev // chunks, width)
    return call(
        functools.partial(attend_body, n_q, n_kv, len(pieces), chunks),
        (
            shape((seq_dev, n_q * hd), F32),
            shape((seq_dev, n_q * hd), BF),
            shape((seq_dev, n_q * PAD), F32),
        )
        + (shape(part, BF),) * chunks,
        (1,),
        specs,
        (whole((seq_dev, n_q * hd)), whole((seq_dev, n_q * hd)), whole((seq_dev, n_q * PAD)))
        + (whole(part),) * chunks,
        flops=4 * n_q * seq_dev * seq * hd + 2 * seq_dev * n_q * hd * width,
        moved=2 * (2 * n_kv * hd * seq + 4 * seq_dev * n_q * hd + 2 * n_q * hd * width),
    )(*arrays)


def attend_back_body(n_q, n_kv, n_pieces, chunks, *refs):
    hd = HEAD_SIZE
    half = hd // 2
    soft = hd ** (-0.5)
    q_ref, qpos_ref, kpos_ref, heads_ref, den_ref, cos_ref, sin_ref, w_ref = refs[:8]
    pieces = refs[8 : 8 + n_pieces]
    grads = refs[8 + n_pieces : 8 + n_pieces + chunks]
    q_back_ref, *outs = refs[8 + n_pieces + chunks :]
    attn_grad = jnp.concatenate([g[...] for g in grads], axis=0)
    qpos = qpos_ref[...]
    group = n_q // n_kv
    for h in range(n_q):
        kv = h // group
        cols = slice(h * hd, (h + 1) * hd)
        k_cols = slice(kv * hd, (kv + 1) * hd)
        v_cols = slice((n_kv + kv) * hd, (n_kv + kv + 1) * hd)
        q = q_ref[:, cols]
        grad = mm(attn_grad, w_ref[:, cols])
        inverse = 1.0 / den_ref[:, h * PAD : h * PAD + 1]
        scaled = (grad * inverse).astype(BF)
        row_dot = jnp.sum(grad * heads_ref[:, cols], axis=-1, keepdims=True) * inverse
        q_grad = 0.0
        for j, piece in enumerate(pieces):
            size = piece.shape[0]
            allowed = kpos_ref[:, j * size : (j + 1) * size] <= qpos
            k, v = piece[:, k_cols], piece[:, v_cols]
            bend, weight = scores(q, k, allowed)
            prob = mm_t(scaled, v)
            score = (weight * (prob - row_dot) * (1.0 - bend * bend)).astype(BF)
            q_grad = q_grad + mm(score, k)
            k_term = tmm(score, q) * soft
            v_term = tmm(weight.astype(BF), scaled)
            if h % group == 0:
                outs[j][:, k_cols] = k_term
                outs[j][:, v_cols] = v_term
            else:
                outs[j][:, k_cols] += k_term
                outs[j][:, v_cols] += v_term
        q_grad = q_grad * soft
        a, b = q_grad[:, :half], q_grad[:, half:]
        q_back_ref[:, h * hd : h * hd + half] = (a * cos_ref[...] + b * sin_ref[...]).astype(BF)
        q_back_ref[:, h * hd + half : (h + 1) * hd] = (
            b * cos_ref[...] - a * sin_ref[...]
        ).astype(BF)


def attend_back(q, q_block, pieces, qpos, kpos, grads, heads, den, cos, sin, n_q, n_kv, weights, out_block):
    hd = HEAD_SIZE
    seq_dev = qpos.shape[0]
    width = weights.shape[0]
    specs = [pl.BlockSpec((seq_dev, n_q * hd), lambda i: (q_block, 0))]
    arrays = [q, qpos, kpos, heads, den, cos, sin]
    specs += [whole(a.shape) for a in arrays[1:]]
    specs.append(pl.BlockSpec((width, n_q * hd), lambda i: (0, out_block)))
    arrays.append(weights)
    out_shapes, out_specs = [shape((seq_dev, n_q * hd), BF)], [whole((seq_dev, n_q * hd))]
    for array, size, row, col in pieces:
        specs.append(pl.BlockSpec((size, 2 * n_kv * hd), lambda i, row=row, col=col: (row, col)))
        arrays.append(array)
        out_shapes.append(shape((size, 2 * n_kv * hd), F32))
        out_specs.append(whole((size, 2 * n_kv * hd)))
    arrays += grads
    specs += [whole(g.shape) for g in grads]
    seq = kpos.shape[1]
    return call(
        functools.partial(attend_back_body, n_q, n_kv, len(pieces), len(grads)),
        tuple(out_shapes),
        (1,),
        specs,
        tuple(out_specs),
        flops=10 * n_q * seq_dev * seq * hd + 2 * seq_dev * n_q * hd * width,
        moved=2 * (6 * n_kv * hd * seq + 8 * seq_dev * n_q * hd + 2 * n_q * hd * width),
    )(*arrays)


def input_back_body(n_q, n_kv, n_terms, chunks, *refs):
    hd = HEAD_SIZE
    half = hd // 2
    kc = n_kv * hd
    q_back_ref, x_ref, cos_ref, sin_ref, w_ref = refs[:5]
    terms = refs[5 : 5 + n_terms]
    back_ref, gain_ref, *outs = refs[5 + n_terms :]
    total = 0.0
    for term in terms:
        total = total + term[...].astype(F32)
    back_ref[:, : n_q * hd] = q_back_ref[...]
    for h in range(n_kv):
        start = (n_q + h) * hd
        a = total[:, h * hd : h * hd + half]
        b = total[:, h * hd + half : (h + 1) * hd]
        back_ref[:, start : start + half] = (a * cos_ref[...] + b * sin_ref[...]).astype(BF)
        back_ref[:, start + half : start + hd] = (b * cos_ref[...] - a * sin_ref[...]).astype(BF)
    back_ref[:, n_q * hd + kc :] = total[:, kc:].astype(BF)
    grad = mm_t(back_ref[...], w_ref[...])
    xhat, _ = apply_norm(x_ref[...].astype(F32))
    gain_ref[...] = jnp.broadcast_to(jnp.sum(grad * xhat, axis=0, keepdims=True), gain_ref.shape)
    put_chunks(grad, outs)


def input_back_call(q_back, terms, x, block, cos, sin, weights, n_q, n_kv, chunks):
    hd = HEAD_SIZE
    seq_dev = q_back.shape[0]
    width = weights.shape[0]
    cols = (n_q + 2 * n_kv) * hd
    part = (seq_dev // chunks, width)
    return call(
        functools.partial(input_back_body, n_q, n_kv, len(terms), chunks),
        (shape((seq_dev, cols), BF), shape((8, width), F32)) + (shape(part, BF),) * chunks,
        (1,),
        [
            whole(q_back.shape),
            pl.BlockSpec((seq_dev, width), lambda i: (block, 0)),
            whole(cos.shape),
            whole(sin.shape),
            pl.BlockSpec((width, cols), lambda i: (0, 0)),
        ]
        + [whole(t.shape) for t in terms],
        (whole((seq_dev, cols)), whole((8, width))) + (whole(part),) * chunks,
        flops=2 * seq_dev * cols * width,
        moved=2 * (width * cols + 3 * seq_dev * width + 4 * seq_dev * cols),
    )(q_back, x, cos, sin, weights, *terms)


def choose(flag_ref, total_ref, third_ref):
    total, third = total_ref[...].astype(F32), third_ref[...].astype(F32)
    return jnp.where(flag_ref[0] == 1, total, third)


def add_gain(gain_ref, rows):
    @pl.when(pl.program_id(0) == 0)
    def _():
        gain_ref[...] = jnp.zeros_like(gain_ref)

    for i, value in enumerate(rows):
        gain_ref[i : i + 1, :] += jnp.sum(value, axis=0, keepdims=True)


def post_attend_body(flag_ref, total_ref, third_ref, x_ref, scale_ref, a_ref, out_ref):
    value = choose(flag_ref, total_ref, third_ref)
    ahat, _ = apply_norm(value)
    h1hat, _ = apply_norm(x_ref[...].astype(F32) + ahat * scale_ref[1:2, :])
    a_ref[...] = value.astype(BF)
    out_ref[...] = (h1hat * scale_ref[2:3, :]).astype(BF)


def post_ffn_body(
    flag_ref, total_ref, third_ref, a_ref, x_ref, dy_ref, scale_ref, out_ref, grad_ref, gain_ref
):
    fhat, factor = apply_norm(choose(flag_ref, total_ref, third_ref))
    ahat, _ = apply_norm(a_ref[...].astype(F32))
    hidden_one = x_ref[...].astype(F32) + ahat * scale_ref[1:2, :]
    scale = scale_ref[3:4, :]
    dy = dy_ref[...].astype(F32)
    out_ref[...] = (hidden_one + fhat * scale).astype(BF)
    grad_ref[...] = norm_backward(dy * scale, fhat, factor).astype(BF)
    add_gain(gain_ref, [dy * fhat])


def post_mid_body(
    flag_ref, total_ref, third_ref, a_ref, x_ref, dy_ref, scale_ref, one_ref, grad_ref, gain_ref
):
    mid = choose(flag_ref, total_ref, third_ref)
    ahat, fac_attn = apply_norm(a_ref[...].astype(F32))
    scale_attn, scale_mid = scale_ref[1:2, :], scale_ref[2:3, :]
    h1hat, fac_mid = apply_norm(x_ref[...].astype(F32) + ahat * scale_attn)
    one_grad = dy_ref[...].astype(F32) + norm_backward(mid * scale_mid, h1hat, fac_mid)
    one_ref[...] = one_grad
    grad_ref[...] = norm_backward(one_grad * scale_attn, ahat, fac_attn).astype(BF)
    add_gain(gain_ref, [mid * h1hat, one_grad * ahat])


def post_in_body(flag_ref, total_ref, third_ref, one_ref, x_ref, scale_ref, out_ref):
    grad = choose(flag_ref, total_ref, third_ref)
    xhat, factor = apply_norm(x_ref[...].astype(F32))
    back = norm_backward(grad * scale_ref[0:1, :], xhat, factor)
    out_ref[...] = (one_ref[...] + back).astype(BF)


def post(body, flag, pair_values, chunk_arrays, row_arrays, k, scales, outs, gain=False):
    rows, width = pair_values[0].shape
    steps = 2 if rows >= 128 else 1
    tile = (rows // steps, width)
    chunk = pl.BlockSpec(tile, lambda i: (i, 0))
    row = pl.BlockSpec(tile, lambda i: (k * steps + i, 0))
    located, located_specs = [], []
    for values in chunk_arrays:
        size = values[0].shape[0]
        base = (k * rows % size) // tile[0]
        located.append(values[k * rows // size])
        located_specs.append(pl.BlockSpec(tile, lambda i, base=base: (base + i, 0)))
    arrays = [flag, *pair_values, *located, *row_arrays, scales]
    specs = [pl.BlockSpec(memory_space=pltpu.SMEM), chunk, chunk, *located_specs]
    specs += [row] * len(row_arrays) + [whole(scales.shape)]
    out_shapes = [shape((rows, width), dtype) for dtype in outs]
    out_specs = [chunk] * len(outs)
    if gain:
        out_shapes.append(shape((8, width), F32))
        out_specs.append(whole((8, width)))
    return call(
        body,
        tuple(out_shapes),
        (steps,),
        specs,
        tuple(out_specs),
        flops=20 * rows * width,
        moved=14 * rows * width,
    )(*arrays)


def ffn_body(n_x, n_out, *refs):
    xs, (wg_ref, wu_ref, wd_ref) = refs[:n_x], refs[n_x : n_x + 3]
    gate_ref, up_ref, hid_ref = refs[n_x + 3 : n_x + 6]
    outs, (x_ref, acc) = refs[n_x + 6 : n_x + 6 + n_out], refs[n_x + 6 + n_out :]
    j = pl.program_id(0)

    @pl.when(j == 0)
    def _():
        gather_rows(xs, x_ref)
        acc[...] = jnp.zeros_like(acc)

    x = x_ref[...]
    gate = mm(x, wg_ref[...])
    up = mm(x, wu_ref[...])
    bend = jnp.tanh(GELU_C * (gate + GELU_A * gate * gate * gate))
    hidden = (0.5 * gate * (1.0 + bend) * up).astype(BF)
    gate_ref[...] = gate.astype(BF)
    up_ref[...] = up.astype(BF)
    hid_ref[...] = hidden
    acc[...] += mm_t(hidden, wd_ref[...])

    @pl.when(j == pl.num_programs(0) - 1)
    def _():
        put_chunks(acc[...], outs)


def gather_rows(pieces, out_ref):
    size = pieces[0].shape[0]
    for i, piece in enumerate(pieces):
        out_ref[i * size : (i + 1) * size, :] = piece[...]


def ffn(xs, weights, ff, n_out):
    width = xs[0].shape[1]
    rows = xs[0].shape[0] * len(xs)
    tile = 256
    steps = ff // tile
    col = lambda part: pl.BlockSpec((width, tile), lambda j: (0, part * steps + j))
    act = pl.BlockSpec((rows, tile), lambda j: (0, j))
    part = (rows // n_out, width)
    return call(
        functools.partial(ffn_body, len(xs), n_out),
        (shape((rows, ff), BF),) * 3 + (shape(part, BF),) * n_out,
        (steps,),
        [whole(xs[0].shape)] * len(xs) + [col(0), col(1), col(2)],
        (act, act, act) + (whole(part),) * n_out,
        [pltpu.VMEM((rows, width), BF), pltpu.VMEM((rows, width), F32)],
        flops=6 * rows * width * ff,
        moved=6 * width * ff + 4 * rows * width + 6 * rows * ff,
    )(*xs, weights, weights, weights)


def ffn_back_body(n_y, n_out, *refs):
    ys, (wg_ref, wu_ref, wd_ref, gate_ref, up_ref) = refs[:n_y], refs[n_y : n_y + 5]
    rest = refs[n_y + 5 :]
    both_ref, outs, (y_ref, acc) = rest[0], rest[1 : 1 + n_out], rest[1 + n_out :]
    tile = gate_ref.shape[1]
    j = pl.program_id(0)

    @pl.when(j == 0)
    def _():
        gather_rows(ys, y_ref)
        acc[...] = jnp.zeros_like(acc)

    grad = mm(y_ref[...], wd_ref[...])
    gate, up = gate_ref[...].astype(F32), up_ref[...].astype(F32)
    square = gate * gate
    bend = jnp.tanh(GELU_C * gate * (1.0 + GELU_A * square))
    rise = 0.5 * (1.0 + bend)
    slope = rise + 0.5 * gate * (1.0 - bend * bend) * (GELU_C * (1.0 + 3.0 * GELU_A * square))
    d_gate = (grad * up * slope).astype(BF)
    d_up = (grad * (gate * rise)).astype(BF)
    both_ref[:, :tile] = d_gate
    both_ref[:, tile:] = d_up
    acc[...] += mm_t(d_gate, wg_ref[...]) + mm_t(d_up, wu_ref[...])

    @pl.when(j == pl.num_programs(0) - 1)
    def _():
        put_chunks(acc[...], outs)


FF_TILE = 256


def ffn_back(ys, weights, gate, up, ff, n_out):
    width = ys[0].shape[1]
    rows = ys[0].shape[0] * len(ys)
    tile = FF_TILE
    steps = ff // tile
    col = lambda part: pl.BlockSpec((width, tile), lambda j: (0, part * steps + j))
    act = pl.BlockSpec((rows, tile), lambda j: (0, j))
    part = (rows // n_out, width)
    return call(
        functools.partial(ffn_back_body, len(ys), n_out),
        (shape((rows, 2 * ff), BF),) + (shape(part, BF),) * n_out,
        (steps,),
        [whole(ys[0].shape)] * len(ys) + [col(0), col(1), col(2), act, act],
        (pl.BlockSpec((rows, 2 * tile), lambda j: (0, j)),) + (whole(part),) * n_out,
        [pltpu.VMEM((rows, width), BF), pltpu.VMEM((rows, width), F32)],
        flops=6 * rows * width * ff,
        moved=6 * width * ff + 4 * rows * width + 8 * rows * ff,
    )(*ys, weights, weights, weights, gate, up)


def sum_body(cuts, part_ref, *outs):
    total = 0.0
    for i in range(part_ref.shape[0]):
        total = total + part_ref[i].astype(F32)
    for out, spans in zip(outs, cuts):
        at = 0
        for start, stop in spans:
            out[:, at : at + stop - start] = total[:, start:stop]
            at += stop - start


def sum_parts(parts, tile, cuts):
    n, rows, cols = parts.shape
    steps = cols // tile
    sizes = [sum(stop - start for start, stop in spans) for spans in cuts]
    return call(
        functools.partial(sum_body, cuts),
        tuple(shape((rows, size * steps), F32) for size in sizes),
        (steps,),
        [pl.BlockSpec((n, rows, tile), lambda j: (0, 0, j))],
        tuple(pl.BlockSpec((rows, size), lambda j: (0, j)) for size in sizes),
        flops=n * rows * cols,
        moved=2 * n * rows * cols + 4 * rows * cols,
    )(parts)


def pack_body(*refs):
    start = 0
    for ref in refs[:-1]:
        refs[-1][:, start : start + ref.shape[1]] = ref[...].astype(BF)
        start += ref.shape[1]


def pack(arrays, steps):
    rows = arrays[0].shape[0] // steps
    cols = sum(a.shape[1] for a in arrays)
    return call(
        pack_body,
        shape((rows * steps, cols), BF),
        (steps,),
        [pl.BlockSpec((rows, a.shape[1]), lambda i: (i, 0)) for a in arrays],
        pl.BlockSpec((rows, cols), lambda i: (i, 0)),
        moved=4 * rows * steps * cols,
    )(*arrays)


class Chain:
    def __init__(self):
        self.token = None

    def after(self, *values):
        if self.token is None:
            return values
        return lax.optimization_barrier((*values, self.token))[:-1]

    def mark(self, value):
        self.token = value
        return value


class Reduce:
    def __init__(self, chain):
        self.chain, self.piece, self.first = chain, {}, {}
        self.sums, self.second, self.total, self.third = {}, {}, {}, {}
        self.line = lax.axis_size("tensor") == 4

    def send(self, k, piece):
        self.piece[k] = piece
        if self.line:
            self.first[k] = lax.ppermute(piece, "tensor", [(0, 1), (3, 2)])
        else:
            self.total[k] = lax.psum(piece.astype(F32), "tensor")

    def add(self, k):
        if self.line:
            piece, first = self.chain.after(self.piece[k], self.first[k])
            total = low(piece.astype(F32) + first.astype(F32))
            self.sums[k] = self.chain.mark(total)
            self.second[k] = lax.ppermute(total, "tensor", [(1, 2), (2, 1)])

    def join(self, k):
        if self.line:
            sums, second = self.chain.after(self.sums[k], self.second[k])
            total = low(sums.astype(F32) + second.astype(F32))
            self.total[k] = self.chain.mark(total)
            self.third[k] = lax.ppermute(total, "tensor", [(1, 0), (2, 3)])

    def load(self, pieces):
        for piece in pieces:
            self.send(len(self.piece), piece)

    def run(self, n, finish, hooks):
        for slot in range(n + 2):
            if slot < n:
                self.add(slot)
            if 0 < slot <= n:
                self.join(slot - 1)
            if slot >= 2:
                finish(slot - 2)
            if slot in hooks:
                hooks[slot]()

    def take(self, k):
        if self.line:
            return self.chain.after(self.total[k], self.third[k])
        return self.chain.after(self.total[k], self.total[k])


def local(
    tokens,
    span_order,
    w_query,
    w_key,
    value_weight,
    w_out,
    w_gate,
    w_up,
    w_down,
    gain_attn_in,
    gain_attn_out,
    gain_ffn_in,
    gain_ffn_out,
    cotangent,
):
    micros, batch, seq_dev, width = tokens.shape
    n_dp, n_ctx, n_t = lax.axis_size("dp"), lax.axis_size("ctx"), lax.axis_size("tensor")
    dpi, ctx, zi = lax.axis_index("dp"), lax.axis_index("ctx"), lax.axis_index("tensor")
    seq = seq_dev * n_ctx
    span_len = seq // span_order.shape[0]
    hd = HEAD_SIZE
    n_kv = w_key.shape[1] // hd
    n_q = w_query.shape[1] // hd
    ff = w_gate.shape[1]
    qc, kc, oc = w_query.shape[1], w_key.shape[1], w_out.shape[1]
    n_seqs, chunks = micros * batch, 2
    swap = n_ctx == 4
    pair = n_dp == 2

    row_index = jnp.arange(seq, dtype=jnp.int32)
    all_pos = span_order[row_index // span_len] * span_len + row_index % span_len
    by_dev = all_pos.reshape(n_ctx, seq_dev)
    query_pos = lax.dynamic_index_in_dim(by_dev, ctx, 0, keepdims=False)
    if swap:
        key_pos = jnp.concatenate(
            [lax.dynamic_index_in_dim(by_dev, ctx ^ j, 0, keepdims=False) for j in range(n_ctx)]
        )
    else:
        key_pos = all_pos
    qpos, kpos = query_pos[:, None], key_pos[None, :]
    cos, sin = rotation(query_pos, hd)

    gains = jnp.stack([gain_attn_in, gain_attn_out, gain_ffn_in, gain_ffn_out], axis=1)
    gains = jnp.pad(gains, ((0, 0), (0, PAD - gains.shape[1])))
    pack_attn = jnp.concatenate([w_query, w_key, value_weight, w_out, gains], axis=1)
    pack_ffn = jnp.concatenate([w_gate, w_up, w_down], axis=1)
    full_attn = lax.all_gather(pack_attn, ("dp", "ctx"), axis=0, tiled=True)
    full_ffn = lax.all_gather(pack_ffn, ("dp", "ctx"), axis=0, tiled=True)
    at_out = qc + 2 * kc
    out_block = at_out // oc
    pick = jnp.eye(8, PAD, dtype=BF)
    gain_cols = mm_t(pick, full_attn[:, at_out + oc :])
    scales = 1.0 + gain_cols

    chain = Chain()
    flips = [[(i, i ^ j) for i in range(n_ctx)] for j in range(n_ctx)]

    def half(full, owner):
        return lax.dynamic_slice_in_dim(full, owner * (width // 2), width // 2, 1)

    def swap_core(value):
        return lax.ppermute(value, "dp", [(0, 1), (1, 0)])

    def left_side(values):
        value = jnp.concatenate(chain.after(*values), axis=0)
        if not pair:
            return value
        return jnp.concatenate([half(value, dpi), swap_core(half(value, 1 - dpi))], axis=0)

    def right_side(values):
        value = jnp.concatenate(chain.after(*values), axis=0)
        return jnp.concatenate([value, swap_core(value)], axis=0) if pair else value

    def spread(grad):
        if pair:
            return lax.all_to_all(grad.reshape(n_ctx, -1, grad.shape[1]), "ctx", 0, 0)
        return lax.psum_scatter(grad, ("dp", "ctx"), scatter_dimension=0, tiled=True)[None]

    def product(left, right):
        left, right = chain.after(left, right)
        return chain.mark(tmm(left, right).astype(BF))

    def scatter(grad):
        axes = "ctx" if pair else ("dp", "ctx")
        return lax.psum_scatter(grad, axes, scatter_dimension=0, tiled=True)[None]

    token_rows = tokens.reshape(n_seqs * seq_dev, width)
    dy_rows = cotangent.reshape(n_seqs * seq_dev, width)
    xhats, _ = apply_norm(token_rows.astype(F32))
    normed = (xhats * scales[0:1]).astype(BF)
    cos_all, sin_all = jnp.tile(cos, (n_seqs, 1)), jnp.tile(sin, (n_seqs, 1))
    qkv = project(normed, full_attn, qc + 2 * kc, n_q + n_kv, cos_all, sin_all)
    kv = qkv[:, qc:]
    if swap:
        others = [lax.ppermute(kv, "ctx", flips[j]) for j in range(1, n_ctx)]
        pieces = [[(a, seq_dev, m, 0) for a in [kv] + others] for m in range(n_seqs)]
    else:
        every = lax.all_gather(kv.reshape(n_seqs, seq_dev, 2 * kc), "ctx", axis=1, tiled=True)
        every = every.reshape(n_seqs * seq, 2 * kc)
        pieces = [[(every, seq, m, 0)] for m in range(n_seqs)]

    def rows_of(value, m):
        return value[m * seq_dev : (m + 1) * seq_dev]

    st = [{}, {}]
    assert n_seqs == 2
    n_one, n_two, n_three, n_four = 4, 4, 4, 4
    inner = ((zi == 1) | (zi == n_t - 2)).astype(jnp.int32).reshape(1)
    attn_outs, normed_two, outputs, ffn_grads = [], [], [], []
    one_grads, attn_grads, input_grads = [], [], []
    gain_fin, gain_mid = [], []

    def post_attend(k):
        values = red.take(k)
        a, n = post(post_attend_body, inner, values, [], [token_rows], k, scales, [BF, BF])
        attn_outs.append(a), normed_two.append(n)
        chain.mark(n)

    def post_ffn(k):
        values, rows = red.take(k), [token_rows, dy_rows]
        out, grad, gain = post(
            post_ffn_body, inner, values, [attn_outs], rows, k, scales, [BF, BF], True
        )
        outputs.append(out), ffn_grads.append(grad), gain_fin.append(gain)
        chain.mark(grad)

    def post_mid(k):
        values, rows = red.take(k), [token_rows, dy_rows]
        one, grad, gain = post(
            post_mid_body, inner, values, [attn_outs], rows, k, scales, [F32, BF], True
        )
        one_grads.append(one), attn_grads.append(grad), gain_mid.append(gain)
        chain.mark(grad)

    def post_in(k):
        values = red.take(k)
        (grad,) = post(post_in_body, inner, values, [one_grads], [token_rows], k, scales, [BF])
        input_grads.append(grad)
        chain.mark(grad)

    def attention(m):
        s = st[m]
        (first, *rest) = chain.after(*[p[0] for p in pieces[m]])
        s["pieces"] = [(v,) + p[1:] for v, p in zip([first, *rest], pieces[m])]
        s["heads"], s["attended"], s["den"], *part = attend(
            qkv, m, s["pieces"], qpos, kpos, n_q, n_kv, full_attn, out_block, n_one // 2
        )
        chain.mark(part[0])
        red.load(part)

    red = Reduce(chain)
    attention(0)
    attention(1)
    red.run(n_one, post_attend, {})

    red = Reduce(chain)
    values = chain.after(*normed_two)
    gate, up, hidden, *part = ffn(list(values), full_ffn, ff, n_two)
    chain.mark(part[0])
    red.load(part)
    held = {}

    def hold(name, make):
        def run():
            held[name] = make()

        return run

    red.run(
        n_two,
        post_ffn,
        {
            0: hold("down_right", lambda: chain.mark(right_side([hidden]))),
            1: hold("mid_left", lambda: chain.mark(left_side(normed_two))),
            2: hold("left", lambda: chain.mark(left_side([normed]))),
        },
    )

    red = Reduce(chain)
    values = chain.after(*ffn_grads)
    d_both, *part = ffn_back(list(values), full_ffn, gate, up, ff, n_three)
    chain.mark(part[0])
    red.load(part)
    both_right = right_side([d_both])
    down_left = left_side(ffn_grads)

    def attention_back(m):
        s = st[m]
        size = n_three // 2
        grads = chain.after(*attn_grads[size * m : size * (m + 1)])
        s["q_back"], *s["terms"] = attend_back(
            qkv,
            m,
            s["pieces"],
            qpos,
            kpos,
            list(grads),
            s["heads"],
            s["den"],
            cos,
            sin,
            n_q,
            n_kv,
            full_attn,
            out_block,
        )
        chain.mark(s["q_back"])
        if swap:
            s["moved"] = [
                lax.ppermute(s["terms"][j].astype(BF), "ctx", flips[j]) for j in range(1, n_ctx)
            ]
        else:
            s["moved"] = [lax.psum_scatter(s["terms"][0], "ctx", scatter_dimension=0, tiled=True)]

    red.run(
        n_three,
        post_mid,
        {
            0: hold("g_down", lambda: scatter(product(down_left, held["down_right"]))),
            1: hold("g_gate_up", lambda: scatter(product(held["mid_left"], both_right))),
            3: lambda: attention_back(0),
        },
    )
    attention_back(1)

    def input_back(m):
        s = st[m]
        moved = list(chain.after(*s["moved"]))
        terms = [s["terms"][0]] + moved if swap else moved
        s["qkv_back"], s["gain"], *part = input_back_call(
            s["q_back"], terms, token_rows, m, cos, sin, full_attn, n_q, n_kv, n_four // 2
        )
        chain.mark(part[0])
        red.load(part)

    def tail():
        d_qkv = product(held["left"], held["right"])
        gain_cols = jnp.stack(
            [
                gain_in[0],
                sum(v[1] for v in gain_mid),
                sum(v[0] for v in gain_mid),
                sum(v[0] for v in gain_fin),
            ],
            axis=1,
        )
        if pair:
            keep = lax.dynamic_slice_in_dim(gain_cols, dpi * (width // 2), width // 2, 0)
            give = lax.dynamic_slice_in_dim(gain_cols, (1 - dpi) * (width // 2), width // 2, 0)
            gain_cols = keep + swap_core(give)
        gain_cols = jnp.pad(gain_cols, ((0, 0), (0, PAD - gain_cols.shape[1])))
        packed = chain.mark(pack(list(chain.after(d_qkv, d_out, gain_cols)), 2))
        held["g_tail"] = spread(packed)

    def finish_down():
        (value,) = chain.after(held["g_down"])
        (held["g_down"],) = sum_parts(value, ff // 3, [[(0, ff // 3)]])
        chain.mark(held["g_down"])

    def finish_both():
        (value,) = chain.after(held["g_gate_up"])
        group = 6 * FF_TILE
        starts = range(0, group, 2 * FF_TILE)
        cuts = [[(i + o, i + o + FF_TILE) for i in starts] for o in (0, FF_TILE)]
        held["g_gate"], held["g_up"] = sum_parts(value, group, cuts)
        chain.mark(held["g_up"])

    def finish_tail():
        (value,) = chain.after(held["g_tail"])
        ends = [0, qc, qc + kc, at_out, at_out + oc, at_out + oc + PAD]
        spans = [[span] for span in zip(ends[:-1], ends[1:])]
        *held["g_attn"], g_gains = sum_parts(value, ends[-1], spans)
        held["g_gains"] = mm_t(pick.astype(F32), g_gains)

    red = Reduce(chain)
    block_out = chain.mark(jnp.concatenate(chain.after(*outputs), axis=0))
    finish_down()
    input_back(0)
    d_out = product(left_side(attn_grads), right_side([s["attended"] for s in st]))
    input_back(1)
    held["right"] = right_side([s["qkv_back"] for s in st])
    gain_in = (st[0]["gain"] + st[1]["gain"])[:4]
    reach = 1
    while reach < n_t:
        steps = [(i, i ^ reach) for i in range(n_t)]
        gain_in = gain_in + lax.ppermute(gain_in, "tensor", steps)
        reach *= 2
    red.run(n_four, post_in, {2: tail, 4: finish_tail})
    finish_both()
    g_gains = held["g_gains"]
    return (
        block_out.reshape(tokens.shape),
        jnp.concatenate(input_grads, axis=0).reshape(tokens.shape),
        *held["g_attn"],
        held["g_gate"],
        held["g_up"],
        held["g_down"],
        g_gains[0],
        g_gains[1],
        g_gains[2],
        g_gains[3],
    )


def solution(mesh):
    act = P(None, "dp", "ctx", None)
    mat = P(("dp", "ctx"), "tensor")
    vec = P(("dp", "ctx"))
    return jax.shard_map(
        local,
        mesh=mesh,
        in_specs=(act, P()) + (mat,) * 7 + (vec,) * 4 + (act,),
        out_specs=(act, act) + (mat,) * 7 + (vec,) * 4,
        check_vma=False,
    )
```

time: 775 us -> 750 us (0.968)
  other arithmetic: 153 us -> 42.4 us
  Pallas kernels: 115 us -> 179 us
  waiting for transfers between devices: 273 us -> 321 us
  matrix products: 50.5 us -> 31.7 us
  local copies, waits for them, and re-layouts: 51.4 us -> 42.2 us
    pallas_call x8 -> x28, Pallas kernels: 107 us -> 172 us  [the longest x16 56.7 us: post(): call(body, tuple(out_shapes), (steps,), specs, tuple(out_specs), flops=20...]
    ppermute x16, waiting for transfers between devices: 62 us -> 114 us  [send(): self.first[k] = lax.ppermute(piece, 'tensor', [(0, 1), (3, 2)])]
    all_to_all x2 -> x1, waiting for transfers between devices: 31.9 us -> 4.27 us  [spread(): return lax.all_to_all(grad.reshape(n_ctx, -1, grad.shape[1]), 'ctx', 0, 0)]
    convert_element_type x15 -> x1, other arithmetic: 27.7 us -> 2.03 us  [local(): normed = (xhats * scales[0:1]).astype(BF)]
    concatenate x12 -> x9, other arithmetic: 35.1 us -> 11 us  [the longest x3 6.43 us: right_side(): return jnp.concatenate([value, swap_core(value)], axis=0) if pair else value]
    reduce_sum x15 -> x0, other arithmetic: 19.8 us -> none  [the longest x6 7.56 us: norm_backward(): jnp.mean(upstream * scaled, axis=-1, keepdims=True)]
    unnamed x195 -> x215, local copies, waits for them, and re-layouts: 14.6 us -> 30.9 us
    dot_general x8 -> x2, matrix products: 17.4 us -> 2.36 us  [mm_t(): lax.dot_general(a, b, (((1,), (1,)), ((), ())), preferred_element_type=F32)]
  transfers between devices with their start and end apart: 80 -> 73, of which waited for: 22 -> 36; matrix products, arithmetic and copies ran while one was open for 31% -> 10% of each run, Pallas kernels for 12% -> 14%
where the time goes in v2:
time: 750 us; the launch traced here: 739 us
  waiting for transfers between devices  321 us (43%)
  Pallas kernels  179 us (24%)
  starting transfers between devices  107 us (14%)
  other arithmetic  42.4 us (6%)
  local copies, waits for them, and re-layouts  42.2 us (6%)
  matrix products  31.7 us (4%)
  between operations  16.2 us (2%)
    ppermute x16, waiting for transfers between devices, send(): self.first[k] = lax.ppermute(piece, 'tensor', [(0, 1), (3, 2)])  114 us
    ppermute x16, waiting for transfers between devices, join(): self.third[k] = lax.ppermute(total, 'tensor', [(1, 0), (2, 3)])  87.8 us
    pallas_call x16, Pallas kernels, post(): call(body, tuple(out_shapes), (steps,), specs, tuple(out_specs), flops=20...  56.7 us
    ppermute x16, starting transfers between devices, send(): self.first[k] = lax.ppermute(piece, 'tensor', [(0, 1), (3, 2)])  50.9 us
    ppermute x3, waiting for transfers between devices, local(): others = [lax.ppermute(kv, 'ctx', flips[j]) for j in range(1, n_ctx)]  43.9 us
    all_gather x1, waiting for transfers between devices, local(): full_attn = lax.all_gather(pack_attn, ('dp', 'ctx'), axis=0, tiled=True)  42 us
    pallas_call x1, Pallas kernels, ffn_back(): call(functools.partial(ffn_back_body, len(ys), n_out), (shape((rows, 2 *...  37.1 us
    unnamed x215, local copies, waits for them, and re-layouts  30.9 us
  transfers between devices with their start and end apart: 73, of which 36 were waited for; matrix products, arithmetic and copies ran while one was open for 10% of the time, Pallas kernels for 14%

profile of v2, /device:TPU:0, one launch (start us, length us, event | category | flops | bytes accessed | tf_op | source)
XLA Modules:
  0.0 739.5 jit_solution(2228267572249309244)
XLA Ops:
  21.3 4.5 compare_select_fusion.1
  27.2 42.0 %all-gather.3.cloned.1.call-done.w_ref.refs_3_.refs_7_.refs_4_ = bf16[2304,1664]{1,0:T(8,128)(2,1)} async-done(((bf16[288,1664]{1,0:T(8,128)(2,1)}), bf16[2304,1664]{1,0:T(8,128)(2,1)}) %all-gather.3.cloned.1.call-update) | async-done | bytes 7667728 | tf_op jit(solution)/shard_map/all_gather | solution.py:644
  74.0 7.0 shard_map.237.refs_0_
  87.1 21.8 %collective-permute-done.2.refs_7_.refs_11_ = bf16[512,512]{1,0:T(8,128)(2,1)S(1)} collective-permute-done((bf16[512,512]{1,0:T(8,128)(2,1)S(1)}, bf16[512,512]{1,0:T(8,128)(2,1)S(1)}, u32[]{:S(2)}, u32[]{:S(2)}) %collective-permute-start.2) | collective-permute-done | bytes 524320 | tf_op jit(solution)/shard_map/ppermute | solution.py:692
  108.9 11.2 %collective-permute-done.1.refs_6_.refs_10_ = bf16[512,512]{1,0:T(8,128)(2,1)S(1)} collective-permute-done((bf16[512,512]{1,0:T(8,128)(2,1)S(1)}, bf16[512,512]{1,0:T(8,128)(2,1)S(1)}, u32[]{:S(2)}, u32[]{:S(2)}) %collective-permute-start.1) | collective-permute-done | bytes 524320 | tf_op jit(solution)/shard_map/ppermute | solution.py:692
  120.1 10.9 %collective-permute-done.refs_5_.refs_9_ = bf16[512,512]{1,0:T(8,128)(2,1)S(1)} collective-permute-done((bf16[512,512]{1,0:T(8,128)(2,1)S(1)}, bf16[512,512]{1,0:T(8,128)(2,1)S(1)}, u32[]{:S(2)}, u32[]{:S(2)}) %collective-permute-start) | collective-permute-done | bytes 524320 | tf_op jit(solution)/shard_map/ppermute | solution.py:692
  131.8 4.8 shard_map.238
  141.5 4.8 shard_map.239
  149.2 4.9 collective-permute-done.3
  155.0 11.6 %collective-permute-done.5 = bf16[128,2304]{1,0:T(8,128)(2,1)S(1)} collective-permute-done((bf16[128,2304]{1,0:T(8,128)(2,1)}, bf16[128,2304]{1,0:T(8,128)(2,1)S(1)}, u32[]{:S(2)}, u32[]{:S(2)}) %collective-permute-start.5) | collective-permute-done | bytes 589856 | tf_op jit(solution)/shard_map/ppermute | solution.py:558
  169.0 21.3 %collective-permute-done.8 = bf16[128,2304]{1,0:T(8,128)(2,1)S(1)} collective-permute-done((bf16[128,2304]{1,0:T(8,128)(2,1)}, bf16[128,2304]{1,0:T(8,128)(2,1)S(1)}, u32[]{:S(2)}, u32[]{:S(2)}) %collective-permute-start.8) | collective-permute-done | bytes 589856 | tf_op jit(solution)/shard_map/ppermute | solution.py:558
  198.7 11.8 %collective-permute-done.9.third_ref = bf16[128,2304]{1,0:T(8,128)(2,1)S(1)} collective-permute-done((bf16[128,2304]{1,0:T(8,128)(2,1)S(1)}, bf16[128,2304]{1,0:T(8,128)(2,1)S(1)}, u32[]{:S(2)}, u32[]{:S(2)}) %collective-permute-start.9) | collective-permute-done | bytes 589856 | tf_op jit(solution)/shard_map/ppermute | solution.py:574
  215.8 7.4 collective-permute-done.12.third_ref
  226.8 8.1 %collective-permute-done.14.third_ref = bf16[128,2304]{1,0:T(8,128)(2,1)S(1)} collective-permute-done((bf16[128,2304]{1,0:T(8,128)(2,1)S(1)}, bf16[128,2304]{1,0:T(8,128)(2,1)S(1)}, u32[]{:S(2)}, u32[]{:S(2)}) %collective-permute-start.14) | collective-permute-done | bytes 589856 | tf_op jit(solution)/shard_map/ppermute | solution.py:574
  238.4 8.6 %all-gather.5.cloned.1.call-done.refs_4_.refs_5_.refs_6_ = bf16[2304,6912]{1,0:T(8,128)(2,1)} async-done(((bf16[288,6912]{1,0:T(8,128)(2,1)}), bf16[2304,6912]{1,0:T(8,128)(2,1)}) %all-gather.5.cloned.1.call-update) | async-done | bytes 31850512 | tf_op jit(solution)/shard_map/all_gather | solution.py:645
  247.0 25.3 %shard_map.244 = (bf16[512,2304]{1,0:T(8,128)(2,1)}, bf16[512,2304]{1,0:T(8,128)(2,1)}, bf16[512,2304]{1,0:T(8,128)(2,1)}, bf16[128,2304]{1,0:T(8,128)(2,1)}, bf...) custom-call(bf16[128,2304]{1,0:T(8,128)(2,1)} %get-tuple-element.298.refs_0_, ...), custom_call_target="tpu_custom_call" | custom-call | flops 16307453952 | bytes 43646976 | tf_op jit(solution)/shard_map/pallas_call | solution.py:425
  275.8 13.3 %collective-permute-done.15 = bf16[128,2304]{1,0:T(8,128)(2,1)S(1)} collective-permute-done((bf16[128,2304]{1,0:T(8,128)(2,1)}, bf16[128,2304]{1,0:T(8,128)(2,1)S(1)}, u32[]{:S(2)}, u32[]{:S(2)}) %collective-permute-start.15) | collective-permute-done | bytes 589856 | tf_op jit(solution)/shard_map/ppermute | solution.py:558
  290.3 4.3 collective-permute-start.17
  297.4 10.7 %collective-permute-done.17 = bf16[128,2304]{1,0:T(8,128)(2,1)S(1)} collective-permute-done((bf16[128,2304]{1,0:T(8,128)(2,1)}, bf16[128,2304]{1,0:T(8,128)(2,1)S(1)}, u32[]{:S(2)}, u32[]{:S(2)}) %collective-permute-start.17) | collective-permute-done | bytes 589856 | tf_op jit(solution)/shard_map/ppermute | solution.py:558
  310.9 5.2 collective-permute-start.21
  319.7 8.9 %collective-permute-done.21 = bf16[128,2304]{1,0:T(8,128)(2,1)S(1)} collective-permute-done((bf16[128,2304]{1,0:T(8,128)(2,1)S(1)}, bf16[128,2304]{1,0:T(8,128)(2,1)S(1)}, u32[]{:S(2)}, u32[]{:S(2)}) %collective-permute-start.21) | collective-permute-done | bytes 589856 | tf_op jit(solution)/shard_map/ppermute | solution.py:558
  338.9 5.8 collective-permute-start.25
  348.4 8.9 %collective-permute-done.25 = bf16[128,2304]{1,0:T(8,128)(2,1)S(1)} collective-permute-done((bf16[128,2304]{1,0:T(8,128)(2,1)S(1)}, bf16[128,2304]{1,0:T(8,128)(2,1)S(1)}, u32[]{:S(2)}, u32[]{:S(2)}) %collective-permute-start.25) | collective-permute-done | bytes 589856 | tf_op jit(solution)/shard_map/ppermute | solution.py:558
  368.1 10.4 %collective-permute-done.27.third_ref = bf16[128,2304]{1,0:T(8,128)(2,1)S(1)} collective-permute-done((bf16[128,2304]{1,0:T(8,128)(2,1)S(1)}, bf16[128,2304]{1,0:T(8,128)(2,1)S(1)}, u32[]{:S(2)}, u32[]{:S(2)}) %collective-permute-start.27) | collective-permute-done | bytes 589856 | tf_op jit(solution)/shard_map/ppermute | solution.py:574
  383.3 7.8 %collective-permute-done.29.third_ref = bf16[128,2304]{1,0:T(8,128)(2,1)S(1)} collective-permute-done((bf16[128,2304]{1,0:T(8,128)(2,1)S(1)}, bf16[128,2304]{1,0:T(8,128)(2,1)S(1)}, u32[]{:S(2)}, u32[]{:S(2)}) %collective-permute-start.29) | collective-permute-done | bytes 589856 | tf_op jit(solution)/shard_map/ppermute | solution.py:574
  395.9 37.1 %shard_map.249 = (bf16[512,4608]{1,0:T(8,128)(2,1)}, bf16[128,2304]{1,0:T(8,128)(2,1)}, bf16[128,2304]{1,0:T(8,128)(2,1)}, bf16[128,2304]{1,0:T(8,128)(2,1)}, bf16[128,2304]{1,0:T(8,128)(2,1)}) custom-call(bf16[128,2304]{1,0:T(8,128)(2,1)} %get-tuple-element.349.refs_0_, bf16[128,2304]{1,0:T(8,128)(2,1)} %get-tuple-element.350.refs_1_, ...), custom_call_target="tpu_custom_call" | custom-call | flops 16307453952 | bytes 46006272 | tf_op jit(solution)/shard_map/pallas_call | solution.py:477
  435.3 10.3 %collective-permute-done.32 = bf16[128,2304]{1,0:T(8,128)(2,1)S(1)} collective-permute-done((bf16[128,2304]{1,0:T(8,128)(2,1)}, bf16[128,2304]{1,0:T(8,128)(2,1)S(1)}, u32[]{:S(2)}, u32[]{:S(2)}) %collective-permute-start.32) | collective-permute-done | bytes 589856 | tf_op jit(solution)/shard_map/ppermute | solution.py:558
  446.0 7.5 %convolution_convert_fusion.1 = bf16[1152,2304]{1,0:T(8,128)(2,1)} fusion(bf16[1024,1152]{1,0:T(8,128)(2,1)S(1)} %pad_maximum_fusion.4, bf16[1024,2304]{1,0:T(8,128)(2,1)S(1)} %bitcast.81), kind=kOutput, calls=%fused_computation.1 | convolution fusion | flops 5438472192 | bytes 12386304 | tf_op jit(solution)/shard_map/dot_general | solution.py:47
  454.6 4.3 collective-permute-start.34
  459.8 11.4 %collective-permute-done.34 = bf16[128,2304]{1,0:T(8,128)(2,1)S(1)} collective-permute-done((bf16[128,2304]{1,0:T(8,128)(2,1)S(1)}, bf16[128,2304]{1,0:T(8,128)(2,1)S(1)}, u32[]{:S(2)}, u32[]{:S(2)}) %collective-permute-start.34) | collective-permute-done | bytes 589856 | tf_op jit(solution)/shard_map/ppermute | solution.py:558
  475.2 13.7 %convolution_convert_fusion = bf16[1152,4608]{1,0:T(8,128)(2,1)} fusion(bf16[1024,1152]{1,0:T(8,128)(2,1)S(1)} %copy-done.25, bf16[1024,4608]{1,0:T(8,128)(2,1)S(1)} %pad_maximum_fusion), kind=kOutput, calls=%fused_computation | convolution fusion | flops 10876944384 | bytes 22413312 | tf_op jit(solution)/shard_map/dot_general | solution.py:47
  490.0 5.9 collective-permute-start.30
  499.2 10.3 %collective-permute-done.30 = bf16[128,2304]{1,0:T(8,128)(2,1)S(1)} collective-permute-done((bf16[128,2304]{1,0:T(8,128)(2,1)S(1)}, bf16[128,2304]{1,0:T(8,128)(2,1)S(1)}, u32[]{:S(2)}, u32[]{:S(2)}) %collective-permute-start.30) | collective-permute-done | bytes 589856 | tf_op jit(solution)/shard_map/ppermute | solution.py:558
  513.8 4.3 shard_map.250
  526.2 4.3 shard_map.251
  530.5 8.1 %shard_map.252 = (bf16[256,512]{1,0:T(8,128)(2,1)}, f32[256,512]{1,0:T(8,128)}, f32[256,512]{1,0:T(8,128)}, f32[256,512]{1,0:T(8,128)}, f32[256,512]{1,0:T(8,128)}) custom-call(bf16[512,1024]{1,0:T(8,128)(2,1)} %shard_map.237.refs_0_, s32[256,1]{1,0:T(8,128)} %copy.44.refs_1_, s32[1,1024]{1,0:T(1,128)} %bitcast.86, f32[256,512]{1,0:T(8,128)} %get-tuple-element.373.refs_3_, ...), custom_call_target="tpu_custom_call" | custom-call | flops 1946157056 | bytes 9961472 | tf_op jit(solution)/shard_map/pallas_call | solution.py:240
  549.9 4.4 collective-permute-done.43.third_ref
  559.4 8.2 %shard_map.255 = (bf16[256,512]{1,0:T(8,128)(2,1)}, f32[256,512]{1,0:T(8,128)}, f32[256,512]{1,0:T(8,128)}, f32[256,512]{1,0:T(8,128)}, f32[256,512]{1,0:T(8,128)}) custom-call(bf16[512,1024]{1,0:T(8,128)(2,1)} %shard_map.237.refs_0_, s32[256,1]{1,0:T(8,128)} %copy.44.refs_1_, s32[1,1024]{1,0:T(1,128)} %bitcast.87, f32[256,512]{1,0:T(8,128)} %get-tuple-element.333.refs_3_, ...), custom_call_target="tpu_custom_call" | custom-call | flops 1946157056 | bytes 9961472 | tf_op jit(solution)/shard_map/pallas_call | solution.py:240
  575.3 6.1 shard_map.257
  600.0 5.0 collective-permute-done.49.refs_7_
  607.1 6.0 shard_map.258
  620.7 9.5 %collective-permute-done.62 = f32[4,2304]{1,0:T(4,128)S(1)} collective-permute-done((f32[4,2304]{1,0:T(4,128)S(1)}, f32[4,2304]{1,0:T(4,128)S(1)}, u32[]{:S(2)}, u32[]{:S(2)}) %collective-permute-start.62) | collective-permute-done | bytes 36896 | tf_op jit(solution)/shard_map/ppermute | solution.py:883
  653.0 9.8 %collective-permute-done.55.third_ref = bf16[128,2304]{1,0:T(8,128)(2,1)S(1)} collective-permute-done((bf16[128,2304]{1,0:T(8,128)(2,1)S(1)}, bf16[128,2304]{1,0:T(8,128)(2,1)S(1)}, u32[]{:S(2)}, u32[]{:S(2)}) %collective-permute-start.55) | collective-permute-done | bytes 589856 | tf_op jit(solution)/shard_map/ppermute | solution.py:574
  666.8 5.6 convolution_convert_fusion.2.refs_0_
  675.9 4.8 all-to-all-start
  689.9 12.1 %collective-permute-done.65.third_ref = bf16[128,2304]{1,0:T(8,128)(2,1)S(1)} collective-permute-done((bf16[128,2304]{1,0:T(8,128)(2,1)S(1)}, bf16[128,2304]{1,0:T(8,128)(2,1)S(1)}, u32[]{:S(2)}, u32[]{:S(2)}) %collective-permute-start.65) | collective-permute-done | bytes 589856 | tf_op jit(solution)/shard_map/ppermute | solution.py:574
  705.9 6.2 collective-permute-done.67.third_ref
  728.1 4.5 shard_map.265
  (447 shorter events, 242.4 us)
Async XLA Ops:
  7.2 62.0 %all-gather.3.cloned.1.call-start = ((), (), s32[]{:S(2)}) async-start(), calls=%async_computation.3 | async-start | bytes 8626176 | tf_op jit(solution)/shard_map/all_gather | solution.py:644
  15.1 232.0 %all-gather.5.cloned.1.call-start = ((), (), s32[]{:S(2)}) async-start(), calls=%async_computation.4 | async-start | bytes 35831808 | tf_op jit(solution)/shard_map/all_gather | solution.py:645
  18.5 552.6 %reduce-scatter.3.cloned.1.call-start = ((), (), s32[]{:S(2)}) async-start(), calls=%async_computation.5 | async-start | bytes 6635520 | tf_op jit(solution)/shard_map/reduce_scatter | solution.py:682
  82.2 26.7 %collective-permute-start.2 = (bf16[512,512]{1,0:T(8,128)(2,1)S(1)}, bf16[512,512]{1,0:T(8,128)(2,1)S(1)}, u32[]{:S(2)}, u32[]{:S(2)}) collective-permute-start(bf16[512,512]{1,0:T(8,128)(2,1)S(1)} %slice.95.refs_4_.refs_8_), channel_id=1, source_target_pairs={{0,12},{4,8},{8,4},{12,0},{1,13},{5,9},{9,5},{13,1},{2,14},{6,10},... | collective-permute-start | bytes 1572872 | tf_op jit(solution)/shard_map/ppermute | solution.py:692
  83.8 36.4 %collective-permute-start.1 = (bf16[512,512]{1,0:T(8,128)(2,1)S(1)}, bf16[512,512]{1,0:T(8,128)(2,1)S(1)}, u32[]{:S(2)}, u32[]{:S(2)}) collective-permute-start(bf16[512,512]{1,0:T(8,128)(2,1)S(1)} %slice.95.refs_4_.refs_8_), channel_id=1, source_target_pairs={{0,8},{4,12},{8,0},{12,4},{1,9},{5,13},{9,1},{13,5},{2,10},{6,14},... | collective-permute-start | bytes 1572872 | tf_op jit(solution)/shard_map/ppermute | solution.py:692
  85.2 45.8 %collective-permute-start = (bf16[512,512]{1,0:T(8,128)(2,1)S(1)}, bf16[512,512]{1,0:T(8,128)(2,1)S(1)}, u32[]{:S(2)}, u32[]{:S(2)}) collective-permute-start(bf16[512,512]{1,0:T(8,128)(2,1)S(1)} %slice.95.refs_4_.refs_8_), channel_id=1, source_target_pairs={{0,4},{4,0},{8,12},{12,8},{1,5},{5,1},{9,13},{13,9},{2,6},{6,2},{1... | collective-permute-start | bytes 1572872 | tf_op jit(solution)/shard_map/ppermute | solution.py:692
  136.6 17.4 %collective-permute-start.3 = (bf16[128,2304]{1,0:T(8,128)(2,1)}, bf16[128,2304]{1,0:T(8,128)(2,1)S(1)}, u32[]{:S(2)}, u32[]{:S(2)}) collective-permute-start(bf16[128,2304]{1,0:T(8,128)(2,1)} %get-tuple-element.253), channel_id=1, source_target_pairs={{0,1},{3,2},{4,5},{7,6},{8,9},{11,10},{12,13},{15,14},{16,17},{19,... | collective-permute-start | bytes 1769480 | tf_op jit(solution)/shard_map/ppermute | solution.py:558
  140.1 26.6 %collective-permute-start.5 = (bf16[128,2304]{1,0:T(8,128)(2,1)}, bf16[128,2304]{1,0:T(8,128)(2,1)S(1)}, u32[]{:S(2)}, u32[]{:S(2)}) collective-permute-start(bf16[128,2304]{1,0:T(8,128)(2,1)} %get-tuple-element.256), channel_id=1, source_target_pairs={{0,1},{3,2},{4,5},{7,6},{8,9},{11,10},{12,13},{15,14},{16,17},{19,... | collective-permute-start | bytes 1769480 | tf_op jit(solution)/shard_map/ppermute | solution.py:558
  146.4 50.0 %collective-permute-start.11 = (bf16[128,2304]{1,0:T(8,128)(2,1)}, bf16[128,2304]{1,0:T(8,128)(2,1)S(1)}, u32[]{:S(2)}, u32[]{:S(2)}) collective-permute-start(bf16[128,2304]{1,0:T(8,128)(2,1)} %get-tuple-element.268), channel_id=1, source_target_pairs={{0,1},{3,2},{4,5},{7,6},{8,9},{11,10},{12,13},{15,14},{16,17},{19,... | collective-permute-start | bytes 1769480 | tf_op jit(solution)/shard_map/ppermute | solution.py:558
  147.8 42.4 %collective-permute-start.8 = (bf16[128,2304]{1,0:T(8,128)(2,1)}, bf16[128,2304]{1,0:T(8,128)(2,1)S(1)}, u32[]{:S(2)}, u32[]{:S(2)}) collective-permute-start(bf16[128,2304]{1,0:T(8,128)(2,1)} %get-tuple-element.260), channel_id=1, source_target_pairs={{0,1},{3,2},{4,5},{7,6},{8,9},{11,10},{12,13},{15,14},{16,17},{19,... | collective-permute-start | bytes 1769480 | tf_op jit(solution)/shard_map/ppermute | solution.py:558
  166.8 24.3 %collective-permute-start.7 = (bf16[128,2304]{1,0:T(8,128)(2,1)S(1)}, bf16[128,2304]{1,0:T(8,128)(2,1)S(1)}, u32[]{:S(2)}, u32[]{:S(2)}) collective-permute-start(bf16[128,2304]{1,0:T(8,128)(2,1)S(1)} %reduce-precision_convert_fusion.30), channel_id=1, source_target_pairs={{1,2},{2,1},{5,6},{6,5},{9,10},{10,9},{13,14},{14,13},{17,18},{18,... | collective-permute-start | bytes 1769480 | tf_op jit(solution)/shard_map/ppermute | solution.py:567
  167.7 25.0 %collective-permute-start.6 = (bf16[128,2304]{1,0:T(8,128)(2,1)S(1)}, bf16[128,2304]{1,0:T(8,128)(2,1)S(1)}, u32[]{:S(2)}, u32[]{:S(2)}) collective-permute-start(bf16[128,2304]{1,0:T(8,128)(2,1)S(1)} %reduce-precision_convert_fusion.29.total_ref), channel_id=1, source_target_pairs={{1,0},{2,3},{5,4},{6,7},{9,8},{10,11},{13,12},{14,15},{17,16},{18,... | collective-permute-start | bytes 1769480 | tf_op jit(solution)/shard_map/ppermute | solution.py:574
  191.3 19.3 %collective-permute-start.9 = (bf16[128,2304]{1,0:T(8,128)(2,1)S(1)}, bf16[128,2304]{1,0:T(8,128)(2,1)S(1)}, u32[]{:S(2)}, u32[]{:S(2)}) collective-permute-start(bf16[128,2304]{1,0:T(8,128)(2,1)S(1)} %reduce-precision_convert_fusion.27.total_ref), channel_id=1, source_target_pairs={{1,0},{2,3},{5,4},{6,7},{9,8},{10,11},{13,12},{14,15},{17,16},{18,... | collective-permute-start | bytes 1769480 | tf_op jit(solution)/shard_map/ppermute | solution.py:574
  196.6 17.6 %collective-permute-start.13 = (bf16[128,2304]{1,0:T(8,128)(2,1)S(1)}, bf16[128,2304]{1,0:T(8,128)(2,1)S(1)}, u32[]{:S(2)}, u32[]{:S(2)}) collective-permute-start(bf16[128,2304]{1,0:T(8,128)(2,1)S(1)} %reduce-precision_convert_fusion.26), channel_id=1, source_target_pairs={{1,2},{2,1},{5,6},{6,5},{9,10},{10,9},{13,14},{14,13},{17,18},{18,... | collective-permute-start | bytes 1769480 | tf_op jit(solution)/shard_map/ppermute | solution.py:567
  197.4 25.8 %collective-permute-start.12 = (bf16[128,2304]{1,0:T(8,128)(2,1)S(1)}, bf16[128,2304]{1,0:T(8,128)(2,1)S(1)}, u32[]{:S(2)}, u32[]{:S(2)}) collective-permute-start(bf16[128,2304]{1,0:T(8,128)(2,1)S(1)} %reduce-precision_convert_fusion.25.total_ref), channel_id=1, source_target_pairs={{1,0},{2,3},{5,4},{6,7},{9,8},{10,11},{13,12},{14,15},{17,16},{18,... | collective-permute-start | bytes 1769480 | tf_op jit(solution)/shard_map/ppermute | solution.py:574
  214.3 20.5 %collective-permute-start.14 = (bf16[128,2304]{1,0:T(8,128)(2,1)S(1)}, bf16[128,2304]{1,0:T(8,128)(2,1)S(1)}, u32[]{:S(2)}, u32[]{:S(2)}) collective-permute-start(bf16[128,2304]{1,0:T(8,128)(2,1)S(1)} %reduce-precision_convert_fusion.24.total_ref), channel_id=1, source_target_pairs={{1,0},{2,3},{5,4},{6,7},{9,8},{10,11},{13,12},{14,15},{17,16},{18,... | collective-permute-start | bytes 1769480 | tf_op jit(solution)/shard_map/ppermute | solution.py:574
  272.3 16.7 %collective-permute-start.15 = (bf16[128,2304]{1,0:T(8,128)(2,1)}, bf16[128,2304]{1,0:T(8,128)(2,1)S(1)}, u32[]{:S(2)}, u32[]{:S(2)}) collective-permute-start(bf16[128,2304]{1,0:T(8,128)(2,1)} %get-tuple-element.288), channel_id=1, source_target_pairs={{0,1},{3,2},{4,5},{7,6},{8,9},{11,10},{12,13},{15,14},{16,17},{19,... | collective-permute-start | bytes 1769480 | tf_op jit(solution)/shard_map/ppermute | solution.py:558
  290.3 17.8 %collective-permute-start.17 = (bf16[128,2304]{1,0:T(8,128)(2,1)}, bf16[128,2304]{1,0:T(8,128)(2,1)S(1)}, u32[]{:S(2)}, u32[]{:S(2)}) collective-permute-start(bf16[128,2304]{1,0:T(8,128)(2,1)} %get-tuple-element.293), channel_id=1, source_target_pairs={{0,1},{3,2},{4,5},{7,6},{8,9},{11,10},{12,13},{15,14},{16,17},{19,... | collective-permute-start | bytes 1769480 | tf_op jit(solution)/shard_map/ppermute | solution.py:558
  310.9 17.7 %collective-permute-start.21 = (bf16[128,2304]{1,0:T(8,128)(2,1)S(1)}, bf16[128,2304]{1,0:T(8,128)(2,1)S(1)}, u32[]{:S(2)}, u32[]{:S(2)}) collective-permute-start(bf16[128,2304]{1,0:T(8,128)(2,1)S(1)} %copy-done.54), channel_id=1, source_target_pairs={{0,1},{3,2},{4,5},{7,6},{8,9},{11,10},{12,13},{15,14},{16,17},{19,... | collective-permute-start | bytes 1769480 | tf_op jit(solution)/shard_map/ppermute | solution.py:558
  316.1 16.7 %collective-permute-start.19 = (bf16[128,2304]{1,0:T(8,128)(2,1)S(1)}, bf16[128,2304]{1,0:T(8,128)(2,1)S(1)}, u32[]{:S(2)}, u32[]{:S(2)}) collective-permute-start(bf16[128,2304]{1,0:T(8,128)(2,1)S(1)} %reduce-precision_convert_fusion.21.total_ref), channel_id=1, source_target_pairs={{1,0},{2,3},{5,4},{6,7},{9,8},{10,11},{13,12},{14,15},{17,16},{18,... | collective-permute-start | bytes 1769480 | tf_op jit(solution)/shard_map/ppermute | solution.py:574
  338.9 18.4 %collective-permute-start.25 = (bf16[128,2304]{1,0:T(8,128)(2,1)S(1)}, bf16[128,2304]{1,0:T(8,128)(2,1)S(1)}, u32[]{:S(2)}, u32[]{:S(2)}) collective-permute-start(bf16[128,2304]{1,0:T(8,128)(2,1)S(1)} %copy-done.50), channel_id=1, source_target_pairs={{0,1},{3,2},{4,5},{7,6},{8,9},{11,10},{12,13},{15,14},{16,17},{19,... | collective-permute-start | bytes 1769480 | tf_op jit(solution)/shard_map/ppermute | solution.py:558
  344.8 16.7 %collective-permute-start.23 = (bf16[128,2304]{1,0:T(8,128)(2,1)S(1)}, bf16[128,2304]{1,0:T(8,128)(2,1)S(1)}, u32[]{:S(2)}, u32[]{:S(2)}) collective-permute-start(bf16[128,2304]{1,0:T(8,128)(2,1)S(1)} %reduce-precision_convert_fusion.19.total_ref), channel_id=1, source_target_pairs={{1,0},{2,3},{5,4},{6,7},{9,8},{10,11},{13,12},{14,15},{17,16},{18,... | collective-permute-start | bytes 1769480 | tf_op jit(solution)/shard_map/ppermute | solution.py:574
  358.3 20.2 %collective-permute-start.27 = (bf16[128,2304]{1,0:T(8,128)(2,1)S(1)}, bf16[128,2304]{1,0:T(8,128)(2,1)S(1)}, u32[]{:S(2)}, u32[]{:S(2)}) collective-permute-start(bf16[128,2304]{1,0:T(8,128)(2,1)S(1)} %reduce-precision_convert_fusion.17.total_ref), channel_id=1, source_target_pairs={{1,0},{2,3},{5,4},{6,7},{9,8},{10,11},{13,12},{14,15},{17,16},{18,... | collective-permute-start | bytes 1769480 | tf_op jit(solution)/shard_map/ppermute | solution.py:574
  366.4 24.7 %collective-permute-start.29 = (bf16[128,2304]{1,0:T(8,128)(2,1)S(1)}, bf16[128,2304]{1,0:T(8,128)(2,1)S(1)}, u32[]{:S(2)}, u32[]{:S(2)}) collective-permute-start(bf16[128,2304]{1,0:T(8,128)(2,1)S(1)} %reduce-precision_convert_fusion.16.total_ref), channel_id=1, source_target_pairs={{1,0},{2,3},{5,4},{6,7},{9,8},{10,11},{13,12},{14,15},{17,16},{18,... | collective-permute-start | bytes 1769480 | tf_op jit(solution)/shard_map/ppermute | solution.py:574
  453.6 274.5 %reduce-scatter.5.cloned.1.call-start = ((), (), s32[]{:S(2)}) async-start(), calls=%async_computation.6 | async-start | bytes 13271040 | tf_op jit(solution)/shard_map/reduce_scatter | solution.py:682
  453.6 17.9 %collective-permute-start.31 = (bf16[512,4608]{1,0:T(8,128)(2,1)}, bf16[512,4608]{1,0:T(8,128)(2,1)S(1)}, u32[]{:S(2)}, u32[]{:S(2)}) collective-permute-start(bf16[512,4608]{1,0:T(8,128)(2,1)} %get-tuple-element.345), channel_id=1, source_target_pairs={{0,16},{16,0},{1,17},{17,1},{2,18},{18,2},{3,19},{19,3},{4,20},{20... | collective-permute-start | bytes 14155784 | tf_op jit(solution)/shard_map/ppermute | solution.py:659
  454.6 16.6 %collective-permute-start.34 = (bf16[128,2304]{1,0:T(8,128)(2,1)S(1)}, bf16[128,2304]{1,0:T(8,128)(2,1)S(1)}, u32[]{:S(2)}, u32[]{:S(2)}) collective-permute-start(bf16[128,2304]{1,0:T(8,128)(2,1)S(1)} %copy-done.58), channel_id=1, source_target_pairs={{0,1},{3,2},{4,5},{7,6},{8,9},{11,10},{12,13},{15,14},{16,17},{19,... | collective-permute-start | bytes 1769480 | tf_op jit(solution)/shard_map/ppermute | solution.py:558
  490.0 19.5 %collective-permute-start.30 = (bf16[128,2304]{1,0:T(8,128)(2,1)S(1)}, bf16[128,2304]{1,0:T(8,128)(2,1)S(1)}, u32[]{:S(2)}, u32[]{:S(2)}) collective-permute-start(bf16[128,2304]{1,0:T(8,128)(2,1)S(1)} %copy-done.55), channel_id=1, source_target_pairs={{0,1},{3,2},{4,5},{7,6},{8,9},{11,10},{12,13},{15,14},{16,17},{19,... | collective-permute-start | bytes 1769480 | tf_op jit(solution)/shard_map/ppermute | solution.py:558
  495.9 24.0 %collective-permute-start.37 = (bf16[128,2304]{1,0:T(8,128)(2,1)S(1)}, bf16[128,2304]{1,0:T(8,128)(2,1)S(1)}, u32[]{:S(2)}, u32[]{:S(2)}) collective-permute-start(bf16[128,2304]{1,0:T(8,128)(2,1)S(1)} %copy-done.52), channel_id=1, source_target_pairs={{0,1},{3,2},{4,5},{7,6},{8,9},{11,10},{12,13},{15,14},{16,17},{19,... | collective-permute-start | bytes 1769480 | tf_op jit(solution)/shard_map/ppermute | solution.py:558
  497.9 15.9 %collective-permute-start.38 = (bf16[128,2304]{1,0:T(8,128)(2,1)S(1)}, bf16[128,2304]{1,0:T(8,128)(2,1)}, u32[]{:S(2)}, u32[]{:S(2)}) collective-permute-start(bf16[128,2304]{1,0:T(8,128)(2,1)S(1)} %reduce-precision_convert_fusion.13.total_ref), channel_id=1, source_target_pairs={{1,0},{2,3},{5,4},{6,7},{9,8},{10,11},{13,12},{14,15},{17,16},{18,... | collective-permute-start | bytes 1769480 | tf_op jit(solution)/shard_map/ppermute | solution.py:574
  520.0 18.6 %collective-permute-start.41 = (bf16[128,2304]{1,0:T(8,128)(2,1)S(1)}, bf16[128,2304]{1,0:T(8,128)(2,1)S(1)}, u32[]{:S(2)}, u32[]{:S(2)}) collective-permute-start(bf16[128,2304]{1,0:T(8,128)(2,1)S(1)} %reduce-precision_convert_fusion.10), channel_id=1, source_target_pairs={{1,2},{2,1},{5,6},{6,5},{9,10},{10,9},{13,14},{14,13},{17,18},{18,... | collective-permute-start | bytes 1769480 | tf_op jit(solution)/shard_map/ppermute | solution.py:567
  522.0 22.9 %collective-permute-start.40 = (bf16[128,2304]{1,0:T(8,128)(2,1)S(1)}, bf16[128,2304]{1,0:T(8,128)(2,1)S(1)}, u32[]{:S(2)}, u32[]{:S(2)}) collective-permute-start(bf16[128,2304]{1,0:T(8,128)(2,1)S(1)} %reduce-precision_convert_fusion.9.total_ref), channel_id=1, source_target_pairs={{1,0},{2,3},{5,4},{6,7},{9,8},{10,11},{13,12},{14,15},{17,16},{18,... | collective-permute-start | bytes 1769480 | tf_op jit(solution)/shard_map/ppermute | solution.py:574
  541.3 33.1 %collective-permute-start.46 = (bf16[256,512]{1,0:T(8,128)(2,1)S(1)}, bf16[256,512]{1,0:T(8,128)(2,1)S(1)}, u32[]{:S(2)}, u32[]{:S(2)}) collective-permute-start(bf16[256,512]{1,0:T(8,128)(2,1)S(1)} %convert_element_type.421), channel_id=1, source_target_pairs={{0,12},{4,8},{8,4},{12,0},{1,13},{5,9},{9,5},{13,1},{2,14},{6,10},... | collective-permute-start | bytes 786440 | tf_op jit(solution)/shard_map/ppermute | solution.py:807
  543.1 31.3 %collective-permute-start.45 = (bf16[256,512]{1,0:T(8,128)(2,1)}, bf16[256,512]{1,0:T(8,128)(2,1)S(1)}, u32[]{:S(2)}, u32[]{:S(2)}) collective-permute-start(bf16[256,512]{1,0:T(8,128)(2,1)} %convert_element_type.420), channel_id=1, source_target_pairs={{0,8},{4,12},{8,0},{12,4},{1,9},{5,13},{9,1},{13,5},{2,10},{6,14},... | collective-permute-start | bytes 786440 | tf_op jit(solution)/shard_map/ppermute | solution.py:807
  544.3 30.2 %collective-permute-start.44 = (bf16[256,512]{1,0:T(8,128)(2,1)S(1)}, bf16[256,512]{1,0:T(8,128)(2,1)S(1)}, u32[]{:S(2)}, u32[]{:S(2)}) collective-permute-start(bf16[256,512]{1,0:T(8,128)(2,1)S(1)} %convert_element_type.419), channel_id=1, source_target_pairs={{0,4},{4,0},{8,12},{12,8},{1,5},{5,1},{9,13},{13,9},{2,6},{6,2},{1... | collective-permute-start | bytes 786440 | tf_op jit(solution)/shard_map/ppermute | solution.py:807
  585.1 19.9 %collective-permute-start.49 = (bf16[256,512]{1,0:T(8,128)(2,1)S(1)}, bf16[256,512]{1,0:T(8,128)(2,1)S(1)}, u32[]{:S(2)}, u32[]{:S(2)}) collective-permute-start(bf16[256,512]{1,0:T(8,128)(2,1)S(1)} %convert_element_type.423), channel_id=1, source_target_pairs={{0,8},{4,12},{8,0},{12,4},{1,9},{5,13},{9,1},{13,5},{2,10},{6,14},... | collective-permute-start | bytes 786440 | tf_op jit(solution)/shard_map/ppermute | solution.py:807
  587.2 19.2 %collective-permute-start.48 = (bf16[256,512]{1,0:T(8,128)(2,1)S(1)}, bf16[256,512]{1,0:T(8,128)(2,1)S(1)}, u32[]{:S(2)}, u32[]{:S(2)}) collective-permute-start(bf16[256,512]{1,0:T(8,128)(2,1)S(1)} %convert_element_type.422), channel_id=1, source_target_pairs={{0,4},{4,0},{8,12},{12,8},{1,5},{5,1},{9,13},{13,9},{2,6},{6,2},{1... | collective-permute-start | bytes 786440 | tf_op jit(solution)/shard_map/ppermute | solution.py:807
  589.8 27.1 %collective-permute-start.47 = (bf16[128,2304]{1,0:T(8,128)(2,1)S(1)}, bf16[128,2304]{1,0:T(8,128)(2,1)S(1)}, u32[]{:S(2)}, u32[]{:S(2)}) collective-permute-start(bf16[128,2304]{1,0:T(8,128)(2,1)S(1)} %copy-done.53), channel_id=1, source_target_pairs={{0,1},{3,2},{4,5},{7,6},{8,9},{11,10},{12,13},{15,14},{16,17},{19,... | collective-permute-start | bytes 1769480 | tf_op jit(solution)/shard_map/ppermute | solution.py:558
  591.5 29.3 %collective-permute-start.54 = (bf16[128,2304]{1,0:T(8,128)(2,1)S(1)}, bf16[128,2304]{1,0:T(8,128)(2,1)}, u32[]{:S(2)}, u32[]{:S(2)}) collective-permute-start(bf16[128,2304]{1,0:T(8,128)(2,1)S(1)} %copy-done.51), channel_id=1, source_target_pairs={{0,1},{3,2},{4,5},{7,6},{8,9},{11,10},{12,13},{15,14},{16,17},{19,... | collective-permute-start | bytes 1769480 | tf_op jit(solution)/shard_map/ppermute | solution.py:558
  613.1 32.9 %collective-permute-start.57 = (bf16[128,2304]{1,0:T(8,128)(2,1)}, bf16[128,2304]{1,0:T(8,128)(2,1)S(1)}, u32[]{:S(2)}, u32[]{:S(2)}) collective-permute-start(bf16[128,2304]{1,0:T(8,128)(2,1)} %get-tuple-element.430), channel_id=1, source_target_pairs={{0,1},{3,2},{4,5},{7,6},{8,9},{11,10},{12,13},{15,14},{16,17},{19,... | collective-permute-start | bytes 1769480 | tf_op jit(solution)/shard_map/ppermute | solution.py:558
  619.2 24.1 %collective-permute-start.53 = (bf16[128,2304]{1,0:T(8,128)(2,1)S(1)}, bf16[128,2304]{1,0:T(8,128)(2,1)}, u32[]{:S(2)}, u32[]{:S(2)}) collective-permute-start(bf16[128,2304]{1,0:T(8,128)(2,1)S(1)} %reduce-precision_convert_fusion.7), channel_id=1, source_target_pairs={{1,2},{2,1},{5,6},{6,5},{9,10},{10,9},{13,14},{14,13},{17,18},{18,... | collective-permute-start | bytes 1769480 | tf_op jit(solution)/shard_map/ppermute | solution.py:567
  636.1 39.9 %collective-permute-start.60 = (bf16[128,2304]{1,0:T(8,128)(2,1)}, bf16[128,2304]{1,0:T(8,128)(2,1)}, u32[]{:S(2)}, u32[]{:S(2)}) collective-permute-start(bf16[128,2304]{1,0:T(8,128)(2,1)} %get-tuple-element.457), channel_id=1, source_target_pairs={{0,1},{3,2},{4,5},{7,6},{8,9},{11,10},{12,13},{15,14},{16,17},{19,... | collective-permute-start | bytes 1769480 | tf_op jit(solution)/shard_map/ppermute | solution.py:558
  644.6 18.2 %collective-permute-start.55 = (bf16[128,2304]{1,0:T(8,128)(2,1)S(1)}, bf16[128,2304]{1,0:T(8,128)(2,1)S(1)}, u32[]{:S(2)}, u32[]{:S(2)}) collective-permute-start(bf16[128,2304]{1,0:T(8,128)(2,1)S(1)} %reduce-precision_convert_fusion.5.total_ref), channel_id=1, source_target_pairs={{1,0},{2,3},{5,4},{6,7},{9,8},{10,11},{13,12},{14,15},{17,16},{18,... | collective-permute-start | bytes 1769480 | tf_op jit(solution)/shard_map/ppermute | solution.py:574
  646.2 36.6 %collective-permute-start.59 = (bf16[128,2304]{1,0:T(8,128)(2,1)S(1)}, bf16[128,2304]{1,0:T(8,128)(2,1)}, u32[]{:S(2)}, u32[]{:S(2)}) collective-permute-start(bf16[128,2304]{1,0:T(8,128)(2,1)S(1)} %reduce-precision_convert_fusion.4), channel_id=1, source_target_pairs={{1,2},{2,1},{5,6},{6,5},{9,10},{10,9},{13,14},{14,13},{17,18},{18,... | collective-permute-start | bytes 1769480 | tf_op jit(solution)/shard_map/ppermute | solution.py:567
  648.9 36.4 %collective-permute-start.58 = (bf16[128,2304]{1,0:T(8,128)(2,1)S(1)}, bf16[128,2304]{1,0:T(8,128)(2,1)}, u32[]{:S(2)}, u32[]{:S(2)}) collective-permute-start(bf16[128,2304]{1,0:T(8,128)(2,1)S(1)} %reduce-precision_convert_fusion.3.total_ref), channel_id=1, source_target_pairs={{1,0},{2,3},{5,4},{6,7},{9,8},{10,11},{13,12},{14,15},{17,16},{18,... | collective-permute-start | bytes 1769480 | tf_op jit(solution)/shard_map/ppermute | solution.py:574
  675.9 47.0 %all-to-all-start = ((bf16[4,288,1664]{2,1,0:T(8,128)(2,1)}), bf16[4,288,1664]{2,1,0:T(8,128)(2,1)}, u32[]{:S(2)}, u32[]{:S(2)}) async-start(bf16[4,288,1664]{2,1,0:T(8,128)(2,1)} %bitcast.76), calls=%async_computation.1 | async-start | bytes 7667712 | tf_op jit(solution)/shard_map/all_to_all | solution.py:673
  684.0 18.0 %collective-permute-start.65 = (bf16[128,2304]{1,0:T(8,128)(2,1)S(1)}, bf16[128,2304]{1,0:T(8,128)(2,1)S(1)}, u32[]{:S(2)}, u32[]{:S(2)}) collective-permute-start(bf16[128,2304]{1,0:T(8,128)(2,1)S(1)} %reduce-precision_convert_fusion.1.total_ref), channel_id=1, source_target_pairs={{1,0},{2,3},{5,4},{6,7},{9,8},{10,11},{13,12},{14,15},{17,16},{18,... | collective-permute-start | bytes 1769480 | tf_op jit(solution)/shard_map/ppermute | solution.py:574
  688.6 23.5 %collective-permute-start.67 = (bf16[128,2304]{1,0:T(8,128)(2,1)S(1)}, bf16[128,2304]{1,0:T(8,128)(2,1)S(1)}, u32[]{:S(2)}, u32[]{:S(2)}) collective-permute-start(bf16[128,2304]{1,0:T(8,128)(2,1)S(1)} %reduce-precision_convert_fusion.total_ref), channel_id=1, source_target_pairs={{1,0},{2,3},{5,4},{6,7},{9,8},{10,11},{13,12},{14,15},{17,16},{18,... | collective-permute-start | bytes 1769480 | tf_op jit(solution)/shard_map/ppermute | solution.py:574
  (123 other events, 1084.9 us)
Sparse Core Ops, SparseCore 0:
  15.2 53.9 all-gather.2
  71.0 175.9 all-gather.4
  453.7 61.8 reduce-scatter.2
  518.5 126.9 reduce-scatter.4

commit v3 on v2

--- a/solution.py
+++ b/solution.py
@@ -748,28 +748,29 @@
     red = Reduce(chain)
     attention(0)
     attention(1)
-    red.run(n_one, post_attend, {})
+    held = {}
+
+    def hold(name, make):
+        def run():
+            held[name] = make()
+
+        return run
+
+    red.run(
+        n_one, post_attend, {n_one + 1: hold("left", lambda: chain.mark(left_side([normed])))}
+    )
 
     red = Reduce(chain)
     values = chain.after(*normed_two)
     gate, up, hidden, *part = ffn(list(values), full_ffn, ff, n_two)
     chain.mark(part[0])
     red.load(part)
-    held = {}
-
-    def hold(name, make):
-        def run():
-            held[name] = make()
-
-        return run
-
     red.run(
         n_two,
         post_ffn,
         {
-            0: hold("down_right", lambda: chain.mark(right_side([hidden]))),
-            1: hold("mid_left", lambda: chain.mark(left_side(normed_two))),
-            2: hold("left", lambda: chain.mark(left_side([normed]))),
+            0: hold("down_right", lambda: right_side([hidden])),
+            1: hold("mid_left", lambda: left_side(normed_two)),
         },
     )
 
@@ -832,12 +833,13 @@
 
     def tail():
         d_qkv = product(held["left"], held["right"])
+        owner = zi == 0
         gain_cols = jnp.stack(
             [
-                gain_in[0],
-                sum(v[1] for v in gain_mid),
-                sum(v[0] for v in gain_mid),
-                sum(v[0] for v in gain_fin),
+                st[0]["gain"][0] + st[1]["gain"][0],
+                jnp.where(owner, sum(v[1] for v in gain_mid), 0.0),
+                jnp.where(owner, sum(v[0] for v in gain_mid), 0.0),
+                jnp.where(owner, sum(v[0] for v in gain_fin), 0.0),
             ],
             axis=1,
         )
@@ -865,28 +867,27 @@
     def finish_tail():
         (value,) = chain.after(held["g_tail"])
         ends = [0, qc, qc + kc, at_out, at_out + oc, at_out + oc + PAD]
-        spans = [[span] for span in zip(ends[:-1], ends[1:])]
-        *held["g_attn"], g_gains = sum_parts(value, ends[-1], spans)
-        held["g_gains"] = mm_t(pick.astype(F32), g_gains)
+        *held["g_attn"], g_gains = sum_parts(value, ends[-1], [[v] for v in zip(ends, ends[1:])])
+        g_gains = chain.mark(mm_t(pick.astype(F32), g_gains))
+        held["g_gains"] = lax.all_to_all(
+            jnp.broadcast_to(g_gains[None], (n_t,) + g_gains.shape), "tensor", 0, 0
+        )
 
     red = Reduce(chain)
-    block_out = chain.mark(jnp.concatenate(chain.after(*outputs), axis=0))
-    finish_down()
     input_back(0)
     d_out = product(left_side(attn_grads), right_side([s["attended"] for s in st]))
     input_back(1)
     held["right"] = right_side([s["qkv_back"] for s in st])
-    gain_in = (st[0]["gain"] + st[1]["gain"])[:4]
-    reach = 1
-    while reach < n_t:
-        steps = [(i, i ^ reach) for i in range(n_t)]
-        gain_in = gain_in + lax.ppermute(gain_in, "tensor", steps)
-        reach *= 2
-    red.run(n_four, post_in, {2: tail, 4: finish_tail})
-    finish_both()
-    g_gains = held["g_gains"]
+
+    def finish_rest():
+        finish_down()
+        finish_both()
+        finish_tail()
+
+    red.run(n_four, post_in, {1: tail, 4: finish_rest})
+    g_gains = jnp.sum(held["g_gains"], axis=0)
     return (
-        block_out.reshape(tokens.shape),
+        jnp.concatenate(outputs, axis=0).reshape(tokens.shape),
         jnp.concatenate(input_grads, axis=0).reshape(tokens.shape),
         *held["g_attn"],
         held["g_gate"],

time: 750 us -> 702 us (0.936)
  waiting for transfers between devices: 321 us -> 281 us
  local copies, waits for them, and re-layouts: 42.2 us -> 33.8 us
    ppermute x16, waiting for transfers between devices: 114 us -> 97.3 us  [send(): self.first[k] = lax.ppermute(piece, 'tensor', [(0, 1), (3, 2)])]
    ppermute x2 -> x0, waiting for transfers between devices: 9.74 us -> none  [local(): gain_in = gain_in + lax.ppermute(gain_in, 'tensor', steps)]
    unnamed x215 -> x191, local copies, waits for them, and re-layouts: 30.9 us -> 22.9 us
  transfers between devices with their start and end apart: 73 -> 72, of which waited for: 36 -> 32; matrix products, arithmetic and copies ran while one was open for 10% -> 11% of each run, Pallas kernels for 14% -> 22%
where the time goes in v3:
time: 702 us; the launch traced here: 691 us
  waiting for transfers between devices  281 us (40%)
  Pallas kernels  179 us (25%)
  starting transfers between devices  106 us (15%)
  other arithmetic  45.4 us (6%)
  local copies, waits for them, and re-layouts  33.8 us (5%)
  matrix products  29.9 us (4%)
  between operations  16.1 us (2%)
    ppermute x16, waiting for transfers between devices, send(): self.first[k] = lax.ppermute(piece, 'tensor', [(0, 1), (3, 2)])  97.3 us
    ppermute x16, waiting for transfers between devices, join(): self.third[k] = lax.ppermute(total, 'tensor', [(1, 0), (2, 3)])  81.5 us
    pallas_call x16, Pallas kernels, post(): call(body, tuple(out_shapes), (steps,), specs, tuple(out_specs), flops=20...  56.6 us
    ppermute x16, starting transfers between devices, send(): self.first[k] = lax.ppermute(piece, 'tensor', [(0, 1), (3, 2)])  49.3 us
    ppermute x3, waiting for transfers between devices, local(): others = [lax.ppermute(kv, 'ctx', flips[j]) for j in range(1, n_ctx)]  43.9 us
    all_gather x1, waiting for transfers between devices, local(): full_attn = lax.all_gather(pack_attn, ('dp', 'ctx'), axis=0, tiled=True)  42 us
    pallas_call x1, Pallas kernels, ffn_back(): call(functools.partial(ffn_back_body, len(ys), n_out), (shape((rows, 2 *...  37.1 us
    dot_general x4, matrix products, tmm(): lax.dot_general(a, b, (((0,), (0,)), ((), ())), preferred_element_type=F32)  27.6 us
  transfers between devices with their start and end apart: 72, of which 32 were waited for; matrix products, arithmetic and copies ran while one was open for 11% of the time, Pallas kernels for 22%

profile of v3, /device:TPU:0, one launch (start us, length us, event | category | flops | bytes accessed | tf_op | source)
XLA Modules:
  0.0 690.8 jit_solution(6976450895032251592)
XLA Ops:
  21.3 4.5 compare_select_fusion.1
  27.2 42.0 %all-gather.3.cloned.1.call-done.w_ref.refs_3_.refs_7_.refs_4_ = bf16[2304,1664]{1,0:T(8,128)(2,1)} async-done(((bf16[288,1664]{1,0:T(8,128)(2,1)}), bf16[2304,1664]{1,0:T(8,128)(2,1)}) %all-gather.3.cloned.1.call-update) | async-done | bytes 7667728 | tf_op jit(solution)/shard_map/all_gather | solution.py:644
  74.0 7.0 %shard_map.237.refs_0_ = bf16[512,1024]{1,0:T(8,128)(2,1)} custom-call(bf16[512,2304]{1,0:T(8,128)(2,1)} %multiply_convert_fusion.x_ref, bf16[2304,1664]{1,0:T(8,128)(2,1)} %all-gather.3.cloned.1.call-done.w_ref.refs_3_.refs_7_.refs_4_, f32[512,128]{1,0:T(8,128)} %bitcast.84, f32[512,128]{1,0:T(8,128)} %bitcast.83), custom_call_target="tpu_custom_call" | custom-call | flops 2415919104 | bytes 8126464 | tf_op jit(solution)/shard_map/pallas_call | solution.py:93
  87.1 21.8 %collective-permute-done.2.refs_7_.refs_11_ = bf16[512,512]{1,0:T(8,128)(2,1)S(1)} collective-permute-done((bf16[512,512]{1,0:T(8,128)(2,1)S(1)}, bf16[512,512]{1,0:T(8,128)(2,1)S(1)}, u32[]{:S(2)}, u32[]{:S(2)}) %collective-permute-start.2) | collective-permute-done | bytes 524320 | tf_op jit(solution)/shard_map/ppermute | solution.py:692
  108.9 11.2 %collective-permute-done.1.refs_6_.refs_10_ = bf16[512,512]{1,0:T(8,128)(2,1)S(1)} collective-permute-done((bf16[512,512]{1,0:T(8,128)(2,1)S(1)}, bf16[512,512]{1,0:T(8,128)(2,1)S(1)}, u32[]{:S(2)}, u32[]{:S(2)}) %collective-permute-start.1) | collective-permute-done | bytes 524320 | tf_op jit(solution)/shard_map/ppermute | solution.py:692
  120.1 10.9 %collective-permute-done.refs_5_.refs_9_ = bf16[512,512]{1,0:T(8,128)(2,1)S(1)} collective-permute-done((bf16[512,512]{1,0:T(8,128)(2,1)S(1)}, bf16[512,512]{1,0:T(8,128)(2,1)S(1)}, u32[]{:S(2)}, u32[]{:S(2)}) %collective-permute-start) | collective-permute-done | bytes 524320 | tf_op jit(solution)/shard_map/ppermute | solution.py:692
  131.8 4.9 shard_map.238
  141.6 4.8 shard_map.239
  149.2 4.9 collective-permute-done.3
  155.0 11.6 %collective-permute-done.5 = bf16[128,2304]{1,0:T(8,128)(2,1)S(1)} collective-permute-done((bf16[128,2304]{1,0:T(8,128)(2,1)}, bf16[128,2304]{1,0:T(8,128)(2,1)S(1)}, u32[]{:S(2)}, u32[]{:S(2)}) %collective-permute-start.5) | collective-permute-done | bytes 589856 | tf_op jit(solution)/shard_map/ppermute | solution.py:558
  169.0 21.3 %collective-permute-done.8 = bf16[128,2304]{1,0:T(8,128)(2,1)S(1)} collective-permute-done((bf16[128,2304]{1,0:T(8,128)(2,1)}, bf16[128,2304]{1,0:T(8,128)(2,1)S(1)}, u32[]{:S(2)}, u32[]{:S(2)}) %collective-permute-start.8) | collective-permute-done | bytes 589856 | tf_op jit(solution)/shard_map/ppermute | solution.py:558
  198.8 11.9 %collective-permute-done.9.third_ref = bf16[128,2304]{1,0:T(8,128)(2,1)} collective-permute-done((bf16[128,2304]{1,0:T(8,128)(2,1)S(1)}, bf16[128,2304]{1,0:T(8,128)(2,1)}, u32[]{:S(2)}, u32[]{:S(2)}) %collective-permute-start.9) | collective-permute-done | bytes 589856 | tf_op jit(solution)/shard_map/ppermute | solution.py:574
  215.1 8.1 %collective-permute-done.12.third_ref = bf16[128,2304]{1,0:T(8,128)(2,1)S(1)} collective-permute-done((bf16[128,2304]{1,0:T(8,128)(2,1)S(1)}, bf16[128,2304]{1,0:T(8,128)(2,1)S(1)}, u32[]{:S(2)}, u32[]{:S(2)}) %collective-permute-start.12) | collective-permute-done | bytes 589856 | tf_op jit(solution)/shard_map/ppermute | solution.py:574
  226.8 8.1 %collective-permute-done.14.third_ref = bf16[128,2304]{1,0:T(8,128)(2,1)S(1)} collective-permute-done((bf16[128,2304]{1,0:T(8,128)(2,1)S(1)}, bf16[128,2304]{1,0:T(8,128)(2,1)S(1)}, u32[]{:S(2)}, u32[]{:S(2)}) %collective-permute-start.14) | collective-permute-done | bytes 589856 | tf_op jit(solution)/shard_map/ppermute | solution.py:574
  247.0 25.4 %shard_map.244 = (bf16[512,2304]{1,0:T(8,128)(2,1)}, bf16[512,2304]{1,0:T(8,128)(2,1)}, bf16[512,2304]{1,0:T(8,128)(2,1)}, bf16[128,2304]{1,0:T(8,128)(2,1)}, bf...) custom-call(bf16[128,2304]{1,0:T(8,128)(2,1)} %get-tuple-element.349.refs_0_, ...), custom_call_target="tpu_custom_call" | custom-call | flops 16307453952 | bytes 43646976 | tf_op jit(solution)/shard_map/pallas_call | solution.py:425
  279.9 10.0 %collective-permute-done.16 = bf16[128,2304]{1,0:T(8,128)(2,1)S(1)} collective-permute-done((bf16[128,2304]{1,0:T(8,128)(2,1)}, bf16[128,2304]{1,0:T(8,128)(2,1)S(1)}, u32[]{:S(2)}, u32[]{:S(2)}) %collective-permute-start.16) | collective-permute-done | bytes 589856 | tf_op jit(solution)/shard_map/ppermute | solution.py:558
  292.0 10.6 %collective-permute-done.18 = bf16[128,2304]{1,0:T(8,128)(2,1)S(1)} collective-permute-done((bf16[128,2304]{1,0:T(8,128)(2,1)}, bf16[128,2304]{1,0:T(8,128)(2,1)S(1)}, u32[]{:S(2)}, u32[]{:S(2)}) %collective-permute-start.18) | collective-permute-done | bytes 589856 | tf_op jit(solution)/shard_map/ppermute | solution.py:558
  304.9 10.3 %collective-permute-done.21 = bf16[128,2304]{1,0:T(8,128)(2,1)S(1)} collective-permute-done((bf16[128,2304]{1,0:T(8,128)(2,1)}, bf16[128,2304]{1,0:T(8,128)(2,1)S(1)}, u32[]{:S(2)}, u32[]{:S(2)}) %collective-permute-start.21) | collective-permute-done | bytes 589856 | tf_op jit(solution)/shard_map/ppermute | solution.py:558
  317.5 4.7 collective-permute-done.19.third_ref
  323.0 4.0 shard_map.245
  329.4 6.5 collective-permute-done.22.third_ref
  342.7 5.8 collective-permute-done.25.third_ref
  353.4 7.8 %collective-permute-done.27.third_ref = bf16[128,2304]{1,0:T(8,128)(2,1)S(1)} collective-permute-done((bf16[128,2304]{1,0:T(8,128)(2,1)S(1)}, bf16[128,2304]{1,0:T(8,128)(2,1)S(1)}, u32[]{:S(2)}, u32[]{:S(2)}) %collective-permute-start.27) | collective-permute-done | bytes 589856 | tf_op jit(solution)/shard_map/ppermute | solution.py:574
  366.1 37.1 %shard_map.249 = (bf16[512,4608]{1,0:T(8,128)(2,1)}, bf16[128,2304]{1,0:T(8,128)(2,1)}, bf16[128,2304]{1,0:T(8,128)(2,1)}, bf16[128,2304]{1,0:T(8,128)(2,1)}, bf16[128,2304]{1,0:T(8,128)(2,1)}) custom-call(bf16[128,2304]{1,0:T(8,128)(2,1)} %get-tuple-element.336.refs_0_, bf16[128,2304]{1,0:T(8,128)(2,1)} %get-tuple-element.337.refs_1_, ...), custom_call_target="tpu_custom_call" | custom-call | flops 16307453952 | bytes 46006272 | tf_op jit(solution)/shard_map/pallas_call | solution.py:477
  408.6 7.6 %collective-permute-done.28 = bf16[128,2304]{1,0:T(8,128)(2,1)S(1)} collective-permute-done((bf16[128,2304]{1,0:T(8,128)(2,1)}, bf16[128,2304]{1,0:T(8,128)(2,1)S(1)}, u32[]{:S(2)}, u32[]{:S(2)}) %collective-permute-start.28) | collective-permute-done | bytes 589856 | tf_op jit(solution)/shard_map/ppermute | solution.py:558
  416.6 7.5 %convolution_convert_fusion.1 = bf16[1152,2304]{1,0:T(8,128)(2,1)} fusion(bf16[1024,1152]{1,0:T(8,128)(2,1)S(1)} %pad_maximum_fusion.5, bf16[1024,2304]{1,0:T(8,128)(2,1)S(1)} %pad_maximum_fusion.1), kind=kOutput, calls=%fused_computation.1 | convolution fusion | flops 5438472192 | bytes 12386304 | tf_op jit(solution)/shard_map/dot_general | solution.py:47
  426.8 4.4 collective-permute-start.30
  435.2 8.5 %collective-permute-done.30 = bf16[128,2304]{1,0:T(8,128)(2,1)S(1)} collective-permute-done((bf16[128,2304]{1,0:T(8,128)(2,1)S(1)}, bf16[128,2304]{1,0:T(8,128)(2,1)S(1)}, u32[]{:S(2)}, u32[]{:S(2)}) %collective-permute-start.30) | collective-permute-done | bytes 589856 | tf_op jit(solution)/shard_map/ppermute | solution.py:558
  444.9 13.7 %convolution_convert_fusion = bf16[1152,4608]{1,0:T(8,128)(2,1)} fusion(bf16[1024,1152]{1,0:T(8,128)(2,1)S(1)} %pad_maximum_fusion.6, bf16[1024,4608]{1,0:T(8,128)(2,1)S(1)} %pad_maximum_fusion), kind=kOutput, calls=%fused_computation | convolution fusion | flops 10876944384 | bytes 22413312 | tf_op jit(solution)/shard_map/dot_general | solution.py:47
  459.7 12.0 %collective-permute-start.35 = (bf16[128,2304]{1,0:T(8,128)(2,1)S(1)}, bf16[128,2304]{1,0:T(8,128)(2,1)S(1)}, u32[]{:S(2)}, u32[]{:S(2)}) collective-permute-start(bf16[128,2304]{1,0:T(8,128)(2,1)S(1)} %copy-done.53), channel_id=1, source_target_pairs={{0,1},{3,2},{4,5},{7,6},{8,9},{11,10},{12,13},{15,14},{16,17},{19,... | collective-permute-start | bytes 1769480 | tf_op jit(solution)/shard_map/ppermute | solution.py:558
  475.0 10.3 %collective-permute-done.35 = bf16[128,2304]{1,0:T(8,128)(2,1)S(1)} collective-permute-done((bf16[128,2304]{1,0:T(8,128)(2,1)S(1)}, bf16[128,2304]{1,0:T(8,128)(2,1)S(1)}, u32[]{:S(2)}, u32[]{:S(2)}) %collective-permute-start.35) | collective-permute-done | bytes 589856 | tf_op jit(solution)/shard_map/ppermute | solution.py:558
  490.1 4.2 shard_map.250
  503.2 4.3 shard_map.251
  507.5 7.9 %shard_map.252 = (bf16[256,512]{1,0:T(8,128)(2,1)}, f32[256,512]{1,0:T(8,128)}, f32[256,512]{1,0:T(8,128)}, f32[256,512]{1,0:T(8,128)}, f32[256,512]{1,0:T(8,128)}) custom-call(bf16[512,1024]{1,0:T(8,128)(2,1)} %shard_map.237.refs_0_, s32[256,1]{1,0:T(8,128)} %copy.53.refs_1_, s32[1,1024]{1,0:T(1,128)} %bitcast.87, f32[256,512]{1,0:T(8,128)} %get-tuple-element.323.refs_3_, ...), custom_call_target="tpu_custom_call" | custom-call | flops 1946157056 | bytes 9961472 | tf_op jit(solution)/shard_map/pallas_call | solution.py:240
  522.4 4.3 shard_map.253
  526.7 4.1 collective-permute-done.46.third_ref
  531.6 4.3 shard_map.254
  535.9 7.8 %shard_map.255 = (bf16[256,512]{1,0:T(8,128)(2,1)}, f32[256,512]{1,0:T(8,128)}, f32[256,512]{1,0:T(8,128)}, f32[256,512]{1,0:T(8,128)}, f32[256,512]{1,0:T(8,128)}) custom-call(bf16[512,1024]{1,0:T(8,128)(2,1)} %shard_map.237.refs_0_, s32[256,1]{1,0:T(8,128)} %copy.53.refs_1_, s32[1,1024]{1,0:T(1,128)} %bitcast.88, f32[256,512]{1,0:T(8,128)} %get-tuple-element.379.refs_3_, ...), custom_call_target="tpu_custom_call" | custom-call | flops 1946157056 | bytes 9961472 | tf_op jit(solution)/shard_map/pallas_call | solution.py:240
  544.7 6.3 shard_map.256
  552.7 4.8 collective-permute-start.47
  572.6 4.5 collective-permute-done.49.refs_7_
  578.5 5.9 shard_map.257
  584.4 4.4 collective-permute-start.57
  597.4 4.2 collective-permute-start.62
  616.5 4.8 all-to-all-start
  631.3 14.2 %collective-permute-done.60.third_ref = bf16[128,2304]{1,0:T(8,128)(2,1)} collective-permute-done((bf16[128,2304]{1,0:T(8,128)(2,1)S(1)}, bf16[128,2304]{1,0:T(8,128)(2,1)}, u32[]{:S(2)}, u32[]{:S(2)}) %collective-permute-start.60) | collective-permute-done | bytes 589856 | tf_op jit(solution)/shard_map/ppermute | solution.py:574
  652.9 5.3 collective-permute-done.63.third_ref
  664.6 4.5 shard_map.263
  (421 shorter events, 219.8 us)
Async XLA Ops:
  7.2 62.0 %all-gather.3.cloned.1.call-start = ((), (), s32[]{:S(2)}) async-start(), calls=%async_computation.4 | async-start | bytes 8626176 | tf_op jit(solution)/shard_map/all_gather | solution.py:644
  15.1 231.9 %all-gather.5.cloned.1.call-start = ((), (), s32[]{:S(2)}) async-start(), calls=%async_computation.5 | async-start | bytes 35831808 | tf_op jit(solution)/shard_map/all_gather | solution.py:645
  18.5 642.7 %reduce-scatter.5.cloned.1.call-start = ((), (), s32[]{:S(2)}) async-start(), calls=%async_computation.7 | async-start | bytes 6635520 | tf_op jit(solution)/shard_map/reduce_scatter | solution.py:682
  82.2 26.7 %collective-permute-start.2 = (bf16[512,512]{1,0:T(8,128)(2,1)S(1)}, bf16[512,512]{1,0:T(8,128)(2,1)S(1)}, u32[]{:S(2)}, u32[]{:S(2)}) collective-permute-start(bf16[512,512]{1,0:T(8,128)(2,1)S(1)} %slice.95.refs_4_.refs_8_), channel_id=1, source_target_pairs={{0,12},{4,8},{8,4},{12,0},{1,13},{5,9},{9,5},{13,1},{2,14},{6,10},... | collective-permute-start | bytes 1572872 | tf_op jit(solution)/shard_map/ppermute | solution.py:692
  83.8 36.4 %collective-permute-start.1 = (bf16[512,512]{1,0:T(8,128)(2,1)S(1)}, bf16[512,512]{1,0:T(8,128)(2,1)S(1)}, u32[]{:S(2)}, u32[]{:S(2)}) collective-permute-start(bf16[512,512]{1,0:T(8,128)(2,1)S(1)} %slice.95.refs_4_.refs_8_), channel_id=1, source_target_pairs={{0,8},{4,12},{8,0},{12,4},{1,9},{5,13},{9,1},{13,5},{2,10},{6,14},... | collective-permute-start | bytes 1572872 | tf_op jit(solution)/shard_map/ppermute | solution.py:692
  85.2 45.8 %collective-permute-start = (bf16[512,512]{1,0:T(8,128)(2,1)S(1)}, bf16[512,512]{1,0:T(8,128)(2,1)S(1)}, u32[]{:S(2)}, u32[]{:S(2)}) collective-permute-start(bf16[512,512]{1,0:T(8,128)(2,1)S(1)} %slice.95.refs_4_.refs_8_), channel_id=1, source_target_pairs={{0,4},{4,0},{8,12},{12,8},{1,5},{5,1},{9,13},{13,9},{2,6},{6,2},{1... | collective-permute-start | bytes 1572872 | tf_op jit(solution)/shard_map/ppermute | solution.py:692
  136.6 17.4 %collective-permute-start.3 = (bf16[128,2304]{1,0:T(8,128)(2,1)}, bf16[128,2304]{1,0:T(8,128)(2,1)S(1)}, u32[]{:S(2)}, u32[]{:S(2)}) collective-permute-start(bf16[128,2304]{1,0:T(8,128)(2,1)} %get-tuple-element.249), channel_id=1, source_target_pairs={{0,1},{3,2},{4,5},{7,6},{8,9},{11,10},{12,13},{15,14},{16,17},{19,... | collective-permute-start | bytes 1769480 | tf_op jit(solution)/shard_map/ppermute | solution.py:558
  140.1 26.6 %collective-permute-start.5 = (bf16[128,2304]{1,0:T(8,128)(2,1)}, bf16[128,2304]{1,0:T(8,128)(2,1)S(1)}, u32[]{:S(2)}, u32[]{:S(2)}) collective-permute-start(bf16[128,2304]{1,0:T(8,128)(2,1)} %get-tuple-element.252), channel_id=1, source_target_pairs={{0,1},{3,2},{4,5},{7,6},{8,9},{11,10},{12,13},{15,14},{16,17},{19,... | collective-permute-start | bytes 1769480 | tf_op jit(solution)/shard_map/ppermute | solution.py:558
  146.4 50.0 %collective-permute-start.11 = (bf16[128,2304]{1,0:T(8,128)(2,1)}, bf16[128,2304]{1,0:T(8,128)(2,1)S(1)}, u32[]{:S(2)}, u32[]{:S(2)}) collective-permute-start(bf16[128,2304]{1,0:T(8,128)(2,1)} %get-tuple-element.264), channel_id=1, source_target_pairs={{0,1},{3,2},{4,5},{7,6},{8,9},{11,10},{12,13},{15,14},{16,17},{19,... | collective-permute-start | bytes 1769480 | tf_op jit(solution)/shard_map/ppermute | solution.py:558
  147.9 42.4 %collective-permute-start.8 = (bf16[128,2304]{1,0:T(8,128)(2,1)}, bf16[128,2304]{1,0:T(8,128)(2,1)S(1)}, u32[]{:S(2)}, u32[]{:S(2)}) collective-permute-start(bf16[128,2304]{1,0:T(8,128)(2,1)} %get-tuple-element.256), channel_id=1, source_target_pairs={{0,1},{3,2},{4,5},{7,6},{8,9},{11,10},{12,13},{15,14},{16,17},{19,... | collective-permute-start | bytes 1769480 | tf_op jit(solution)/shard_map/ppermute | solution.py:558
  166.8 24.3 %collective-permute-start.7 = (bf16[128,2304]{1,0:T(8,128)(2,1)S(1)}, bf16[128,2304]{1,0:T(8,128)(2,1)S(1)}, u32[]{:S(2)}, u32[]{:S(2)}) collective-permute-start(bf16[128,2304]{1,0:T(8,128)(2,1)S(1)} %reduce-precision_convert_fusion.30), channel_id=1, source_target_pairs={{1,2},{2,1},{5,6},{6,5},{9,10},{10,9},{13,14},{14,13},{17,18},{18,... | collective-permute-start | bytes 1769480 | tf_op jit(solution)/shard_map/ppermute | solution.py:567
  167.7 25.0 %collective-permute-start.6 = (bf16[128,2304]{1,0:T(8,128)(2,1)S(1)}, bf16[128,2304]{1,0:T(8,128)(2,1)S(1)}, u32[]{:S(2)}, u32[]{:S(2)}) collective-permute-start(bf16[128,2304]{1,0:T(8,128)(2,1)S(1)} %reduce-precision_convert_fusion.29.total_ref), channel_id=1, source_target_pairs={{1,0},{2,3},{5,4},{6,7},{9,8},{10,11},{13,12},{14,15},{17,16},{18,... | collective-permute-start | bytes 1769480 | tf_op jit(solution)/shard_map/ppermute | solution.py:574
  191.3 19.3 %collective-permute-start.9 = (bf16[128,2304]{1,0:T(8,128)(2,1)S(1)}, bf16[128,2304]{1,0:T(8,128)(2,1)}, u32[]{:S(2)}, u32[]{:S(2)}) collective-permute-start(bf16[128,2304]{1,0:T(8,128)(2,1)S(1)} %reduce-precision_convert_fusion.27.total_ref), channel_id=1, source_target_pairs={{1,0},{2,3},{5,4},{6,7},{9,8},{10,11},{13,12},{14,15},{17,16},{18,... | collective-permute-start | bytes 1769480 | tf_op jit(solution)/shard_map/ppermute | solution.py:574
  196.6 16.8 %collective-permute-start.13 = (bf16[128,2304]{1,0:T(8,128)(2,1)S(1)}, bf16[128,2304]{1,0:T(8,128)(2,1)S(1)}, u32[]{:S(2)}, u32[]{:S(2)}) collective-permute-start(bf16[128,2304]{1,0:T(8,128)(2,1)S(1)} %reduce-precision_convert_fusion.26), channel_id=1, source_target_pairs={{1,2},{2,1},{5,6},{6,5},{9,10},{10,9},{13,14},{14,13},{17,18},{18,... | collective-permute-start | bytes 1769480 | tf_op jit(solution)/shard_map/ppermute | solution.py:567
  197.4 25.7 %collective-permute-start.12 = (bf16[128,2304]{1,0:T(8,128)(2,1)S(1)}, bf16[128,2304]{1,0:T(8,128)(2,1)S(1)}, u32[]{:S(2)}, u32[]{:S(2)}) collective-permute-start(bf16[128,2304]{1,0:T(8,128)(2,1)S(1)} %reduce-precision_convert_fusion.25.total_ref), channel_id=1, source_target_pairs={{1,0},{2,3},{5,4},{6,7},{9,8},{10,11},{13,12},{14,15},{17,16},{18,... | collective-permute-start | bytes 1769480 | tf_op jit(solution)/shard_map/ppermute | solution.py:574
  213.6 21.3 %collective-permute-start.14 = (bf16[128,2304]{1,0:T(8,128)(2,1)S(1)}, bf16[128,2304]{1,0:T(8,128)(2,1)S(1)}, u32[]{:S(2)}, u32[]{:S(2)}) collective-permute-start(bf16[128,2304]{1,0:T(8,128)(2,1)S(1)} %reduce-precision_convert_fusion.24.total_ref), channel_id=1, source_target_pairs={{1,0},{2,3},{5,4},{6,7},{9,8},{10,11},{13,12},{14,15},{17,16},{18,... | collective-permute-start | bytes 1769480 | tf_op jit(solution)/shard_map/ppermute | solution.py:574
  272.4 17.5 %collective-permute-start.16 = (bf16[128,2304]{1,0:T(8,128)(2,1)}, bf16[128,2304]{1,0:T(8,128)(2,1)S(1)}, u32[]{:S(2)}, u32[]{:S(2)}) collective-permute-start(bf16[128,2304]{1,0:T(8,128)(2,1)} %get-tuple-element.285), channel_id=1, source_target_pairs={{0,1},{3,2},{4,5},{7,6},{8,9},{11,10},{12,13},{15,14},{16,17},{19,... | collective-permute-start | bytes 1769480 | tf_op jit(solution)/shard_map/ppermute | solution.py:558
  275.9 26.6 %collective-permute-start.18 = (bf16[128,2304]{1,0:T(8,128)(2,1)}, bf16[128,2304]{1,0:T(8,128)(2,1)S(1)}, u32[]{:S(2)}, u32[]{:S(2)}) collective-permute-start(bf16[128,2304]{1,0:T(8,128)(2,1)} %get-tuple-element.288), channel_id=1, source_target_pairs={{0,1},{3,2},{4,5},{7,6},{8,9},{11,10},{12,13},{15,14},{16,17},{19,... | collective-permute-start | bytes 1769480 | tf_op jit(solution)/shard_map/ppermute | solution.py:558
  277.3 37.9 %collective-permute-start.21 = (bf16[128,2304]{1,0:T(8,128)(2,1)}, bf16[128,2304]{1,0:T(8,128)(2,1)S(1)}, u32[]{:S(2)}, u32[]{:S(2)}) collective-permute-start(bf16[128,2304]{1,0:T(8,128)(2,1)} %get-tuple-element.293), channel_id=1, source_target_pairs={{0,1},{3,2},{4,5},{7,6},{8,9},{11,10},{12,13},{15,14},{16,17},{19,... | collective-permute-start | bytes 1769480 | tf_op jit(solution)/shard_map/ppermute | solution.py:558
  278.6 48.5 %collective-permute-start.24 = (bf16[128,2304]{1,0:T(8,128)(2,1)}, bf16[128,2304]{1,0:T(8,128)(2,1)S(1)}, u32[]{:S(2)}, u32[]{:S(2)}) collective-permute-start(bf16[128,2304]{1,0:T(8,128)(2,1)} %get-tuple-element.303), channel_id=1, source_target_pairs={{0,1},{3,2},{4,5},{7,6},{8,9},{11,10},{12,13},{15,14},{16,17},{19,... | collective-permute-start | bytes 1769480 | tf_op jit(solution)/shard_map/ppermute | solution.py:558
  303.6 18.6 %collective-permute-start.19 = (bf16[128,2304]{1,0:T(8,128)(2,1)S(1)}, bf16[128,2304]{1,0:T(8,128)(2,1)S(1)}, u32[]{:S(2)}, u32[]{:S(2)}) collective-permute-start(bf16[128,2304]{1,0:T(8,128)(2,1)S(1)} %reduce-precision_convert_fusion.21.total_ref), channel_id=1, source_target_pairs={{1,0},{2,3},{5,4},{6,7},{9,8},{10,11},{13,12},{14,15},{17,16},{18,... | collective-permute-start | bytes 1769480 | tf_op jit(solution)/shard_map/ppermute | solution.py:574
  316.2 19.7 %collective-permute-start.22 = (bf16[128,2304]{1,0:T(8,128)(2,1)S(1)}, bf16[128,2304]{1,0:T(8,128)(2,1)S(1)}, u32[]{:S(2)}, u32[]{:S(2)}) collective-permute-start(bf16[128,2304]{1,0:T(8,128)(2,1)S(1)} %reduce-precision_convert_fusion.19.total_ref), channel_id=1, source_target_pairs={{1,0},{2,3},{5,4},{6,7},{9,8},{10,11},{13,12},{14,15},{17,16},{18,... | collective-permute-start | bytes 1769480 | tf_op jit(solution)/shard_map/ppermute | solution.py:574
  328.1 20.4 %collective-permute-start.25 = (bf16[128,2304]{1,0:T(8,128)(2,1)S(1)}, bf16[128,2304]{1,0:T(8,128)(2,1)S(1)}, u32[]{:S(2)}, u32[]{:S(2)}) collective-permute-start(bf16[128,2304]{1,0:T(8,128)(2,1)S(1)} %reduce-precision_convert_fusion.17.total_ref), channel_id=1, source_target_pairs={{1,0},{2,3},{5,4},{6,7},{9,8},{10,11},{13,12},{14,15},{17,16},{18,... | collective-permute-start | bytes 1769480 | tf_op jit(solution)/shard_map/ppermute | solution.py:574
  340.9 20.3 %collective-permute-start.27 = (bf16[128,2304]{1,0:T(8,128)(2,1)S(1)}, bf16[128,2304]{1,0:T(8,128)(2,1)S(1)}, u32[]{:S(2)}, u32[]{:S(2)}) collective-permute-start(bf16[128,2304]{1,0:T(8,128)(2,1)S(1)} %reduce-precision_convert_fusion.16.total_ref), channel_id=1, source_target_pairs={{1,0},{2,3},{5,4},{6,7},{9,8},{10,11},{13,12},{14,15},{17,16},{18,... | collective-permute-start | bytes 1769480 | tf_op jit(solution)/shard_map/ppermute | solution.py:574
  342.6 62.8 %collective-permute-start.32 = (bf16[512,2304]{1,0:T(8,128)(2,1)}, bf16[512,2304]{1,0:T(8,128)(2,1)}, u32[]{:S(2)}, u32[]{:S(2)}) collective-permute-start(bf16[512,2304]{1,0:T(8,128)(2,1)} %get-tuple-element.341), channel_id=1, source_target_pairs={{0,16},{16,0},{1,17},{17,1},{2,18},{18,2},{3,19},{19,3},{4,20},{20... | collective-permute-start | bytes 7077896 | tf_op jit(solution)/shard_map/ppermute | solution.py:659
  424.2 240.4 %reduce-scatter.3.cloned.1.call-start = ((), (), s32[]{:S(2)}) async-start(), calls=%async_computation.6 | async-start | bytes 13271040 | tf_op jit(solution)/shard_map/reduce_scatter | solution.py:682
  424.3 19.8 %collective-permute-start.37 = (bf16[512,4608]{1,0:T(8,128)(2,1)}, bf16[512,4608]{1,0:T(8,128)(2,1)S(1)}, u32[]{:S(2)}, u32[]{:S(2)}) collective-permute-start(bf16[512,4608]{1,0:T(8,128)(2,1)} %get-tuple-element.354), channel_id=1, source_target_pairs={{0,16},{16,0},{1,17},{17,1},{2,18},{18,2},{3,19},{19,3},{4,20},{20... | collective-permute-start | bytes 14155784 | tf_op jit(solution)/shard_map/ppermute | solution.py:659
  426.8 16.9 %collective-permute-start.30 = (bf16[128,2304]{1,0:T(8,128)(2,1)S(1)}, bf16[128,2304]{1,0:T(8,128)(2,1)S(1)}, u32[]{:S(2)}, u32[]{:S(2)}) collective-permute-start(bf16[128,2304]{1,0:T(8,128)(2,1)S(1)} %copy-done.55), channel_id=1, source_target_pairs={{0,1},{3,2},{4,5},{7,6},{8,9},{11,10},{12,13},{15,14},{16,17},{19,... | collective-permute-start | bytes 1769480 | tf_op jit(solution)/shard_map/ppermute | solution.py:558
  459.7 25.7 %collective-permute-start.35 = (bf16[128,2304]{1,0:T(8,128)(2,1)S(1)}, bf16[128,2304]{1,0:T(8,128)(2,1)S(1)}, u32[]{:S(2)}, u32[]{:S(2)}) collective-permute-start(bf16[128,2304]{1,0:T(8,128)(2,1)S(1)} %copy-done.53), channel_id=1, source_target_pairs={{0,1},{3,2},{4,5},{7,6},{8,9},{11,10},{12,13},{15,14},{16,17},{19,... | collective-permute-start | bytes 1769480 | tf_op jit(solution)/shard_map/ppermute | solution.py:558
  471.7 24.7 %collective-permute-start.40 = (bf16[128,2304]{1,0:T(8,128)(2,1)S(1)}, bf16[128,2304]{1,0:T(8,128)(2,1)S(1)}, u32[]{:S(2)}, u32[]{:S(2)}) collective-permute-start(bf16[128,2304]{1,0:T(8,128)(2,1)S(1)} %copy-done.52), channel_id=1, source_target_pairs={{0,1},{3,2},{4,5},{7,6},{8,9},{11,10},{12,13},{15,14},{16,17},{19,... | collective-permute-start | bytes 1769480 | tf_op jit(solution)/shard_map/ppermute | solution.py:558
  473.7 16.3 %collective-permute-start.33 = (bf16[128,2304]{1,0:T(8,128)(2,1)S(1)}, bf16[128,2304]{1,0:T(8,128)(2,1)}, u32[]{:S(2)}, u32[]{:S(2)}) collective-permute-start(bf16[128,2304]{1,0:T(8,128)(2,1)S(1)} %reduce-precision_convert_fusion.13.total_ref), channel_id=1, source_target_pairs={{1,0},{2,3},{5,4},{6,7},{9,8},{10,11},{13,12},{14,15},{17,16},{18,... | collective-permute-start | bytes 1769480 | tf_op jit(solution)/shard_map/ppermute | solution.py:574
  487.1 16.1 %collective-permute-start.38 = (bf16[128,2304]{1,0:T(8,128)(2,1)S(1)}, bf16[128,2304]{1,0:T(8,128)(2,1)}, u32[]{:S(2)}, u32[]{:S(2)}) collective-permute-start(bf16[128,2304]{1,0:T(8,128)(2,1)S(1)} %reduce-precision_convert_fusion.11.total_ref), channel_id=1, source_target_pairs={{1,0},{2,3},{5,4},{6,7},{9,8},{10,11},{13,12},{14,15},{17,16},{18,... | collective-permute-start | bytes 1769480 | tf_op jit(solution)/shard_map/ppermute | solution.py:574
  496.5 18.8 %collective-permute-start.45 = (bf16[128,2304]{1,0:T(8,128)(2,1)S(1)}, bf16[128,2304]{1,0:T(8,128)(2,1)S(1)}, u32[]{:S(2)}, u32[]{:S(2)}) collective-permute-start(bf16[128,2304]{1,0:T(8,128)(2,1)S(1)} %reduce-precision_convert_fusion.10), channel_id=1, source_target_pairs={{1,2},{2,1},{5,6},{6,5},{9,10},{10,9},{13,14},{14,13},{17,18},{18,... | collective-permute-start | bytes 1769480 | tf_op jit(solution)/shard_map/ppermute | solution.py:567
  498.5 23.1 %collective-permute-start.44 = (bf16[128,2304]{1,0:T(8,128)(2,1)S(1)}, bf16[128,2304]{1,0:T(8,128)(2,1)S(1)}, u32[]{:S(2)}, u32[]{:S(2)}) collective-permute-start(bf16[128,2304]{1,0:T(8,128)(2,1)S(1)} %reduce-precision_convert_fusion.9.total_ref), channel_id=1, source_target_pairs={{1,0},{2,3},{5,4},{6,7},{9,8},{10,11},{13,12},{14,15},{17,16},{18,... | collective-permute-start | bytes 1769480 | tf_op jit(solution)/shard_map/ppermute | solution.py:574
  518.0 25.8 %collective-permute-start.43 = (bf16[256,512]{1,0:T(8,128)(2,1)S(1)}, bf16[256,512]{1,0:T(8,128)(2,1)S(1)}, u32[]{:S(2)}, u32[]{:S(2)}) collective-permute-start(bf16[256,512]{1,0:T(8,128)(2,1)S(1)} %convert_element_type.418), channel_id=1, source_target_pairs={{0,12},{4,8},{8,4},{12,0},{1,13},{5,9},{9,5},{13,1},{2,14},{6,10},... | collective-permute-start | bytes 786440 | tf_op jit(solution)/shard_map/ppermute | solution.py:808
  519.5 24.3 %collective-permute-start.42 = (bf16[256,512]{1,0:T(8,128)(2,1)}, bf16[256,512]{1,0:T(8,128)(2,1)S(1)}, u32[]{:S(2)}, u32[]{:S(2)}) collective-permute-start(bf16[256,512]{1,0:T(8,128)(2,1)} %convert_element_type.417), channel_id=1, source_target_pairs={{0,8},{4,12},{8,0},{12,4},{1,9},{5,13},{9,1},{13,5},{2,10},{6,14},... | collective-permute-start | bytes 786440 | tf_op jit(solution)/shard_map/ppermute | solution.py:808
  521.0 22.8 %collective-permute-start.41 = (bf16[256,512]{1,0:T(8,128)(2,1)S(1)}, bf16[256,512]{1,0:T(8,128)(2,1)S(1)}, u32[]{:S(2)}, u32[]{:S(2)}) collective-permute-start(bf16[256,512]{1,0:T(8,128)(2,1)S(1)} %convert_element_type.416), channel_id=1, source_target_pairs={{0,4},{4,0},{8,12},{12,8},{1,5},{5,1},{9,13},{13,9},{2,6},{6,2},{1... | collective-permute-start | bytes 786440 | tf_op jit(solution)/shard_map/ppermute | solution.py:808
  552.7 36.1 %collective-permute-start.47 = (bf16[128,2304]{1,0:T(8,128)(2,1)}, bf16[128,2304]{1,0:T(8,128)(2,1)}, u32[]{:S(2)}, u32[]{:S(2)}) collective-permute-start(bf16[128,2304]{1,0:T(8,128)(2,1)} %get-tuple-element.414), channel_id=1, source_target_pairs={{0,1},{3,2},{4,5},{7,6},{8,9},{11,10},{12,13},{15,14},{16,17},{19,... | collective-permute-start | bytes 1769480 | tf_op jit(solution)/shard_map/ppermute | solution.py:558
  566.5 25.2 %collective-permute-start.54 = (bf16[128,2304]{1,0:T(8,128)(2,1)}, bf16[128,2304]{1,0:T(8,128)(2,1)S(1)}, u32[]{:S(2)}, u32[]{:S(2)}) collective-permute-start(bf16[128,2304]{1,0:T(8,128)(2,1)} %get-tuple-element.417), channel_id=1, source_target_pairs={{0,1},{3,2},{4,5},{7,6},{8,9},{11,10},{12,13},{15,14},{16,17},{19,... | collective-permute-start | bytes 1769480 | tf_op jit(solution)/shard_map/ppermute | solution.py:558
  584.4 30.2 %collective-permute-start.57 = (bf16[128,2304]{1,0:T(8,128)(2,1)}, bf16[128,2304]{1,0:T(8,128)(2,1)}, u32[]{:S(2)}, u32[]{:S(2)}) collective-permute-start(bf16[128,2304]{1,0:T(8,128)(2,1)} %get-tuple-element.440), channel_id=1, source_target_pairs={{0,1},{3,2},{4,5},{7,6},{8,9},{11,10},{12,13},{15,14},{16,17},{19,... | collective-permute-start | bytes 1769480 | tf_op jit(solution)/shard_map/ppermute | solution.py:558
  595.9 20.6 %collective-permute-start.56 = (bf16[128,2304]{1,0:T(8,128)(2,1)S(1)}, bf16[128,2304]{1,0:T(8,128)(2,1)}, u32[]{:S(2)}, u32[]{:S(2)}) collective-permute-start(bf16[128,2304]{1,0:T(8,128)(2,1)S(1)} %reduce-precision_convert_fusion.6), channel_id=1, source_target_pairs={{1,2},{2,1},{5,6},{6,5},{9,10},{10,9},{13,14},{14,13},{17,18},{18,... | collective-permute-start | bytes 1769480 | tf_op jit(solution)/shard_map/ppermute | solution.py:567
  597.4 29.5 %collective-permute-start.62 = (bf16[128,2304]{1,0:T(8,128)(2,1)}, bf16[128,2304]{1,0:T(8,128)(2,1)}, u32[]{:S(2)}, u32[]{:S(2)}) collective-permute-start(bf16[128,2304]{1,0:T(8,128)(2,1)} %get-tuple-element.448), channel_id=1, source_target_pairs={{0,1},{3,2},{4,5},{7,6},{8,9},{11,10},{12,13},{15,14},{16,17},{19,... | collective-permute-start | bytes 1769480 | tf_op jit(solution)/shard_map/ppermute | solution.py:558
  604.1 19.8 %collective-permute-start.55 = (bf16[128,2304]{1,0:T(8,128)(2,1)S(1)}, bf16[128,2304]{1,0:T(8,128)(2,1)}, u32[]{:S(2)}, u32[]{:S(2)}) collective-permute-start(bf16[128,2304]{1,0:T(8,128)(2,1)S(1)} %reduce-precision_convert_fusion.5.total_ref), channel_id=1, source_target_pairs={{1,0},{2,3},{5,4},{6,7},{9,8},{10,11},{13,12},{14,15},{17,16},{18,... | collective-permute-start | bytes 1769480 | tf_op jit(solution)/shard_map/ppermute | solution.py:574
  616.5 52.5 %all-to-all-start = ((bf16[4,288,1664]{2,1,0:T(8,128)(2,1)}), bf16[4,288,1664]{2,1,0:T(8,128)(2,1)}, u32[]{:S(2)}, u32[]{:S(2)}) async-start(bf16[4,288,1664]{2,1,0:T(8,128)(2,1)} %bitcast.76), calls=%async_computation | async-start | bytes 7667712 | tf_op jit(solution)/shard_map/all_to_all | solution.py:673
  622.5 22.9 %collective-permute-start.60 = (bf16[128,2304]{1,0:T(8,128)(2,1)S(1)}, bf16[128,2304]{1,0:T(8,128)(2,1)}, u32[]{:S(2)}, u32[]{:S(2)}) collective-permute-start(bf16[128,2304]{1,0:T(8,128)(2,1)S(1)} %reduce-precision_convert_fusion.3.total_ref), channel_id=1, source_target_pairs={{1,0},{2,3},{5,4},{6,7},{9,8},{10,11},{13,12},{14,15},{17,16},{18,... | collective-permute-start | bytes 1769480 | tf_op jit(solution)/shard_map/ppermute | solution.py:574
  628.3 20.3 %collective-permute-start.64 = (bf16[128,2304]{1,0:T(8,128)(2,1)S(1)}, bf16[128,2304]{1,0:T(8,128)(2,1)}, u32[]{:S(2)}, u32[]{:S(2)}) collective-permute-start(bf16[128,2304]{1,0:T(8,128)(2,1)S(1)} %reduce-precision_convert_fusion.2), channel_id=1, source_target_pairs={{1,2},{2,1},{5,6},{6,5},{9,10},{10,9},{13,14},{14,13},{17,18},{18,... | collective-permute-start | bytes 1769480 | tf_op jit(solution)/shard_map/ppermute | solution.py:567
  630.0 28.2 %collective-permute-start.63 = (bf16[128,2304]{1,0:T(8,128)(2,1)S(1)}, bf16[128,2304]{1,0:T(8,128)(2,1)}, u32[]{:S(2)}, u32[]{:S(2)}) collective-permute-start(bf16[128,2304]{1,0:T(8,128)(2,1)S(1)} %reduce-precision_convert_fusion.1.total_ref), channel_id=1, source_target_pairs={{1,0},{2,3},{5,4},{6,7},{9,8},{10,11},{13,12},{14,15},{17,16},{18,... | collective-permute-start | bytes 1769480 | tf_op jit(solution)/shard_map/ppermute | solution.py:574
  649.9 23.5 %collective-permute-start.65 = (bf16[128,2304]{1,0:T(8,128)(2,1)S(1)}, bf16[128,2304]{1,0:T(8,128)(2,1)}, u32[]{:S(2)}, u32[]{:S(2)}) collective-permute-start(bf16[128,2304]{1,0:T(8,128)(2,1)S(1)} %reduce-precision_convert_fusion.total_ref), channel_id=1, source_target_pairs={{1,0},{2,3},{5,4},{6,7},{9,8},{10,11},{13,12},{14,15},{17,16},{18,... | collective-permute-start | bytes 1769480 | tf_op jit(solution)/shard_map/ppermute | solution.py:574
  (112 other events, 1093.8 us)
Sparse Core Ops, SparseCore 0:
  15.2 53.9 all-gather.2
  71.0 175.9 all-gather.4
  424.3 61.8 reduce-scatter.4
  489.1 124.8 reduce-scatter.2

commit v4 on v3

--- a/solution.py
+++ b/solution.py
@@ -51,10 +51,11 @@
     return lax.reduce_precision(values, 8, 7).astype(BF)
 
 
-def call(body, out_shape, grid, in_specs, out_specs, scratch=(), flops=0, moved=0):
+def call(body, out_shape, grid, in_specs, out_specs, scratch=(), flops=0, moved=0, aliases=None):
     return pl.pallas_call(
         body,
         out_shape=out_shape,
+        input_output_aliases=aliases or {},
         grid_spec=pltpu.PrefetchScalarGridSpec(
             num_scalar_prefetch=0,
             grid=grid,
@@ -351,7 +352,11 @@
     out_ref[...] = (one_ref[...] + back).astype(BF)
 
 
-def post(body, flag, pair_values, chunk_arrays, row_arrays, k, scales, outs, gain=False):
+def skip_ref(body, index, *refs):
+    body(*refs[:index], *refs[index + 1 :])
+
+
+def post(body, flag, pair_values, chunk_arrays, row_arrays, k, scales, outs, gain=False, into=None):
     rows, width = pair_values[0].shape
     steps = 2 if rows >= 128 else 1
     tile = (rows // steps, width)
@@ -371,6 +376,15 @@
     if gain:
         out_shapes.append(shape((8, width), F32))
         out_specs.append(whole((8, width)))
+    aliases = {}
+    if into is not None:
+        total, previous = into
+        out_shapes[0], out_specs[0] = shape((total, width), outs[0]), row
+        if previous is not None:
+            aliases = {len(arrays): 0}
+            body = functools.partial(skip_ref, body, len(arrays))
+            arrays.append(previous)
+            specs.append(pl.BlockSpec(memory_space=pl.ANY))
     return call(
         body,
         tuple(out_shapes),
@@ -379,6 +393,7 @@
         tuple(out_specs),
         flops=20 * rows * width,
         moved=14 * rows * width,
+        aliases=aliases,
     )(*arrays)
 
 
@@ -637,9 +652,11 @@
     qpos, kpos = query_pos[:, None], key_pos[None, :]
     cos, sin = rotation(query_pos, hd)
 
-    gains = jnp.stack([gain_attn_in, gain_attn_out, gain_ffn_in, gain_ffn_out], axis=1)
-    gains = jnp.pad(gains, ((0, 0), (0, PAD - gains.shape[1])))
-    pack_attn = jnp.concatenate([w_query, w_key, value_weight, w_out, gains], axis=1)
+    lane = lax.broadcasted_iota(jnp.int32, (gain_attn_in.shape[0], PAD), 1)
+    gains = jnp.zeros(lane.shape, BF)
+    for i, gain in enumerate((gain_attn_in, gain_attn_out, gain_ffn_in, gain_ffn_out)):
+        gains = jnp.where(lane == i, gain[:, None], gains)
+    pack_attn = pack([w_query, w_key, value_weight, w_out, gains], 1)
     pack_ffn = jnp.concatenate([w_gate, w_up, w_down], axis=1)
     full_attn = lax.all_gather(pack_attn, ("dp", "ctx"), axis=0, tiled=True)
     full_ffn = lax.all_gather(pack_ffn, ("dp", "ctx"), axis=0, tiled=True)
@@ -715,8 +732,9 @@
 
     def post_ffn(k):
         values, rows = red.take(k), [token_rows, dy_rows]
+        into = (n_seqs * seq_dev, outputs[-1] if outputs else None)
         out, grad, gain = post(
-            post_ffn_body, inner, values, [attn_outs], rows, k, scales, [BF, BF], True
+            post_ffn_body, inner, values, [attn_outs], rows, k, scales, [BF, BF], True, into
         )
         outputs.append(out), ffn_grads.append(grad), gain_fin.append(gain)
         chain.mark(grad)
@@ -731,7 +749,10 @@
 
     def post_in(k):
         values = red.take(k)
-        (grad,) = post(post_in_body, inner, values, [one_grads], [token_rows], k, scales, [BF])
+        into = (n_seqs * seq_dev, input_grads[-1] if input_grads else None)
+        (grad,) = post(
+            post_in_body, inner, values, [one_grads], [token_rows], k, scales, [BF], False, into
+        )
         input_grads.append(grad)
         chain.mark(grad)
 
@@ -876,19 +897,19 @@
     red = Reduce(chain)
     input_back(0)
     d_out = product(left_side(attn_grads), right_side([s["attended"] for s in st]))
+    finish_down()
     input_back(1)
     held["right"] = right_side([s["qkv_back"] for s in st])
 
     def finish_rest():
-        finish_down()
         finish_both()
         finish_tail()
 
     red.run(n_four, post_in, {1: tail, 4: finish_rest})
     g_gains = jnp.sum(held["g_gains"], axis=0)
     return (
-        jnp.concatenate(outputs, axis=0).reshape(tokens.shape),
-        jnp.concatenate(input_grads, axis=0).reshape(tokens.shape),
+        outputs[-1].reshape(tokens.shape),
+        input_grads[-1].reshape(tokens.shape),
         *held["g_attn"],
         held["g_gate"],
         held["g_up"],

time: 702 us -> 707 us (level)
  waiting for transfers between devices: 281 us -> 292 us
  local copies, waits for them, and re-layouts: 33.8 us -> 24.9 us
    ppermute x16, waiting for transfers between devices: 97.3 us -> 110 us  [send(): self.first[k] = lax.ppermute(piece, 'tensor', [(0, 1), (3, 2)])]
    unnamed x191 -> x177, local copies, waits for them, and re-layouts: 22.9 us -> 17.1 us
  transfers between devices with their start and end apart: 72 -> 72, of which waited for: 32 -> 32; matrix products, arithmetic and copies ran while one was open for 11% -> 10% of each run, Pallas kernels for 22% -> 22%
where the time goes in v4:
time: 707 us; the launch traced here: 697 us
  waiting for transfers between devices  292 us (41%)
  Pallas kernels  180 us (25%)
  starting transfers between devices  110 us (16%)
  other arithmetic  43.5 us (6%)
  matrix products  30 us (4%)
  local copies, waits for them, and re-layouts  24.9 us (4%)
  between operations  16 us (2%)
    ppermute x16, waiting for transfers between devices, send(): self.first[k] = lax.ppermute(piece, 'tensor', [(0, 1), (3, 2)])  110 us
    ppermute x16, waiting for transfers between devices, join(): self.third[k] = lax.ppermute(total, 'tensor', [(1, 0), (2, 3)])  79.7 us
    pallas_call x16, Pallas kernels, post(): call(body, tuple(out_shapes), (steps,), specs, tuple(out_specs), flops=20...  56.2 us
    ppermute x16, starting transfers between devices, send(): self.first[k] = lax.ppermute(piece, 'tensor', [(0, 1), (3, 2)])  49.5 us
    ppermute x3, waiting for transfers between devices, local(): others = [lax.ppermute(kv, 'ctx', flips[j]) for j in range(1, n_ctx)]  43.8 us
    all_gather x1, waiting for transfers between devices, local(): full_attn = lax.all_gather(pack_attn, ('dp', 'ctx'), axis=0, tiled=True)  42.2 us
    pallas_call x1, Pallas kernels, ffn_back(): call(functools.partial(ffn_back_body, len(ys), n_out), (shape((rows, 2 *...  37 us
    dot_general x4, matrix products, tmm(): lax.dot_general(a, b, (((0,), (0,)), ((), ())), preferred_element_type=F32)  27.6 us
  transfers between devices with their start and end apart: 72, of which 32 were waited for; matrix products, arithmetic and copies ran while one was open for 10% of the time, Pallas kernels for 22%

profile of v4, /device:TPU:0, one launch (start us, length us, event | category | flops | bytes accessed | tf_op | source)
XLA Modules:
  0.0 696.5 jit_solution(3470628742479445575)
XLA Ops:
  17.3 4.5 compare_select_fusion.1
  23.1 42.2 %all-gather.3.cloned.1.call-done.w_ref.refs_3_.refs_7_.refs_4_ = bf16[2304,1664]{1,0:T(8,128)(2,1)} async-done(((bf16[288,1664]{1,0:T(8,128)(2,1)}), bf16[2304,1664]{1,0:T(8,128)(2,1)}) %all-gather.3.cloned.1.call-update) | async-done | bytes 7667728 | tf_op jit(solution)/shard_map/all_gather | solution.py:661
  70.2 7.0 %shard_map.238.refs_0_ = bf16[512,1024]{1,0:T(8,128)(2,1)} custom-call(bf16[512,2304]{1,0:T(8,128)(2,1)} %multiply_convert_fusion.x_ref, bf16[2304,1664]{1,0:T(8,128)(2,1)} %all-gather.3.cloned.1.call-done.w_ref.refs_3_.refs_7_.refs_4_, f32[512,128]{1,0:T(8,128)} %bitcast.84, f32[512,128]{1,0:T(8,128)} %bitcast.83), custom_call_target="tpu_custom_call" | custom-call | flops 2415919104 | bytes 8126464 | tf_op jit(solution)/shard_map/pallas_call | solution.py:94
  83.3 21.8 %collective-permute-done.2.refs_7_.refs_11_ = bf16[512,512]{1,0:T(8,128)(2,1)S(1)} collective-permute-done((bf16[512,512]{1,0:T(8,128)(2,1)S(1)}, bf16[512,512]{1,0:T(8,128)(2,1)S(1)}, u32[]{:S(2)}, u32[]{:S(2)}) %collective-permute-start.2) | collective-permute-done | bytes 524320 | tf_op jit(solution)/shard_map/ppermute | solution.py:709
  105.1 11.2 %collective-permute-done.1.refs_6_.refs_10_ = bf16[512,512]{1,0:T(8,128)(2,1)S(1)} collective-permute-done((bf16[512,512]{1,0:T(8,128)(2,1)S(1)}, bf16[512,512]{1,0:T(8,128)(2,1)S(1)}, u32[]{:S(2)}, u32[]{:S(2)}) %collective-permute-start.1) | collective-permute-done | bytes 524320 | tf_op jit(solution)/shard_map/ppermute | solution.py:709
  116.3 10.9 %collective-permute-done.refs_5_.refs_9_ = bf16[512,512]{1,0:T(8,128)(2,1)S(1)} collective-permute-done((bf16[512,512]{1,0:T(8,128)(2,1)S(1)}, bf16[512,512]{1,0:T(8,128)(2,1)S(1)}, u32[]{:S(2)}, u32[]{:S(2)}) %collective-permute-start) | collective-permute-done | bytes 524320 | tf_op jit(solution)/shard_map/ppermute | solution.py:709
  128.0 4.8 shard_map.239
  137.7 4.8 shard_map.240
  145.3 4.9 collective-permute-done.3
  151.2 11.6 %collective-permute-done.5 = bf16[128,2304]{1,0:T(8,128)(2,1)S(1)} collective-permute-done((bf16[128,2304]{1,0:T(8,128)(2,1)}, bf16[128,2304]{1,0:T(8,128)(2,1)S(1)}, u32[]{:S(2)}, u32[]{:S(2)}) %collective-permute-start.5) | collective-permute-done | bytes 589856 | tf_op jit(solution)/shard_map/ppermute | solution.py:573
  165.2 21.3 %collective-permute-done.8 = bf16[128,2304]{1,0:T(8,128)(2,1)S(1)} collective-permute-done((bf16[128,2304]{1,0:T(8,128)(2,1)}, bf16[128,2304]{1,0:T(8,128)(2,1)S(1)}, u32[]{:S(2)}, u32[]{:S(2)}) %collective-permute-start.8) | collective-permute-done | bytes 589856 | tf_op jit(solution)/shard_map/ppermute | solution.py:573
  194.9 11.9 %collective-permute-done.9.third_ref = bf16[128,2304]{1,0:T(8,128)(2,1)} collective-permute-done((bf16[128,2304]{1,0:T(8,128)(2,1)S(1)}, bf16[128,2304]{1,0:T(8,128)(2,1)}, u32[]{:S(2)}, u32[]{:S(2)}) %collective-permute-start.9) | collective-permute-done | bytes 589856 | tf_op jit(solution)/shard_map/ppermute | solution.py:589
  211.2 8.1 %collective-permute-done.12.third_ref = bf16[128,2304]{1,0:T(8,128)(2,1)S(1)} collective-permute-done((bf16[128,2304]{1,0:T(8,128)(2,1)S(1)}, bf16[128,2304]{1,0:T(8,128)(2,1)S(1)}, u32[]{:S(2)}, u32[]{:S(2)}) %collective-permute-start.12) | collective-permute-done | bytes 589856 | tf_op jit(solution)/shard_map/ppermute | solution.py:589
  222.9 8.1 %collective-permute-done.14.third_ref = bf16[128,2304]{1,0:T(8,128)(2,1)S(1)} collective-permute-done((bf16[128,2304]{1,0:T(8,128)(2,1)S(1)}, bf16[128,2304]{1,0:T(8,128)(2,1)S(1)}, u32[]{:S(2)}, u32[]{:S(2)}) %collective-permute-start.14) | collective-permute-done | bytes 589856 | tf_op jit(solution)/shard_map/ppermute | solution.py:589
  243.1 25.3 %shard_map.245 = (bf16[512,2304]{1,0:T(8,128)(2,1)}, bf16[512,2304]{1,0:T(8,128)(2,1)}, bf16[512,2304]{1,0:T(8,128)(2,1)}, bf16[128,2304]{1,0:T(8,128)(2,1)}, bf...) custom-call(bf16[128,2304]{1,0:T(8,128)(2,1)} %get-tuple-element.333.refs_0_, ...), custom_call_target="tpu_custom_call" | custom-call | flops 16307453952 | bytes 43646976 | tf_op jit(solution)/shard_map/pallas_call | solution.py:440
  276.1 10.0 %collective-permute-done.17 = bf16[128,2304]{1,0:T(8,128)(2,1)S(1)} collective-permute-done((bf16[128,2304]{1,0:T(8,128)(2,1)}, bf16[128,2304]{1,0:T(8,128)(2,1)S(1)}, u32[]{:S(2)}, u32[]{:S(2)}) %collective-permute-start.17) | collective-permute-done | bytes 589856 | tf_op jit(solution)/shard_map/ppermute | solution.py:573
  288.1 23.2 %collective-permute-done.19 = bf16[128,2304]{1,0:T(8,128)(2,1)S(1)} collective-permute-done((bf16[128,2304]{1,0:T(8,128)(2,1)}, bf16[128,2304]{1,0:T(8,128)(2,1)S(1)}, u32[]{:S(2)}, u32[]{:S(2)}) %collective-permute-start.19) | collective-permute-done | bytes 589856 | tf_op jit(solution)/shard_map/ppermute | solution.py:573
  313.6 9.6 %collective-permute-done.22 = bf16[128,2304]{1,0:T(8,128)(2,1)S(1)} collective-permute-done((bf16[128,2304]{1,0:T(8,128)(2,1)}, bf16[128,2304]{1,0:T(8,128)(2,1)S(1)}, u32[]{:S(2)}, u32[]{:S(2)}) %collective-permute-start.22) | collective-permute-done | bytes 589856 | tf_op jit(solution)/shard_map/ppermute | solution.py:573
  325.6 5.0 collective-permute-done.20.third_ref
  331.4 4.0 shard_map.246
  339.3 4.0 collective-permute-done.24.refs_2_
  343.3 4.1 shard_map.247
  350.5 6.4 collective-permute-done.27.refs_2_
  360.8 8.7 %collective-permute-done.26.refs_2_ = bf16[128,2304]{1,0:T(8,128)(2,1)S(1)} collective-permute-done((bf16[128,2304]{1,0:T(8,128)(2,1)S(1)}, bf16[128,2304]{1,0:T(8,128)(2,1)S(1)}, u32[]{:S(2)}, u32[]{:S(2)}) %collective-permute-start.26) | collective-permute-done | bytes 589856 | tf_op jit(solution)/shard_map/ppermute | solution.py:589
  374.4 37.0 %shard_map.250 = (bf16[512,4608]{1,0:T(8,128)(2,1)}, bf16[128,2304]{1,0:T(8,128)(2,1)}, bf16[128,2304]{1,0:T(8,128)(2,1)}, bf16[128,2304]{1,0:T(8,128)(2,1)}, bf16[128,2304]{1,0:T(8,128)(2,1)}) custom-call(bf16[128,2304]{1,0:T(8,128)(2,1)} %get-tuple-element.343.refs_0_, bf16[128,2304]{1,0:T(8,128)(2,1)} %get-tuple-element.344.refs_1_, ...), custom_call_target="tpu_custom_call" | custom-call | flops 16307453952 | bytes 46006272 | tf_op jit(solution)/shard_map/pallas_call | solution.py:492
  415.7 8.4 %collective-permute-done.31 = bf16[128,2304]{1,0:T(8,128)(2,1)S(1)} collective-permute-done((bf16[128,2304]{1,0:T(8,128)(2,1)}, bf16[128,2304]{1,0:T(8,128)(2,1)S(1)}, u32[]{:S(2)}, u32[]{:S(2)}) %collective-permute-start.31) | collective-permute-done | bytes 589856 | tf_op jit(solution)/shard_map/ppermute | solution.py:573
  424.5 7.6 %convolution_convert_fusion.1 = bf16[1152,2304]{1,0:T(8,128)(2,1)} fusion(bf16[1024,1152]{1,0:T(8,128)(2,1)S(1)} %pad_maximum_fusion.5, bf16[1024,2304]{1,0:T(8,128)(2,1)S(1)} %pad_maximum_fusion.1), kind=kOutput, calls=%fused_computation.1 | convolution fusion | flops 5438472192 | bytes 12386304 | tf_op jit(solution)/shard_map/dot_general | solution.py:47
  434.7 4.4 collective-permute-start.33
  443.1 8.5 %collective-permute-done.33 = bf16[128,2304]{1,0:T(8,128)(2,1)S(1)} collective-permute-done((bf16[128,2304]{1,0:T(8,128)(2,1)S(1)}, bf16[128,2304]{1,0:T(8,128)(2,1)S(1)}, u32[]{:S(2)}, u32[]{:S(2)}) %collective-permute-start.33) | collective-permute-done | bytes 589856 | tf_op jit(solution)/shard_map/ppermute | solution.py:573
  452.8 13.7 %convolution_convert_fusion = bf16[1152,4608]{1,0:T(8,128)(2,1)} fusion(bf16[1024,1152]{1,0:T(8,128)(2,1)S(1)} %pad_maximum_fusion.4, bf16[1024,4608]{1,0:T(8,128)(2,1)S(1)} %pad_maximum_fusion), kind=kOutput, calls=%fused_computation | convolution fusion | flops 10876944384 | bytes 22413312 | tf_op jit(solution)/shard_map/dot_general | solution.py:47
  467.6 12.0 %collective-permute-start.28 = (bf16[128,2304]{1,0:T(8,128)(2,1)S(1)}, bf16[128,2304]{1,0:T(8,128)(2,1)S(1)}, u32[]{:S(2)}, u32[]{:S(2)}) collective-permute-start(bf16[128,2304]{1,0:T(8,128)(2,1)S(1)} %copy-done.49), channel_id=1, source_target_pairs={{0,1},{3,2},{4,5},{7,6},{8,9},{11,10},{12,13},{15,14},{16,17},{19,... | collective-permute-start | bytes 1769480 | tf_op jit(solution)/shard_map/ppermute | solution.py:573
  482.9 10.3 %collective-permute-done.28 = bf16[128,2304]{1,0:T(8,128)(2,1)S(1)} collective-permute-done((bf16[128,2304]{1,0:T(8,128)(2,1)S(1)}, bf16[128,2304]{1,0:T(8,128)(2,1)S(1)}, u32[]{:S(2)}, u32[]{:S(2)}) %collective-permute-start.28) | collective-permute-done | bytes 589856 | tf_op jit(solution)/shard_map/ppermute | solution.py:573
  498.0 4.3 shard_map.251
  511.1 4.3 shard_map.252
  515.4 7.8 %shard_map.253 = (bf16[256,512]{1,0:T(8,128)(2,1)}, f32[256,512]{1,0:T(8,128)}, f32[256,512]{1,0:T(8,128)}, f32[256,512]{1,0:T(8,128)}, f32[256,512]{1,0:T(8,128)}) custom-call(bf16[512,1024]{1,0:T(8,128)(2,1)} %shard_map.238.refs_0_, s32[256,1]{1,0:T(8,128)} %copy.53.refs_1_, s32[1,1024]{1,0:T(1,128)} %bitcast.87, f32[256,512]{1,0:T(8,128)} %get-tuple-element.369.refs_3_, ...), custom_call_target="tpu_custom_call" | custom-call | flops 1946157056 | bytes 9961472 | tf_op jit(solution)/shard_map/pallas_call | solution.py:241
  530.9 4.2 shard_map.254
  539.5 4.4 shard_map.255
  543.9 7.8 %shard_map.256 = (bf16[256,512]{1,0:T(8,128)(2,1)}, f32[256,512]{1,0:T(8,128)}, f32[256,512]{1,0:T(8,128)}, f32[256,512]{1,0:T(8,128)}, f32[256,512]{1,0:T(8,128)}) custom-call(bf16[512,1024]{1,0:T(8,128)(2,1)} %shard_map.238.refs_0_, s32[256,1]{1,0:T(8,128)} %copy.53.refs_1_, s32[1,1024]{1,0:T(1,128)} %bitcast.88, f32[256,512]{1,0:T(8,128)} %get-tuple-element.323.refs_3_, ...), custom_call_target="tpu_custom_call" | custom-call | flops 1946157056 | bytes 9961472 | tf_op jit(solution)/shard_map/pallas_call | solution.py:241
  552.6 6.3 shard_map.257
  562.1 4.4 collective-permute-start.53
  585.7 5.9 shard_map.259
  591.6 4.4 collective-permute-start.58
  603.5 4.1 collective-permute-start.52
  623.3 4.8 all-to-all-start
  639.1 12.5 %collective-permute-done.62.refs_2_ = bf16[128,2304]{1,0:T(8,128)(2,1)S(1)} collective-permute-done((bf16[128,2304]{1,0:T(8,128)(2,1)S(1)}, bf16[128,2304]{1,0:T(8,128)(2,1)S(1)}, u32[]{:S(2)}, u32[]{:S(2)}) %collective-permute-start.62) | collective-permute-done | bytes 589856 | tf_op jit(solution)/shard_map/ppermute | solution.py:589
  657.9 6.4 collective-permute-done.65.refs_2_
  668.0 4.5 shard_map.264
  677.6 5.6 all-to-all-start.1
  (403 shorter events, 213.5 us)
Async XLA Ops:
  7.2 58.1 %all-gather.3.cloned.1.call-start = ((), (), s32[]{:S(2)}) async-start(), calls=%async_computation.4 | async-start | bytes 8626176 | tf_op jit(solution)/shard_map/all_gather | solution.py:661
  11.2 231.9 %all-gather.5.cloned.1.call-start = ((), (), s32[]{:S(2)}) async-start(), calls=%async_computation.5 | async-start | bytes 35831808 | tf_op jit(solution)/shard_map/all_gather | solution.py:662
  14.4 563.3 %reduce-scatter.3.cloned.1.call-start = ((), (), s32[]{:S(2)}) async-start(), calls=%async_computation.6 | async-start | bytes 6635520 | tf_op jit(solution)/shard_map/reduce_scatter | solution.py:699
  78.3 26.7 %collective-permute-start.2 = (bf16[512,512]{1,0:T(8,128)(2,1)S(1)}, bf16[512,512]{1,0:T(8,128)(2,1)S(1)}, u32[]{:S(2)}, u32[]{:S(2)}) collective-permute-start(bf16[512,512]{1,0:T(8,128)(2,1)S(1)} %slice.95.refs_4_.refs_8_), channel_id=1, source_target_pairs={{0,12},{4,8},{8,4},{12,0},{1,13},{5,9},{9,5},{13,1},{2,14},{6,10},... | collective-permute-start | bytes 1572872 | tf_op jit(solution)/shard_map/ppermute | solution.py:709
  79.9 36.4 %collective-permute-start.1 = (bf16[512,512]{1,0:T(8,128)(2,1)S(1)}, bf16[512,512]{1,0:T(8,128)(2,1)S(1)}, u32[]{:S(2)}, u32[]{:S(2)}) collective-permute-start(bf16[512,512]{1,0:T(8,128)(2,1)S(1)} %slice.95.refs_4_.refs_8_), channel_id=1, source_target_pairs={{0,8},{4,12},{8,0},{12,4},{1,9},{5,13},{9,1},{13,5},{2,10},{6,14},... | collective-permute-start | bytes 1572872 | tf_op jit(solution)/shard_map/ppermute | solution.py:709
  81.3 45.8 %collective-permute-start = (bf16[512,512]{1,0:T(8,128)(2,1)S(1)}, bf16[512,512]{1,0:T(8,128)(2,1)S(1)}, u32[]{:S(2)}, u32[]{:S(2)}) collective-permute-start(bf16[512,512]{1,0:T(8,128)(2,1)S(1)} %slice.95.refs_4_.refs_8_), channel_id=1, source_target_pairs={{0,4},{4,0},{8,12},{12,8},{1,5},{5,1},{9,13},{13,9},{2,6},{6,2},{1... | collective-permute-start | bytes 1572872 | tf_op jit(solution)/shard_map/ppermute | solution.py:709
  132.8 17.4 %collective-permute-start.3 = (bf16[128,2304]{1,0:T(8,128)(2,1)}, bf16[128,2304]{1,0:T(8,128)(2,1)S(1)}, u32[]{:S(2)}, u32[]{:S(2)}) collective-permute-start(bf16[128,2304]{1,0:T(8,128)(2,1)} %get-tuple-element.249), channel_id=1, source_target_pairs={{0,1},{3,2},{4,5},{7,6},{8,9},{11,10},{12,13},{15,14},{16,17},{19,... | collective-permute-start | bytes 1769480 | tf_op jit(solution)/shard_map/ppermute | solution.py:573
  136.2 26.6 %collective-permute-start.5 = (bf16[128,2304]{1,0:T(8,128)(2,1)}, bf16[128,2304]{1,0:T(8,128)(2,1)S(1)}, u32[]{:S(2)}, u32[]{:S(2)}) collective-permute-start(bf16[128,2304]{1,0:T(8,128)(2,1)} %get-tuple-element.252), channel_id=1, source_target_pairs={{0,1},{3,2},{4,5},{7,6},{8,9},{11,10},{12,13},{15,14},{16,17},{19,... | collective-permute-start | bytes 1769480 | tf_op jit(solution)/shard_map/ppermute | solution.py:573
  142.5 50.0 %collective-permute-start.11 = (bf16[128,2304]{1,0:T(8,128)(2,1)}, bf16[128,2304]{1,0:T(8,128)(2,1)S(1)}, u32[]{:S(2)}, u32[]{:S(2)}) collective-permute-start(bf16[128,2304]{1,0:T(8,128)(2,1)} %get-tuple-element.264), channel_id=1, source_target_pairs={{0,1},{3,2},{4,5},{7,6},{8,9},{11,10},{12,13},{15,14},{16,17},{19,... | collective-permute-start | bytes 1769480 | tf_op jit(solution)/shard_map/ppermute | solution.py:573
  144.0 42.4 %collective-permute-start.8 = (bf16[128,2304]{1,0:T(8,128)(2,1)}, bf16[128,2304]{1,0:T(8,128)(2,1)S(1)}, u32[]{:S(2)}, u32[]{:S(2)}) collective-permute-start(bf16[128,2304]{1,0:T(8,128)(2,1)} %get-tuple-element.256), channel_id=1, source_target_pairs={{0,1},{3,2},{4,5},{7,6},{8,9},{11,10},{12,13},{15,14},{16,17},{19,... | collective-permute-start | bytes 1769480 | tf_op jit(solution)/shard_map/ppermute | solution.py:573
  163.0 24.3 %collective-permute-start.7 = (bf16[128,2304]{1,0:T(8,128)(2,1)S(1)}, bf16[128,2304]{1,0:T(8,128)(2,1)S(1)}, u32[]{:S(2)}, u32[]{:S(2)}) collective-permute-start(bf16[128,2304]{1,0:T(8,128)(2,1)S(1)} %reduce-precision_convert_fusion.30), channel_id=1, source_target_pairs={{1,2},{2,1},{5,6},{6,5},{9,10},{10,9},{13,14},{14,13},{17,18},{18,... | collective-permute-start | bytes 1769480 | tf_op jit(solution)/shard_map/ppermute | solution.py:582
  163.9 25.0 %collective-permute-start.6 = (bf16[128,2304]{1,0:T(8,128)(2,1)S(1)}, bf16[128,2304]{1,0:T(8,128)(2,1)S(1)}, u32[]{:S(2)}, u32[]{:S(2)}) collective-permute-start(bf16[128,2304]{1,0:T(8,128)(2,1)S(1)} %reduce-precision_convert_fusion.29.total_ref), channel_id=1, source_target_pairs={{1,0},{2,3},{5,4},{6,7},{9,8},{10,11},{13,12},{14,15},{17,16},{18,... | collective-permute-start | bytes 1769480 | tf_op jit(solution)/shard_map/ppermute | solution.py:589
  187.5 19.3 %collective-permute-start.9 = (bf16[128,2304]{1,0:T(8,128)(2,1)S(1)}, bf16[128,2304]{1,0:T(8,128)(2,1)}, u32[]{:S(2)}, u32[]{:S(2)}) collective-permute-start(bf16[128,2304]{1,0:T(8,128)(2,1)S(1)} %reduce-precision_convert_fusion.27.total_ref), channel_id=1, source_target_pairs={{1,0},{2,3},{5,4},{6,7},{9,8},{10,11},{13,12},{14,15},{17,16},{18,... | collective-permute-start | bytes 1769480 | tf_op jit(solution)/shard_map/ppermute | solution.py:589
  192.7 16.8 %collective-permute-start.13 = (bf16[128,2304]{1,0:T(8,128)(2,1)S(1)}, bf16[128,2304]{1,0:T(8,128)(2,1)S(1)}, u32[]{:S(2)}, u32[]{:S(2)}) collective-permute-start(bf16[128,2304]{1,0:T(8,128)(2,1)S(1)} %reduce-precision_convert_fusion.26), channel_id=1, source_target_pairs={{1,2},{2,1},{5,6},{6,5},{9,10},{10,9},{13,14},{14,13},{17,18},{18,... | collective-permute-start | bytes 1769480 | tf_op jit(solution)/shard_map/ppermute | solution.py:582
  193.6 25.7 %collective-permute-start.12 = (bf16[128,2304]{1,0:T(8,128)(2,1)S(1)}, bf16[128,2304]{1,0:T(8,128)(2,1)S(1)}, u32[]{:S(2)}, u32[]{:S(2)}) collective-permute-start(bf16[128,2304]{1,0:T(8,128)(2,1)S(1)} %reduce-precision_convert_fusion.25.total_ref), channel_id=1, source_target_pairs={{1,0},{2,3},{5,4},{6,7},{9,8},{10,11},{13,12},{14,15},{17,16},{18,... | collective-permute-start | bytes 1769480 | tf_op jit(solution)/shard_map/ppermute | solution.py:589
  209.7 21.3 %collective-permute-start.14 = (bf16[128,2304]{1,0:T(8,128)(2,1)S(1)}, bf16[128,2304]{1,0:T(8,128)(2,1)S(1)}, u32[]{:S(2)}, u32[]{:S(2)}) collective-permute-start(bf16[128,2304]{1,0:T(8,128)(2,1)S(1)} %reduce-precision_convert_fusion.24.total_ref), channel_id=1, source_target_pairs={{1,0},{2,3},{5,4},{6,7},{9,8},{10,11},{13,12},{14,15},{17,16},{18,... | collective-permute-start | bytes 1769480 | tf_op jit(solution)/shard_map/ppermute | solution.py:589
  268.5 17.5 %collective-permute-start.17 = (bf16[128,2304]{1,0:T(8,128)(2,1)}, bf16[128,2304]{1,0:T(8,128)(2,1)S(1)}, u32[]{:S(2)}, u32[]{:S(2)}) collective-permute-start(bf16[128,2304]{1,0:T(8,128)(2,1)} %get-tuple-element.286), channel_id=1, source_target_pairs={{0,1},{3,2},{4,5},{7,6},{8,9},{11,10},{12,13},{15,14},{16,17},{19,... | collective-permute-start | bytes 1769480 | tf_op jit(solution)/shard_map/ppermute | solution.py:573
  272.1 63.3 %collective-permute-start.16 = (bf16[128,2304]{1,0:T(8,128)(2,1)}, bf16[128,2304]{1,0:T(8,128)(2,1)S(1)}, u32[]{:S(2)}, u32[]{:S(2)}) collective-permute-start(bf16[128,2304]{1,0:T(8,128)(2,1)} %get-tuple-element.302), channel_id=1, source_target_pairs={{0,1},{3,2},{4,5},{7,6},{8,9},{11,10},{12,13},{15,14},{16,17},{19,... | collective-permute-start | bytes 1769480 | tf_op jit(solution)/shard_map/ppermute | solution.py:573
  273.4 37.9 %collective-permute-start.19 = (bf16[128,2304]{1,0:T(8,128)(2,1)}, bf16[128,2304]{1,0:T(8,128)(2,1)S(1)}, u32[]{:S(2)}, u32[]{:S(2)}) collective-permute-start(bf16[128,2304]{1,0:T(8,128)(2,1)} %get-tuple-element.289), channel_id=1, source_target_pairs={{0,1},{3,2},{4,5},{7,6},{8,9},{11,10},{12,13},{15,14},{16,17},{19,... | collective-permute-start | bytes 1769480 | tf_op jit(solution)/shard_map/ppermute | solution.py:573
  274.7 48.5 %collective-permute-start.22 = (bf16[128,2304]{1,0:T(8,128)(2,1)}, bf16[128,2304]{1,0:T(8,128)(2,1)S(1)}, u32[]{:S(2)}, u32[]{:S(2)}) collective-permute-start(bf16[128,2304]{1,0:T(8,128)(2,1)} %get-tuple-element.294), channel_id=1, source_target_pairs={{0,1},{3,2},{4,5},{7,6},{8,9},{11,10},{12,13},{15,14},{16,17},{19,... | collective-permute-start | bytes 1769480 | tf_op jit(solution)/shard_map/ppermute | solution.py:573
  287.3 24.9 %collective-permute-start.18 = (bf16[128,2304]{1,0:T(8,128)(2,1)S(1)}, bf16[128,2304]{1,0:T(8,128)(2,1)S(1)}, u32[]{:S(2)}, u32[]{:S(2)}) collective-permute-start(bf16[128,2304]{1,0:T(8,128)(2,1)S(1)} %reduce-precision_convert_fusion.23), channel_id=1, source_target_pairs={{1,2},{2,1},{5,6},{6,5},{9,10},{10,9},{13,14},{14,13},{17,18},{18,... | collective-permute-start | bytes 1769480 | tf_op jit(solution)/shard_map/ppermute | solution.py:582
  312.3 18.2 %collective-permute-start.20 = (bf16[128,2304]{1,0:T(8,128)(2,1)S(1)}, bf16[128,2304]{1,0:T(8,128)(2,1)S(1)}, u32[]{:S(2)}, u32[]{:S(2)}) collective-permute-start(bf16[128,2304]{1,0:T(8,128)(2,1)S(1)} %reduce-precision_convert_fusion.21.total_ref), channel_id=1, source_target_pairs={{1,0},{2,3},{5,4},{6,7},{9,8},{10,11},{13,12},{14,15},{17,16},{18,... | collective-permute-start | bytes 1769480 | tf_op jit(solution)/shard_map/ppermute | solution.py:589
  324.3 19.1 %collective-permute-start.24 = (bf16[128,2304]{1,0:T(8,128)(2,1)S(1)}, bf16[128,2304]{1,0:T(8,128)(2,1)}, u32[]{:S(2)}, u32[]{:S(2)}) collective-permute-start(bf16[128,2304]{1,0:T(8,128)(2,1)S(1)} %reduce-precision_convert_fusion.19.refs_1_), channel_id=1, source_target_pairs={{1,0},{2,3},{5,4},{6,7},{9,8},{10,11},{13,12},{14,15},{17,16},{18,... | collective-permute-start | bytes 1769480 | tf_op jit(solution)/shard_map/ppermute | solution.py:589
  338.1 18.8 %collective-permute-start.27 = (bf16[128,2304]{1,0:T(8,128)(2,1)}, bf16[128,2304]{1,0:T(8,128)(2,1)}, u32[]{:S(2)}, u32[]{:S(2)}) collective-permute-start(bf16[128,2304]{1,0:T(8,128)(2,1)} %reduce-precision_convert_fusion.17.refs_1_), channel_id=1, source_target_pairs={{1,0},{2,3},{5,4},{6,7},{9,8},{10,11},{13,12},{14,15},{17,16},{18,... | collective-permute-start | bytes 1769480 | tf_op jit(solution)/shard_map/ppermute | solution.py:589
  348.7 20.9 %collective-permute-start.26 = (bf16[128,2304]{1,0:T(8,128)(2,1)S(1)}, bf16[128,2304]{1,0:T(8,128)(2,1)S(1)}, u32[]{:S(2)}, u32[]{:S(2)}) collective-permute-start(bf16[128,2304]{1,0:T(8,128)(2,1)S(1)} %reduce-precision_convert_fusion.16.refs_1_), channel_id=1, source_target_pairs={{1,0},{2,3},{5,4},{6,7},{9,8},{10,11},{13,12},{14,15},{17,16},{18,... | collective-permute-start | bytes 1769480 | tf_op jit(solution)/shard_map/ppermute | solution.py:589
  350.4 63.3 %collective-permute-start.35 = (bf16[512,2304]{1,0:T(8,128)(2,1)S(1)}, bf16[512,2304]{1,0:T(8,128)(2,1)}, u32[]{:S(2)}, u32[]{:S(2)}) collective-permute-start(bf16[512,2304]{1,0:T(8,128)(2,1)S(1)} %copy-done.31), channel_id=1, source_target_pairs={{0,16},{16,0},{1,17},{17,1},{2,18},{18,2},{3,19},{19,3},{4,20},{20... | collective-permute-start | bytes 7077896 | tf_op jit(solution)/shard_map/ppermute | solution.py:676
  432.1 235.9 %reduce-scatter.5.cloned.1.call-start = ((), (), s32[]{:S(2)}) async-start(), calls=%async_computation.7 | async-start | bytes 13271040 | tf_op jit(solution)/shard_map/reduce_scatter | solution.py:699
  432.2 19.8 %collective-permute-start.30 = (bf16[512,4608]{1,0:T(8,128)(2,1)}, bf16[512,4608]{1,0:T(8,128)(2,1)S(1)}, u32[]{:S(2)}, u32[]{:S(2)}) collective-permute-start(bf16[512,4608]{1,0:T(8,128)(2,1)} %get-tuple-element.339), channel_id=1, source_target_pairs={{0,16},{16,0},{1,17},{17,1},{2,18},{18,2},{3,19},{19,3},{4,20},{20... | collective-permute-start | bytes 14155784 | tf_op jit(solution)/shard_map/ppermute | solution.py:676
  434.7 16.9 %collective-permute-start.33 = (bf16[128,2304]{1,0:T(8,128)(2,1)S(1)}, bf16[128,2304]{1,0:T(8,128)(2,1)S(1)}, u32[]{:S(2)}, u32[]{:S(2)}) collective-permute-start(bf16[128,2304]{1,0:T(8,128)(2,1)S(1)} %copy-done.51), channel_id=1, source_target_pairs={{0,1},{3,2},{4,5},{7,6},{8,9},{11,10},{12,13},{15,14},{16,17},{19,... | collective-permute-start | bytes 1769480 | tf_op jit(solution)/shard_map/ppermute | solution.py:573
  467.6 25.6 %collective-permute-start.28 = (bf16[128,2304]{1,0:T(8,128)(2,1)S(1)}, bf16[128,2304]{1,0:T(8,128)(2,1)S(1)}, u32[]{:S(2)}, u32[]{:S(2)}) collective-permute-start(bf16[128,2304]{1,0:T(8,128)(2,1)S(1)} %copy-done.49), channel_id=1, source_target_pairs={{0,1},{3,2},{4,5},{7,6},{8,9},{11,10},{12,13},{15,14},{16,17},{19,... | collective-permute-start | bytes 1769480 | tf_op jit(solution)/shard_map/ppermute | solution.py:573
  479.6 24.7 %collective-permute-start.37 = (bf16[128,2304]{1,0:T(8,128)(2,1)S(1)}, bf16[128,2304]{1,0:T(8,128)(2,1)S(1)}, u32[]{:S(2)}, u32[]{:S(2)}) collective-permute-start(bf16[128,2304]{1,0:T(8,128)(2,1)S(1)} %copy-done.47), channel_id=1, source_target_pairs={{0,1},{3,2},{4,5},{7,6},{8,9},{11,10},{12,13},{15,14},{16,17},{19,... | collective-permute-start | bytes 1769480 | tf_op jit(solution)/shard_map/ppermute | solution.py:573
  481.6 16.3 %collective-permute-start.38 = (bf16[128,2304]{1,0:T(8,128)(2,1)S(1)}, bf16[128,2304]{1,0:T(8,128)(2,1)}, u32[]{:S(2)}, u32[]{:S(2)}) collective-permute-start(bf16[128,2304]{1,0:T(8,128)(2,1)S(1)} %reduce-precision_convert_fusion.13.total_ref), channel_id=1, source_target_pairs={{1,0},{2,3},{5,4},{6,7},{9,8},{10,11},{13,12},{14,15},{17,16},{18,... | collective-permute-start | bytes 1769480 | tf_op jit(solution)/shard_map/ppermute | solution.py:589
  504.4 18.8 %collective-permute-start.41 = (bf16[128,2304]{1,0:T(8,128)(2,1)S(1)}, bf16[128,2304]{1,0:T(8,128)(2,1)S(1)}, u32[]{:S(2)}, u32[]{:S(2)}) collective-permute-start(bf16[128,2304]{1,0:T(8,128)(2,1)S(1)} %reduce-precision_convert_fusion.10), channel_id=1, source_target_pairs={{1,2},{2,1},{5,6},{6,5},{9,10},{10,9},{13,14},{14,13},{17,18},{18,... | collective-permute-start | bytes 1769480 | tf_op jit(solution)/shard_map/ppermute | solution.py:582
  506.4 23.7 %collective-permute-start.40 = (bf16[128,2304]{1,0:T(8,128)(2,1)S(1)}, bf16[128,2304]{1,0:T(8,128)(2,1)S(1)}, u32[]{:S(2)}, u32[]{:S(2)}) collective-permute-start(bf16[128,2304]{1,0:T(8,128)(2,1)S(1)} %reduce-precision_convert_fusion.9.total_ref), channel_id=1, source_target_pairs={{1,0},{2,3},{5,4},{6,7},{9,8},{10,11},{13,12},{14,15},{17,16},{18,... | collective-permute-start | bytes 1769480 | tf_op jit(solution)/shard_map/ppermute | solution.py:589
  526.5 25.1 %collective-permute-start.49 = (bf16[256,512]{1,0:T(8,128)(2,1)}, bf16[256,512]{1,0:T(8,128)(2,1)S(1)}, u32[]{:S(2)}, u32[]{:S(2)}) collective-permute-start(bf16[256,512]{1,0:T(8,128)(2,1)} %convert_element_type.422), channel_id=1, source_target_pairs={{0,12},{4,8},{8,4},{12,0},{1,13},{5,9},{9,5},{13,1},{2,14},{6,10},... | collective-permute-start | bytes 786440 | tf_op jit(solution)/shard_map/ppermute | solution.py:829
  528.0 23.7 %collective-permute-start.48 = (bf16[256,512]{1,0:T(8,128)(2,1)}, bf16[256,512]{1,0:T(8,128)(2,1)S(1)}, u32[]{:S(2)}, u32[]{:S(2)}) collective-permute-start(bf16[256,512]{1,0:T(8,128)(2,1)} %convert_element_type.421), channel_id=1, source_target_pairs={{0,8},{4,12},{8,0},{12,4},{1,9},{5,13},{9,1},{13,5},{2,10},{6,14},... | collective-permute-start | bytes 786440 | tf_op jit(solution)/shard_map/ppermute | solution.py:829
  529.5 22.2 %collective-permute-start.47 = (bf16[256,512]{1,0:T(8,128)(2,1)S(1)}, bf16[256,512]{1,0:T(8,128)(2,1)S(1)}, u32[]{:S(2)}, u32[]{:S(2)}) collective-permute-start(bf16[256,512]{1,0:T(8,128)(2,1)S(1)} %convert_element_type.420), channel_id=1, source_target_pairs={{0,4},{4,0},{8,12},{12,8},{1,5},{5,1},{9,13},{13,9},{2,6},{6,2},{1... | collective-permute-start | bytes 786440 | tf_op jit(solution)/shard_map/ppermute | solution.py:829
  562.1 33.8 %collective-permute-start.53 = (bf16[128,2304]{1,0:T(8,128)(2,1)S(1)}, bf16[128,2304]{1,0:T(8,128)(2,1)S(1)}, u32[]{:S(2)}, u32[]{:S(2)}) collective-permute-start(bf16[128,2304]{1,0:T(8,128)(2,1)S(1)} %copy-done.50), channel_id=1, source_target_pairs={{0,1},{3,2},{4,5},{7,6},{8,9},{11,10},{12,13},{15,14},{16,17},{19,... | collective-permute-start | bytes 1769480 | tf_op jit(solution)/shard_map/ppermute | solution.py:573
  573.0 24.9 %collective-permute-start.55 = (bf16[128,2304]{1,0:T(8,128)(2,1)S(1)}, bf16[128,2304]{1,0:T(8,128)(2,1)}, u32[]{:S(2)}, u32[]{:S(2)}) collective-permute-start(bf16[128,2304]{1,0:T(8,128)(2,1)S(1)} %copy-done.48), channel_id=1, source_target_pairs={{0,1},{3,2},{4,5},{7,6},{8,9},{11,10},{12,13},{15,14},{16,17},{19,... | collective-permute-start | bytes 1769480 | tf_op jit(solution)/shard_map/ppermute | solution.py:573
  591.6 28.9 %collective-permute-start.58 = (bf16[128,2304]{1,0:T(8,128)(2,1)}, bf16[128,2304]{1,0:T(8,128)(2,1)}, u32[]{:S(2)}, u32[]{:S(2)}) collective-permute-start(bf16[128,2304]{1,0:T(8,128)(2,1)} %get-tuple-element.442), channel_id=1, source_target_pairs={{0,1},{3,2},{4,5},{7,6},{8,9},{11,10},{12,13},{15,14},{16,17},{19,... | collective-permute-start | bytes 1769480 | tf_op jit(solution)/shard_map/ppermute | solution.py:573
  602.0 21.3 %collective-permute-start.57 = (bf16[128,2304]{1,0:T(8,128)(2,1)S(1)}, bf16[128,2304]{1,0:T(8,128)(2,1)}, u32[]{:S(2)}, u32[]{:S(2)}) collective-permute-start(bf16[128,2304]{1,0:T(8,128)(2,1)S(1)} %reduce-precision_convert_fusion.6), channel_id=1, source_target_pairs={{1,2},{2,1},{5,6},{6,5},{9,10},{10,9},{13,14},{14,13},{17,18},{18,... | collective-permute-start | bytes 1769480 | tf_op jit(solution)/shard_map/ppermute | solution.py:582
  603.5 30.2 %collective-permute-start.52 = (bf16[128,2304]{1,0:T(8,128)(2,1)}, bf16[128,2304]{1,0:T(8,128)(2,1)}, u32[]{:S(2)}, u32[]{:S(2)}) collective-permute-start(bf16[128,2304]{1,0:T(8,128)(2,1)} %get-tuple-element.449), channel_id=1, source_target_pairs={{0,1},{3,2},{4,5},{7,6},{8,9},{11,10},{12,13},{15,14},{16,17},{19,... | collective-permute-start | bytes 1769480 | tf_op jit(solution)/shard_map/ppermute | solution.py:573
  610.0 20.6 %collective-permute-start.56 = (bf16[128,2304]{1,0:T(8,128)(2,1)S(1)}, bf16[128,2304]{1,0:T(8,128)(2,1)}, u32[]{:S(2)}, u32[]{:S(2)}) collective-permute-start(bf16[128,2304]{1,0:T(8,128)(2,1)S(1)} %reduce-precision_convert_fusion.5.total_ref), channel_id=1, source_target_pairs={{1,0},{2,3},{5,4},{6,7},{9,8},{10,11},{13,12},{14,15},{17,16},{18,... | collective-permute-start | bytes 1769480 | tf_op jit(solution)/shard_map/ppermute | solution.py:589
  623.3 49.2 %all-to-all-start = ((bf16[4,288,1664]{2,1,0:T(8,128)(2,1)}), bf16[4,288,1664]{2,1,0:T(8,128)(2,1)}, u32[]{:S(2)}, u32[]{:S(2)}) async-start(bf16[4,288,1664]{2,1,0:T(8,128)(2,1)} %bitcast.78), calls=%async_computation.1 | async-start | bytes 7667712 | tf_op jit(solution)/shard_map/all_to_all | solution.py:690
  629.3 22.3 %collective-permute-start.62 = (bf16[128,2304]{1,0:T(8,128)(2,1)S(1)}, bf16[128,2304]{1,0:T(8,128)(2,1)S(1)}, u32[]{:S(2)}, u32[]{:S(2)}) collective-permute-start(bf16[128,2304]{1,0:T(8,128)(2,1)S(1)} %reduce-precision_convert_fusion.3.refs_1_), channel_id=1, source_target_pairs={{1,0},{2,3},{5,4},{6,7},{9,8},{10,11},{13,12},{14,15},{17,16},{18,... | collective-permute-start | bytes 1769480 | tf_op jit(solution)/shard_map/ppermute | solution.py:589
  635.0 20.3 %collective-permute-start.61 = (bf16[128,2304]{1,0:T(8,128)(2,1)S(1)}, bf16[128,2304]{1,0:T(8,128)(2,1)}, u32[]{:S(2)}, u32[]{:S(2)}) collective-permute-start(bf16[128,2304]{1,0:T(8,128)(2,1)S(1)} %reduce-precision_convert_fusion.2), channel_id=1, source_target_pairs={{1,2},{2,1},{5,6},{6,5},{9,10},{10,9},{13,14},{14,13},{17,18},{18,... | collective-permute-start | bytes 1769480 | tf_op jit(solution)/shard_map/ppermute | solution.py:582
  637.8 26.5 %collective-permute-start.65 = (bf16[128,2304]{1,0:T(8,128)(2,1)S(1)}, bf16[128,2304]{1,0:T(8,128)(2,1)S(1)}, u32[]{:S(2)}, u32[]{:S(2)}) collective-permute-start(bf16[128,2304]{1,0:T(8,128)(2,1)S(1)} %reduce-precision_convert_fusion.1.refs_1_), channel_id=1, source_target_pairs={{1,0},{2,3},{5,4},{6,7},{9,8},{10,11},{13,12},{14,15},{17,16},{18,... | collective-permute-start | bytes 1769480 | tf_op jit(solution)/shard_map/ppermute | solution.py:589
  656.6 26.7 %collective-permute-start.64 = (bf16[128,2304]{1,0:T(8,128)(2,1)S(1)}, bf16[128,2304]{1,0:T(8,128)(2,1)S(1)}, u32[]{:S(2)}, u32[]{:S(2)}) collective-permute-start(bf16[128,2304]{1,0:T(8,128)(2,1)S(1)} %reduce-precision_convert_fusion.refs_1_), channel_id=1, source_target_pairs={{1,0},{2,3},{5,4},{6,7},{9,8},{10,11},{13,12},{14,15},{17,16},{18,... | collective-permute-start | bytes 1769480 | tf_op jit(solution)/shard_map/ppermute | solution.py:589
  (107 other events, 1085.6 us)
Sparse Core Ops, SparseCore 0:
  11.3 53.9 all-gather.2
  67.2 175.9 all-gather.4
  432.2 61.8 reduce-scatter.2
  497.0 125.3 reduce-scatter.4

commit v5 on v4

--- a/solution.py
+++ b/solution.py
@@ -732,9 +732,8 @@
 
     def post_ffn(k):
         values, rows = red.take(k), [token_rows, dy_rows]
-        into = (n_seqs * seq_dev, outputs[-1] if outputs else None)
         out, grad, gain = post(
-            post_ffn_body, inner, values, [attn_outs], rows, k, scales, [BF, BF], True, into
+            post_ffn_body, inner, values, [attn_outs], rows, k, scales, [BF, BF], True
         )
         outputs.append(out), ffn_grads.append(grad), gain_fin.append(gain)
         chain.mark(grad)
@@ -908,7 +907,7 @@
     red.run(n_four, post_in, {1: tail, 4: finish_rest})
     g_gains = jnp.sum(held["g_gains"], axis=0)
     return (
-        outputs[-1].reshape(tokens.shape),
+        jnp.concatenate(outputs, axis=0).reshape(tokens.shape),
         input_grads[-1].reshape(tokens.shape),
         *held["g_attn"],
         held["g_gate"],

time: 707 us -> 697 us (0.986)
  waiting for transfers between devices: 292 us -> 278 us
    ppermute x16, waiting for transfers between devices: 110 us -> 97.3 us  [send(): self.first[k] = lax.ppermute(piece, 'tensor', [(0, 1), (3, 2)])]
    unnamed x177 -> x191, local copies, waits for them, and re-layouts: 17.1 us -> 20 us
  transfers between devices with their start and end apart: 72 -> 72, of which waited for: 32 -> 33; matrix products, arithmetic and copies ran while one was open for 10% -> 10% of each run, Pallas kernels for 22% -> 22%
where the time goes in v5:
time: 697 us; the launch traced here: 686 us
  waiting for transfers between devices  278 us (40%)
  Pallas kernels  180 us (26%)
  starting transfers between devices  109 us (16%)
  other arithmetic  43.9 us (6%)
  matrix products  29.9 us (4%)
  local copies, waits for them, and re-layouts  27.9 us (4%)
  between operations  16.1 us (2%)
    ppermute x16, waiting for transfers between devices, send(): self.first[k] = lax.ppermute(piece, 'tensor', [(0, 1), (3, 2)])  97.3 us
    ppermute x16, waiting for transfers between devices, join(): self.third[k] = lax.ppermute(total, 'tensor', [(1, 0), (2, 3)])  80.4 us
    pallas_call x16, Pallas kernels, post(): call(body, tuple(out_shapes), (steps,), specs, tuple(out_specs), flops=20...  56.1 us
    ppermute x16, starting transfers between devices, send(): self.first[k] = lax.ppermute(piece, 'tensor', [(0, 1), (3, 2)])  49.6 us
    ppermute x3, waiting for transfers between devices, local(): others = [lax.ppermute(kv, 'ctx', flips[j]) for j in range(1, n_ctx)]  43.8 us
    all_gather x1, waiting for transfers between devices, local(): full_attn = lax.all_gather(pack_attn, ('dp', 'ctx'), axis=0, tiled=True)  42.2 us
    pallas_call x1, Pallas kernels, ffn_back(): call(functools.partial(ffn_back_body, len(ys), n_out), (shape((rows, 2 *...  37.1 us
    dot_general x4, matrix products, tmm(): lax.dot_general(a, b, (((0,), (0,)), ((), ())), preferred_element_type=F32)  27.6 us
  transfers between devices with their start and end apart: 72, of which 33 were waited for; matrix products, arithmetic and copies ran while one was open for 10% of the time, Pallas kernels for 22%

profile of v5, /device:TPU:0, one launch (start us, length us, event | category | flops | bytes accessed | tf_op | source)
XLA Modules:
  0.0 685.8 jit_solution(6332508586520366071)
XLA Ops:
  17.3 4.5 compare_select_fusion.1
  23.1 42.2 %all-gather.3.cloned.1.call-done.w_ref.refs_3_.refs_7_.refs_4_ = bf16[2304,1664]{1,0:T(8,128)(2,1)} async-done(((bf16[288,1664]{1,0:T(8,128)(2,1)}), bf16[2304,1664]{1,0:T(8,128)(2,1)}) %all-gather.3.cloned.1.call-update) | async-done | bytes 7667728 | tf_op jit(solution)/shard_map/all_gather | solution.py:661
  70.2 7.0 %shard_map.238.refs_0_ = bf16[512,1024]{1,0:T(8,128)(2,1)} custom-call(bf16[512,2304]{1,0:T(8,128)(2,1)} %multiply_convert_fusion.x_ref, bf16[2304,1664]{1,0:T(8,128)(2,1)} %all-gather.3.cloned.1.call-done.w_ref.refs_3_.refs_7_.refs_4_, f32[512,128]{1,0:T(8,128)} %bitcast.84, f32[512,128]{1,0:T(8,128)} %bitcast.83), custom_call_target="tpu_custom_call" | custom-call | flops 2415919104 | bytes 8126464 | tf_op jit(solution)/shard_map/pallas_call | solution.py:94
  83.3 21.7 %collective-permute-done.2.refs_7_.refs_11_ = bf16[512,512]{1,0:T(8,128)(2,1)S(1)} collective-permute-done((bf16[512,512]{1,0:T(8,128)(2,1)S(1)}, bf16[512,512]{1,0:T(8,128)(2,1)S(1)}, u32[]{:S(2)}, u32[]{:S(2)}) %collective-permute-start.2) | collective-permute-done | bytes 524320 | tf_op jit(solution)/shard_map/ppermute | solution.py:709
  105.0 11.2 %collective-permute-done.1.refs_6_.refs_10_ = bf16[512,512]{1,0:T(8,128)(2,1)S(1)} collective-permute-done((bf16[512,512]{1,0:T(8,128)(2,1)S(1)}, bf16[512,512]{1,0:T(8,128)(2,1)S(1)}, u32[]{:S(2)}, u32[]{:S(2)}) %collective-permute-start.1) | collective-permute-done | bytes 524320 | tf_op jit(solution)/shard_map/ppermute | solution.py:709
  116.3 10.9 %collective-permute-done.refs_5_.refs_9_ = bf16[512,512]{1,0:T(8,128)(2,1)S(1)} collective-permute-done((bf16[512,512]{1,0:T(8,128)(2,1)S(1)}, bf16[512,512]{1,0:T(8,128)(2,1)S(1)}, u32[]{:S(2)}, u32[]{:S(2)}) %collective-permute-start) | collective-permute-done | bytes 524320 | tf_op jit(solution)/shard_map/ppermute | solution.py:709
  127.9 4.8 shard_map.239
  137.7 4.8 shard_map.240
  145.3 4.9 collective-permute-done.3
  151.2 11.6 %collective-permute-done.5 = bf16[128,2304]{1,0:T(8,128)(2,1)S(1)} collective-permute-done((bf16[128,2304]{1,0:T(8,128)(2,1)}, bf16[128,2304]{1,0:T(8,128)(2,1)S(1)}, u32[]{:S(2)}, u32[]{:S(2)}) %collective-permute-start.5) | collective-permute-done | bytes 589856 | tf_op jit(solution)/shard_map/ppermute | solution.py:573
  165.1 21.3 %collective-permute-done.8 = bf16[128,2304]{1,0:T(8,128)(2,1)S(1)} collective-permute-done((bf16[128,2304]{1,0:T(8,128)(2,1)}, bf16[128,2304]{1,0:T(8,128)(2,1)S(1)}, u32[]{:S(2)}, u32[]{:S(2)}) %collective-permute-start.8) | collective-permute-done | bytes 589856 | tf_op jit(solution)/shard_map/ppermute | solution.py:573
  194.9 11.9 %collective-permute-done.9.third_ref = bf16[128,2304]{1,0:T(8,128)(2,1)} collective-permute-done((bf16[128,2304]{1,0:T(8,128)(2,1)S(1)}, bf16[128,2304]{1,0:T(8,128)(2,1)}, u32[]{:S(2)}, u32[]{:S(2)}) %collective-permute-start.9) | collective-permute-done | bytes 589856 | tf_op jit(solution)/shard_map/ppermute | solution.py:589
  211.2 8.1 %collective-permute-done.12.third_ref = bf16[128,2304]{1,0:T(8,128)(2,1)S(1)} collective-permute-done((bf16[128,2304]{1,0:T(8,128)(2,1)S(1)}, bf16[128,2304]{1,0:T(8,128)(2,1)S(1)}, u32[]{:S(2)}, u32[]{:S(2)}) %collective-permute-start.12) | collective-permute-done | bytes 589856 | tf_op jit(solution)/shard_map/ppermute | solution.py:589
  222.9 8.1 %collective-permute-done.14.third_ref = bf16[128,2304]{1,0:T(8,128)(2,1)S(1)} collective-permute-done((bf16[128,2304]{1,0:T(8,128)(2,1)S(1)}, bf16[128,2304]{1,0:T(8,128)(2,1)S(1)}, u32[]{:S(2)}, u32[]{:S(2)}) %collective-permute-start.14) | collective-permute-done | bytes 589856 | tf_op jit(solution)/shard_map/ppermute | solution.py:589
  243.1 25.4 %shard_map.245 = (bf16[512,2304]{1,0:T(8,128)(2,1)}, bf16[512,2304]{1,0:T(8,128)(2,1)}, bf16[512,2304]{1,0:T(8,128)(2,1)}, bf16[128,2304]{1,0:T(8,128)(2,1)}, bf...) custom-call(bf16[128,2304]{1,0:T(8,128)(2,1)} %get-tuple-element.333.refs_0_, ...), custom_call_target="tpu_custom_call" | custom-call | flops 16307453952 | bytes 43646976 | tf_op jit(solution)/shard_map/pallas_call | solution.py:440
  276.1 10.0 %collective-permute-done.16 = bf16[128,2304]{1,0:T(8,128)(2,1)S(1)} collective-permute-done((bf16[128,2304]{1,0:T(8,128)(2,1)}, bf16[128,2304]{1,0:T(8,128)(2,1)S(1)}, u32[]{:S(2)}, u32[]{:S(2)}) %collective-permute-start.16) | collective-permute-done | bytes 589856 | tf_op jit(solution)/shard_map/ppermute | solution.py:573
  288.1 10.6 %collective-permute-done.18 = bf16[128,2304]{1,0:T(8,128)(2,1)S(1)} collective-permute-done((bf16[128,2304]{1,0:T(8,128)(2,1)}, bf16[128,2304]{1,0:T(8,128)(2,1)S(1)}, u32[]{:S(2)}, u32[]{:S(2)}) %collective-permute-start.18) | collective-permute-done | bytes 589856 | tf_op jit(solution)/shard_map/ppermute | solution.py:573
  301.0 10.3 %collective-permute-done.21 = bf16[128,2304]{1,0:T(8,128)(2,1)S(1)} collective-permute-done((bf16[128,2304]{1,0:T(8,128)(2,1)}, bf16[128,2304]{1,0:T(8,128)(2,1)S(1)}, u32[]{:S(2)}, u32[]{:S(2)}) %collective-permute-start.21) | collective-permute-done | bytes 589856 | tf_op jit(solution)/shard_map/ppermute | solution.py:573
  313.7 4.7 collective-permute-done.19.third_ref
  325.6 6.5 collective-permute-done.22.third_ref
  332.9 4.0 shard_map.247
  338.9 5.8 collective-permute-done.25.third_ref
  349.5 7.8 %collective-permute-done.27.third_ref = bf16[128,2304]{1,0:T(8,128)(2,1)S(1)} collective-permute-done((bf16[128,2304]{1,0:T(8,128)(2,1)S(1)}, bf16[128,2304]{1,0:T(8,128)(2,1)S(1)}, u32[]{:S(2)}, u32[]{:S(2)}) %collective-permute-start.27) | collective-permute-done | bytes 589856 | tf_op jit(solution)/shard_map/ppermute | solution.py:589
  358.2 4.0 shard_map.249
  362.2 37.1 %shard_map.250 = (bf16[512,4608]{1,0:T(8,128)(2,1)}, bf16[128,2304]{1,0:T(8,128)(2,1)}, bf16[128,2304]{1,0:T(8,128)(2,1)}, bf16[128,2304]{1,0:T(8,128)(2,1)}, bf16[128,2304]{1,0:T(8,128)(2,1)}) custom-call(bf16[128,2304]{1,0:T(8,128)(2,1)} %get-tuple-element.343.refs_0_, bf16[128,2304]{1,0:T(8,128)(2,1)} %get-tuple-element.344.refs_1_, ...), custom_call_target="tpu_custom_call" | custom-call | flops 16307453952 | bytes 46006272 | tf_op jit(solution)/shard_map/pallas_call | solution.py:492
  404.8 7.6 %collective-permute-done.31 = bf16[128,2304]{1,0:T(8,128)(2,1)S(1)} collective-permute-done((bf16[128,2304]{1,0:T(8,128)(2,1)}, bf16[128,2304]{1,0:T(8,128)(2,1)S(1)}, u32[]{:S(2)}, u32[]{:S(2)}) %collective-permute-start.31) | collective-permute-done | bytes 589856 | tf_op jit(solution)/shard_map/ppermute | solution.py:573
  412.8 7.5 %convolution_convert_fusion.1 = bf16[1152,2304]{1,0:T(8,128)(2,1)} fusion(bf16[1024,1152]{1,0:T(8,128)(2,1)S(1)} %pad_maximum_fusion.6, bf16[1024,2304]{1,0:T(8,128)(2,1)S(1)} %pad_maximum_fusion.1), kind=kOutput, calls=%fused_computation.1 | convolution fusion | flops 5438472192 | bytes 12386304 | tf_op jit(solution)/shard_map/dot_general | solution.py:47
  423.1 4.4 collective-permute-start.33
  431.4 8.5 %collective-permute-done.33 = bf16[128,2304]{1,0:T(8,128)(2,1)S(1)} collective-permute-done((bf16[128,2304]{1,0:T(8,128)(2,1)S(1)}, bf16[128,2304]{1,0:T(8,128)(2,1)S(1)}, u32[]{:S(2)}, u32[]{:S(2)}) %collective-permute-start.33) | collective-permute-done | bytes 589856 | tf_op jit(solution)/shard_map/ppermute | solution.py:573
  441.1 13.7 %convolution_convert_fusion = bf16[1152,4608]{1,0:T(8,128)(2,1)} fusion(bf16[1024,1152]{1,0:T(8,128)(2,1)S(1)} %pad_maximum_fusion.5, bf16[1024,4608]{1,0:T(8,128)(2,1)S(1)} %pad_maximum_fusion), kind=kOutput, calls=%fused_computation | convolution fusion | flops 10876944384 | bytes 22413312 | tf_op jit(solution)/shard_map/dot_general | solution.py:47
  455.9 12.0 %collective-permute-start.28 = (bf16[128,2304]{1,0:T(8,128)(2,1)S(1)}, bf16[128,2304]{1,0:T(8,128)(2,1)S(1)}, u32[]{:S(2)}, u32[]{:S(2)}) collective-permute-start(bf16[128,2304]{1,0:T(8,128)(2,1)S(1)} %copy-done.54), channel_id=1, source_target_pairs={{0,1},{3,2},{4,5},{7,6},{8,9},{11,10},{12,13},{15,14},{16,17},{19,... | collective-permute-start | bytes 1769480 | tf_op jit(solution)/shard_map/ppermute | solution.py:573
  471.3 10.3 %collective-permute-done.28 = bf16[128,2304]{1,0:T(8,128)(2,1)S(1)} collective-permute-done((bf16[128,2304]{1,0:T(8,128)(2,1)S(1)}, bf16[128,2304]{1,0:T(8,128)(2,1)S(1)}, u32[]{:S(2)}, u32[]{:S(2)}) %collective-permute-start.28) | collective-permute-done | bytes 589856 | tf_op jit(solution)/shard_map/ppermute | solution.py:573
  486.3 4.2 shard_map.251
  499.4 4.4 shard_map.252
  503.8 7.8 %shard_map.253 = (bf16[256,512]{1,0:T(8,128)(2,1)}, f32[256,512]{1,0:T(8,128)}, f32[256,512]{1,0:T(8,128)}, f32[256,512]{1,0:T(8,128)}, f32[256,512]{1,0:T(8,128)}) custom-call(bf16[512,1024]{1,0:T(8,128)(2,1)} %shard_map.238.refs_0_, s32[256,1]{1,0:T(8,128)} %copy.50.refs_1_, s32[1,1024]{1,0:T(1,128)} %bitcast.87, f32[256,512]{1,0:T(8,128)} %get-tuple-element.369.refs_3_, ...), custom_call_target="tpu_custom_call" | custom-call | flops 1946157056 | bytes 9961472 | tf_op jit(solution)/shard_map/pallas_call | solution.py:241
  519.3 4.2 shard_map.254
  527.9 4.3 shard_map.255
  532.2 7.8 %shard_map.256 = (bf16[256,512]{1,0:T(8,128)(2,1)}, f32[256,512]{1,0:T(8,128)}, f32[256,512]{1,0:T(8,128)}, f32[256,512]{1,0:T(8,128)}, f32[256,512]{1,0:T(8,128)}) custom-call(bf16[512,1024]{1,0:T(8,128)(2,1)} %shard_map.238.refs_0_, s32[256,1]{1,0:T(8,128)} %copy.50.refs_1_, s32[1,1024]{1,0:T(1,128)} %bitcast.88, f32[256,512]{1,0:T(8,128)} %get-tuple-element.323.refs_3_, ...), custom_call_target="tpu_custom_call" | custom-call | flops 1946157056 | bytes 9961472 | tf_op jit(solution)/shard_map/pallas_call | solution.py:241
  540.9 6.3 shard_map.257
  550.4 4.4 collective-permute-start.53
  574.1 5.9 shard_map.259
  579.9 4.3 collective-permute-start.58
  591.8 4.1 collective-permute-start.52
  611.6 4.8 all-to-all-start
  627.4 12.6 %collective-permute-done.62.refs_2_ = bf16[128,2304]{1,0:T(8,128)(2,1)S(1)} collective-permute-done((bf16[128,2304]{1,0:T(8,128)(2,1)S(1)}, bf16[128,2304]{1,0:T(8,128)(2,1)S(1)}, u32[]{:S(2)}, u32[]{:S(2)}) %collective-permute-start.62) | collective-permute-done | bytes 589856 | tf_op jit(solution)/shard_map/ppermute | solution.py:589
  646.2 6.4 collective-permute-done.65.refs_2_
  656.4 4.5 shard_map.264
  666.1 5.5 all-to-all-start.1
  (418 shorter events, 214.9 us)
Async XLA Ops:
  7.2 58.1 %all-gather.3.cloned.1.call-start = ((), (), s32[]{:S(2)}) async-start(), calls=%async_computation.4 | async-start | bytes 8626176 | tf_op jit(solution)/shard_map/all_gather | solution.py:661
  11.2 231.9 %all-gather.5.cloned.1.call-start = ((), (), s32[]{:S(2)}) async-start(), calls=%async_computation.5 | async-start | bytes 35831808 | tf_op jit(solution)/shard_map/all_gather | solution.py:662
  14.4 551.6 %reduce-scatter.3.cloned.1.call-start = ((), (), s32[]{:S(2)}) async-start(), calls=%async_computation.6 | async-start | bytes 6635520 | tf_op jit(solution)/shard_map/reduce_scatter | solution.py:699
  78.3 26.7 %collective-permute-start.2 = (bf16[512,512]{1,0:T(8,128)(2,1)S(1)}, bf16[512,512]{1,0:T(8,128)(2,1)S(1)}, u32[]{:S(2)}, u32[]{:S(2)}) collective-permute-start(bf16[512,512]{1,0:T(8,128)(2,1)S(1)} %slice.95.refs_4_.refs_8_), channel_id=1, source_target_pairs={{0,12},{4,8},{8,4},{12,0},{1,13},{5,9},{9,5},{13,1},{2,14},{6,10},... | collective-permute-start | bytes 1572872 | tf_op jit(solution)/shard_map/ppermute | solution.py:709
  79.9 36.4 %collective-permute-start.1 = (bf16[512,512]{1,0:T(8,128)(2,1)S(1)}, bf16[512,512]{1,0:T(8,128)(2,1)S(1)}, u32[]{:S(2)}, u32[]{:S(2)}) collective-permute-start(bf16[512,512]{1,0:T(8,128)(2,1)S(1)} %slice.95.refs_4_.refs_8_), channel_id=1, source_target_pairs={{0,8},{4,12},{8,0},{12,4},{1,9},{5,13},{9,1},{13,5},{2,10},{6,14},... | collective-permute-start | bytes 1572872 | tf_op jit(solution)/shard_map/ppermute | solution.py:709
  81.3 45.8 %collective-permute-start = (bf16[512,512]{1,0:T(8,128)(2,1)S(1)}, bf16[512,512]{1,0:T(8,128)(2,1)S(1)}, u32[]{:S(2)}, u32[]{:S(2)}) collective-permute-start(bf16[512,512]{1,0:T(8,128)(2,1)S(1)} %slice.95.refs_4_.refs_8_), channel_id=1, source_target_pairs={{0,4},{4,0},{8,12},{12,8},{1,5},{5,1},{9,13},{13,9},{2,6},{6,2},{1... | collective-permute-start | bytes 1572872 | tf_op jit(solution)/shard_map/ppermute | solution.py:709
  132.8 17.4 %collective-permute-start.3 = (bf16[128,2304]{1,0:T(8,128)(2,1)}, bf16[128,2304]{1,0:T(8,128)(2,1)S(1)}, u32[]{:S(2)}, u32[]{:S(2)}) collective-permute-start(bf16[128,2304]{1,0:T(8,128)(2,1)} %get-tuple-element.249), channel_id=1, source_target_pairs={{0,1},{3,2},{4,5},{7,6},{8,9},{11,10},{12,13},{15,14},{16,17},{19,... | collective-permute-start | bytes 1769480 | tf_op jit(solution)/shard_map/ppermute | solution.py:573
  136.2 26.6 %collective-permute-start.5 = (bf16[128,2304]{1,0:T(8,128)(2,1)}, bf16[128,2304]{1,0:T(8,128)(2,1)S(1)}, u32[]{:S(2)}, u32[]{:S(2)}) collective-permute-start(bf16[128,2304]{1,0:T(8,128)(2,1)} %get-tuple-element.252), channel_id=1, source_target_pairs={{0,1},{3,2},{4,5},{7,6},{8,9},{11,10},{12,13},{15,14},{16,17},{19,... | collective-permute-start | bytes 1769480 | tf_op jit(solution)/shard_map/ppermute | solution.py:573
  142.5 50.0 %collective-permute-start.11 = (bf16[128,2304]{1,0:T(8,128)(2,1)}, bf16[128,2304]{1,0:T(8,128)(2,1)S(1)}, u32[]{:S(2)}, u32[]{:S(2)}) collective-permute-start(bf16[128,2304]{1,0:T(8,128)(2,1)} %get-tuple-element.264), channel_id=1, source_target_pairs={{0,1},{3,2},{4,5},{7,6},{8,9},{11,10},{12,13},{15,14},{16,17},{19,... | collective-permute-start | bytes 1769480 | tf_op jit(solution)/shard_map/ppermute | solution.py:573
  144.0 42.4 %collective-permute-start.8 = (bf16[128,2304]{1,0:T(8,128)(2,1)}, bf16[128,2304]{1,0:T(8,128)(2,1)S(1)}, u32[]{:S(2)}, u32[]{:S(2)}) collective-permute-start(bf16[128,2304]{1,0:T(8,128)(2,1)} %get-tuple-element.256), channel_id=1, source_target_pairs={{0,1},{3,2},{4,5},{7,6},{8,9},{11,10},{12,13},{15,14},{16,17},{19,... | collective-permute-start | bytes 1769480 | tf_op jit(solution)/shard_map/ppermute | solution.py:573
  163.0 24.3 %collective-permute-start.7 = (bf16[128,2304]{1,0:T(8,128)(2,1)S(1)}, bf16[128,2304]{1,0:T(8,128)(2,1)S(1)}, u32[]{:S(2)}, u32[]{:S(2)}) collective-permute-start(bf16[128,2304]{1,0:T(8,128)(2,1)S(1)} %reduce-precision_convert_fusion.30), channel_id=1, source_target_pairs={{1,2},{2,1},{5,6},{6,5},{9,10},{10,9},{13,14},{14,13},{17,18},{18,... | collective-permute-start | bytes 1769480 | tf_op jit(solution)/shard_map/ppermute | solution.py:582
  163.8 25.0 %collective-permute-start.6 = (bf16[128,2304]{1,0:T(8,128)(2,1)S(1)}, bf16[128,2304]{1,0:T(8,128)(2,1)S(1)}, u32[]{:S(2)}, u32[]{:S(2)}) collective-permute-start(bf16[128,2304]{1,0:T(8,128)(2,1)S(1)} %reduce-precision_convert_fusion.29.total_ref), channel_id=1, source_target_pairs={{1,0},{2,3},{5,4},{6,7},{9,8},{10,11},{13,12},{14,15},{17,16},{18,... | collective-permute-start | bytes 1769480 | tf_op jit(solution)/shard_map/ppermute | solution.py:589
  187.4 19.3 %collective-permute-start.9 = (bf16[128,2304]{1,0:T(8,128)(2,1)S(1)}, bf16[128,2304]{1,0:T(8,128)(2,1)}, u32[]{:S(2)}, u32[]{:S(2)}) collective-permute-start(bf16[128,2304]{1,0:T(8,128)(2,1)S(1)} %reduce-precision_convert_fusion.27.total_ref), channel_id=1, source_target_pairs={{1,0},{2,3},{5,4},{6,7},{9,8},{10,11},{13,12},{14,15},{17,16},{18,... | collective-permute-start | bytes 1769480 | tf_op jit(solution)/shard_map/ppermute | solution.py:589
  192.7 16.8 %collective-permute-start.13 = (bf16[128,2304]{1,0:T(8,128)(2,1)S(1)}, bf16[128,2304]{1,0:T(8,128)(2,1)S(1)}, u32[]{:S(2)}, u32[]{:S(2)}) collective-permute-start(bf16[128,2304]{1,0:T(8,128)(2,1)S(1)} %reduce-precision_convert_fusion.26), channel_id=1, source_target_pairs={{1,2},{2,1},{5,6},{6,5},{9,10},{10,9},{13,14},{14,13},{17,18},{18,... | collective-permute-start | bytes 1769480 | tf_op jit(solution)/shard_map/ppermute | solution.py:582
  193.6 25.7 %collective-permute-start.12 = (bf16[128,2304]{1,0:T(8,128)(2,1)S(1)}, bf16[128,2304]{1,0:T(8,128)(2,1)S(1)}, u32[]{:S(2)}, u32[]{:S(2)}) collective-permute-start(bf16[128,2304]{1,0:T(8,128)(2,1)S(1)} %reduce-precision_convert_fusion.25.total_ref), channel_id=1, source_target_pairs={{1,0},{2,3},{5,4},{6,7},{9,8},{10,11},{13,12},{14,15},{17,16},{18,... | collective-permute-start | bytes 1769480 | tf_op jit(solution)/shard_map/ppermute | solution.py:589
  209.7 21.3 %collective-permute-start.14 = (bf16[128,2304]{1,0:T(8,128)(2,1)S(1)}, bf16[128,2304]{1,0:T(8,128)(2,1)S(1)}, u32[]{:S(2)}, u32[]{:S(2)}) collective-permute-start(bf16[128,2304]{1,0:T(8,128)(2,1)S(1)} %reduce-precision_convert_fusion.24.total_ref), channel_id=1, source_target_pairs={{1,0},{2,3},{5,4},{6,7},{9,8},{10,11},{13,12},{14,15},{17,16},{18,... | collective-permute-start | bytes 1769480 | tf_op jit(solution)/shard_map/ppermute | solution.py:589
  268.5 17.5 %collective-permute-start.16 = (bf16[128,2304]{1,0:T(8,128)(2,1)}, bf16[128,2304]{1,0:T(8,128)(2,1)S(1)}, u32[]{:S(2)}, u32[]{:S(2)}) collective-permute-start(bf16[128,2304]{1,0:T(8,128)(2,1)} %get-tuple-element.285), channel_id=1, source_target_pairs={{0,1},{3,2},{4,5},{7,6},{8,9},{11,10},{12,13},{15,14},{16,17},{19,... | collective-permute-start | bytes 1769480 | tf_op jit(solution)/shard_map/ppermute | solution.py:573
  272.1 26.6 %collective-permute-start.18 = (bf16[128,2304]{1,0:T(8,128)(2,1)}, bf16[128,2304]{1,0:T(8,128)(2,1)S(1)}, u32[]{:S(2)}, u32[]{:S(2)}) collective-permute-start(bf16[128,2304]{1,0:T(8,128)(2,1)} %get-tuple-element.288), channel_id=1, source_target_pairs={{0,1},{3,2},{4,5},{7,6},{8,9},{11,10},{12,13},{15,14},{16,17},{19,... | collective-permute-start | bytes 1769480 | tf_op jit(solution)/shard_map/ppermute | solution.py:573
  273.4 37.9 %collective-permute-start.21 = (bf16[128,2304]{1,0:T(8,128)(2,1)}, bf16[128,2304]{1,0:T(8,128)(2,1)S(1)}, u32[]{:S(2)}, u32[]{:S(2)}) collective-permute-start(bf16[128,2304]{1,0:T(8,128)(2,1)} %get-tuple-element.293), channel_id=1, source_target_pairs={{0,1},{3,2},{4,5},{7,6},{8,9},{11,10},{12,13},{15,14},{16,17},{19,... | collective-permute-start | bytes 1769480 | tf_op jit(solution)/shard_map/ppermute | solution.py:573
  274.7 48.5 %collective-permute-start.24 = (bf16[128,2304]{1,0:T(8,128)(2,1)}, bf16[128,2304]{1,0:T(8,128)(2,1)S(1)}, u32[]{:S(2)}, u32[]{:S(2)}) collective-permute-start(bf16[128,2304]{1,0:T(8,128)(2,1)} %get-tuple-element.303), channel_id=1, source_target_pairs={{0,1},{3,2},{4,5},{7,6},{8,9},{11,10},{12,13},{15,14},{16,17},{19,... | collective-permute-start | bytes 1769480 | tf_op jit(solution)/shard_map/ppermute | solution.py:573
  299.7 18.6 %collective-permute-start.19 = (bf16[128,2304]{1,0:T(8,128)(2,1)S(1)}, bf16[128,2304]{1,0:T(8,128)(2,1)S(1)}, u32[]{:S(2)}, u32[]{:S(2)}) collective-permute-start(bf16[128,2304]{1,0:T(8,128)(2,1)S(1)} %reduce-precision_convert_fusion.21.total_ref), channel_id=1, source_target_pairs={{1,0},{2,3},{5,4},{6,7},{9,8},{10,11},{13,12},{14,15},{17,16},{18,... | collective-permute-start | bytes 1769480 | tf_op jit(solution)/shard_map/ppermute | solution.py:589
  312.4 19.7 %collective-permute-start.22 = (bf16[128,2304]{1,0:T(8,128)(2,1)S(1)}, bf16[128,2304]{1,0:T(8,128)(2,1)S(1)}, u32[]{:S(2)}, u32[]{:S(2)}) collective-permute-start(bf16[128,2304]{1,0:T(8,128)(2,1)S(1)} %reduce-precision_convert_fusion.19.total_ref), channel_id=1, source_target_pairs={{1,0},{2,3},{5,4},{6,7},{9,8},{10,11},{13,12},{14,15},{17,16},{18,... | collective-permute-start | bytes 1769480 | tf_op jit(solution)/shard_map/ppermute | solution.py:589
  324.3 20.4 %collective-permute-start.25 = (bf16[128,2304]{1,0:T(8,128)(2,1)S(1)}, bf16[128,2304]{1,0:T(8,128)(2,1)S(1)}, u32[]{:S(2)}, u32[]{:S(2)}) collective-permute-start(bf16[128,2304]{1,0:T(8,128)(2,1)S(1)} %reduce-precision_convert_fusion.17.total_ref), channel_id=1, source_target_pairs={{1,0},{2,3},{5,4},{6,7},{9,8},{10,11},{13,12},{14,15},{17,16},{18,... | collective-permute-start | bytes 1769480 | tf_op jit(solution)/shard_map/ppermute | solution.py:589
  337.1 20.3 %collective-permute-start.27 = (bf16[128,2304]{1,0:T(8,128)(2,1)S(1)}, bf16[128,2304]{1,0:T(8,128)(2,1)S(1)}, u32[]{:S(2)}, u32[]{:S(2)}) collective-permute-start(bf16[128,2304]{1,0:T(8,128)(2,1)S(1)} %reduce-precision_convert_fusion.16.total_ref), channel_id=1, source_target_pairs={{1,0},{2,3},{5,4},{6,7},{9,8},{10,11},{13,12},{14,15},{17,16},{18,... | collective-permute-start | bytes 1769480 | tf_op jit(solution)/shard_map/ppermute | solution.py:589
  338.8 62.9 %collective-permute-start.35 = (bf16[512,2304]{1,0:T(8,128)(2,1)}, bf16[512,2304]{1,0:T(8,128)(2,1)}, u32[]{:S(2)}, u32[]{:S(2)}) collective-permute-start(bf16[512,2304]{1,0:T(8,128)(2,1)} %get-tuple-element.348), channel_id=1, source_target_pairs={{0,16},{16,0},{1,17},{17,1},{2,18},{18,2},{3,19},{19,3},{4,20},{20... | collective-permute-start | bytes 7077896 | tf_op jit(solution)/shard_map/ppermute | solution.py:676
  420.4 235.9 %reduce-scatter.5.cloned.1.call-start = ((), (), s32[]{:S(2)}) async-start(), calls=%async_computation.7 | async-start | bytes 13271040 | tf_op jit(solution)/shard_map/reduce_scatter | solution.py:699
  420.5 19.8 %collective-permute-start.30 = (bf16[512,4608]{1,0:T(8,128)(2,1)}, bf16[512,4608]{1,0:T(8,128)(2,1)S(1)}, u32[]{:S(2)}, u32[]{:S(2)}) collective-permute-start(bf16[512,4608]{1,0:T(8,128)(2,1)} %get-tuple-element.339), channel_id=1, source_target_pairs={{0,16},{16,0},{1,17},{17,1},{2,18},{18,2},{3,19},{19,3},{4,20},{20... | collective-permute-start | bytes 14155784 | tf_op jit(solution)/shard_map/ppermute | solution.py:676
  423.1 16.9 %collective-permute-start.33 = (bf16[128,2304]{1,0:T(8,128)(2,1)S(1)}, bf16[128,2304]{1,0:T(8,128)(2,1)S(1)}, u32[]{:S(2)}, u32[]{:S(2)}) collective-permute-start(bf16[128,2304]{1,0:T(8,128)(2,1)S(1)} %copy-done.56), channel_id=1, source_target_pairs={{0,1},{3,2},{4,5},{7,6},{8,9},{11,10},{12,13},{15,14},{16,17},{19,... | collective-permute-start | bytes 1769480 | tf_op jit(solution)/shard_map/ppermute | solution.py:573
  455.9 25.7 %collective-permute-start.28 = (bf16[128,2304]{1,0:T(8,128)(2,1)S(1)}, bf16[128,2304]{1,0:T(8,128)(2,1)S(1)}, u32[]{:S(2)}, u32[]{:S(2)}) collective-permute-start(bf16[128,2304]{1,0:T(8,128)(2,1)S(1)} %copy-done.54), channel_id=1, source_target_pairs={{0,1},{3,2},{4,5},{7,6},{8,9},{11,10},{12,13},{15,14},{16,17},{19,... | collective-permute-start | bytes 1769480 | tf_op jit(solution)/shard_map/ppermute | solution.py:573
  467.9 24.7 %collective-permute-start.37 = (bf16[128,2304]{1,0:T(8,128)(2,1)S(1)}, bf16[128,2304]{1,0:T(8,128)(2,1)S(1)}, u32[]{:S(2)}, u32[]{:S(2)}) collective-permute-start(bf16[128,2304]{1,0:T(8,128)(2,1)S(1)} %copy-done.52), channel_id=1, source_target_pairs={{0,1},{3,2},{4,5},{7,6},{8,9},{11,10},{12,13},{15,14},{16,17},{19,... | collective-permute-start | bytes 1769480 | tf_op jit(solution)/shard_map/ppermute | solution.py:573
  470.0 16.3 %collective-permute-start.38 = (bf16[128,2304]{1,0:T(8,128)(2,1)S(1)}, bf16[128,2304]{1,0:T(8,128)(2,1)}, u32[]{:S(2)}, u32[]{:S(2)}) collective-permute-start(bf16[128,2304]{1,0:T(8,128)(2,1)S(1)} %reduce-precision_convert_fusion.13.total_ref), channel_id=1, source_target_pairs={{1,0},{2,3},{5,4},{6,7},{9,8},{10,11},{13,12},{14,15},{17,16},{18,... | collective-permute-start | bytes 1769480 | tf_op jit(solution)/shard_map/ppermute | solution.py:589
  483.4 16.1 %collective-permute-start.42 = (bf16[128,2304]{1,0:T(8,128)(2,1)S(1)}, bf16[128,2304]{1,0:T(8,128)(2,1)}, u32[]{:S(2)}, u32[]{:S(2)}) collective-permute-start(bf16[128,2304]{1,0:T(8,128)(2,1)S(1)} %reduce-precision_convert_fusion.11.total_ref), channel_id=1, source_target_pairs={{1,0},{2,3},{5,4},{6,7},{9,8},{10,11},{13,12},{14,15},{17,16},{18,... | collective-permute-start | bytes 1769480 | tf_op jit(solution)/shard_map/ppermute | solution.py:589
  492.8 18.9 %collective-permute-start.41 = (bf16[128,2304]{1,0:T(8,128)(2,1)S(1)}, bf16[128,2304]{1,0:T(8,128)(2,1)S(1)}, u32[]{:S(2)}, u32[]{:S(2)}) collective-permute-start(bf16[128,2304]{1,0:T(8,128)(2,1)S(1)} %reduce-precision_convert_fusion.10), channel_id=1, source_target_pairs={{1,2},{2,1},{5,6},{6,5},{9,10},{10,9},{13,14},{14,13},{17,18},{18,... | collective-permute-start | bytes 1769480 | tf_op jit(solution)/shard_map/ppermute | solution.py:582
  494.7 23.8 %collective-permute-start.40 = (bf16[128,2304]{1,0:T(8,128)(2,1)S(1)}, bf16[128,2304]{1,0:T(8,128)(2,1)S(1)}, u32[]{:S(2)}, u32[]{:S(2)}) collective-permute-start(bf16[128,2304]{1,0:T(8,128)(2,1)S(1)} %reduce-precision_convert_fusion.9.total_ref), channel_id=1, source_target_pairs={{1,0},{2,3},{5,4},{6,7},{9,8},{10,11},{13,12},{14,15},{17,16},{18,... | collective-permute-start | bytes 1769480 | tf_op jit(solution)/shard_map/ppermute | solution.py:589
  515.0 25.0 %collective-permute-start.49 = (bf16[256,512]{1,0:T(8,128)(2,1)}, bf16[256,512]{1,0:T(8,128)(2,1)S(1)}, u32[]{:S(2)}, u32[]{:S(2)}) collective-permute-start(bf16[256,512]{1,0:T(8,128)(2,1)} %convert_element_type.422), channel_id=1, source_target_pairs={{0,12},{4,8},{8,4},{12,0},{1,13},{5,9},{9,5},{13,1},{2,14},{6,10},... | collective-permute-start | bytes 786440 | tf_op jit(solution)/shard_map/ppermute | solution.py:828
  516.4 23.6 %collective-permute-start.48 = (bf16[256,512]{1,0:T(8,128)(2,1)}, bf16[256,512]{1,0:T(8,128)(2,1)S(1)}, u32[]{:S(2)}, u32[]{:S(2)}) collective-permute-start(bf16[256,512]{1,0:T(8,128)(2,1)} %convert_element_type.421), channel_id=1, source_target_pairs={{0,8},{4,12},{8,0},{12,4},{1,9},{5,13},{9,1},{13,5},{2,10},{6,14},... | collective-permute-start | bytes 786440 | tf_op jit(solution)/shard_map/ppermute | solution.py:828
  517.9 22.1 %collective-permute-start.47 = (bf16[256,512]{1,0:T(8,128)(2,1)S(1)}, bf16[256,512]{1,0:T(8,128)(2,1)S(1)}, u32[]{:S(2)}, u32[]{:S(2)}) collective-permute-start(bf16[256,512]{1,0:T(8,128)(2,1)S(1)} %convert_element_type.420), channel_id=1, source_target_pairs={{0,4},{4,0},{8,12},{12,8},{1,5},{5,1},{9,13},{13,9},{2,6},{6,2},{1... | collective-permute-start | bytes 786440 | tf_op jit(solution)/shard_map/ppermute | solution.py:828
  550.4 33.9 %collective-permute-start.53 = (bf16[128,2304]{1,0:T(8,128)(2,1)S(1)}, bf16[128,2304]{1,0:T(8,128)(2,1)S(1)}, u32[]{:S(2)}, u32[]{:S(2)}) collective-permute-start(bf16[128,2304]{1,0:T(8,128)(2,1)S(1)} %copy-done.55), channel_id=1, source_target_pairs={{0,1},{3,2},{4,5},{7,6},{8,9},{11,10},{12,13},{15,14},{16,17},{19,... | collective-permute-start | bytes 1769480 | tf_op jit(solution)/shard_map/ppermute | solution.py:573
  561.3 24.9 %collective-permute-start.55 = (bf16[128,2304]{1,0:T(8,128)(2,1)S(1)}, bf16[128,2304]{1,0:T(8,128)(2,1)}, u32[]{:S(2)}, u32[]{:S(2)}) collective-permute-start(bf16[128,2304]{1,0:T(8,128)(2,1)S(1)} %copy-done.53), channel_id=1, source_target_pairs={{0,1},{3,2},{4,5},{7,6},{8,9},{11,10},{12,13},{15,14},{16,17},{19,... | collective-permute-start | bytes 1769480 | tf_op jit(solution)/shard_map/ppermute | solution.py:573
  579.9 29.0 %collective-permute-start.58 = (bf16[128,2304]{1,0:T(8,128)(2,1)}, bf16[128,2304]{1,0:T(8,128)(2,1)}, u32[]{:S(2)}, u32[]{:S(2)}) collective-permute-start(bf16[128,2304]{1,0:T(8,128)(2,1)} %get-tuple-element.442), channel_id=1, source_target_pairs={{0,1},{3,2},{4,5},{7,6},{8,9},{11,10},{12,13},{15,14},{16,17},{19,... | collective-permute-start | bytes 1769480 | tf_op jit(solution)/shard_map/ppermute | solution.py:573
  590.4 21.2 %collective-permute-start.57 = (bf16[128,2304]{1,0:T(8,128)(2,1)S(1)}, bf16[128,2304]{1,0:T(8,128)(2,1)}, u32[]{:S(2)}, u32[]{:S(2)}) collective-permute-start(bf16[128,2304]{1,0:T(8,128)(2,1)S(1)} %reduce-precision_convert_fusion.6), channel_id=1, source_target_pairs={{1,2},{2,1},{5,6},{6,5},{9,10},{10,9},{13,14},{14,13},{17,18},{18,... | collective-permute-start | bytes 1769480 | tf_op jit(solution)/shard_map/ppermute | solution.py:582
  591.8 30.1 %collective-permute-start.52 = (bf16[128,2304]{1,0:T(8,128)(2,1)}, bf16[128,2304]{1,0:T(8,128)(2,1)}, u32[]{:S(2)}, u32[]{:S(2)}) collective-permute-start(bf16[128,2304]{1,0:T(8,128)(2,1)} %get-tuple-element.449), channel_id=1, source_target_pairs={{0,1},{3,2},{4,5},{7,6},{8,9},{11,10},{12,13},{15,14},{16,17},{19,... | collective-permute-start | bytes 1769480 | tf_op jit(solution)/shard_map/ppermute | solution.py:573
  598.4 20.5 %collective-permute-start.56 = (bf16[128,2304]{1,0:T(8,128)(2,1)S(1)}, bf16[128,2304]{1,0:T(8,128)(2,1)}, u32[]{:S(2)}, u32[]{:S(2)}) collective-permute-start(bf16[128,2304]{1,0:T(8,128)(2,1)S(1)} %reduce-precision_convert_fusion.5.total_ref), channel_id=1, source_target_pairs={{1,0},{2,3},{5,4},{6,7},{9,8},{10,11},{13,12},{14,15},{17,16},{18,... | collective-permute-start | bytes 1769480 | tf_op jit(solution)/shard_map/ppermute | solution.py:589
  611.6 49.3 %all-to-all-start = ((bf16[4,288,1664]{2,1,0:T(8,128)(2,1)}), bf16[4,288,1664]{2,1,0:T(8,128)(2,1)}, u32[]{:S(2)}, u32[]{:S(2)}) async-start(bf16[4,288,1664]{2,1,0:T(8,128)(2,1)} %bitcast.77), calls=%async_computation.1 | async-start | bytes 7667712 | tf_op jit(solution)/shard_map/all_to_all | solution.py:690
  617.6 22.3 %collective-permute-start.62 = (bf16[128,2304]{1,0:T(8,128)(2,1)S(1)}, bf16[128,2304]{1,0:T(8,128)(2,1)S(1)}, u32[]{:S(2)}, u32[]{:S(2)}) collective-permute-start(bf16[128,2304]{1,0:T(8,128)(2,1)S(1)} %reduce-precision_convert_fusion.3.refs_1_), channel_id=1, source_target_pairs={{1,0},{2,3},{5,4},{6,7},{9,8},{10,11},{13,12},{14,15},{17,16},{18,... | collective-permute-start | bytes 1769480 | tf_op jit(solution)/shard_map/ppermute | solution.py:589
  623.4 20.3 %collective-permute-start.61 = (bf16[128,2304]{1,0:T(8,128)(2,1)S(1)}, bf16[128,2304]{1,0:T(8,128)(2,1)}, u32[]{:S(2)}, u32[]{:S(2)}) collective-permute-start(bf16[128,2304]{1,0:T(8,128)(2,1)S(1)} %reduce-precision_convert_fusion.2), channel_id=1, source_target_pairs={{1,2},{2,1},{5,6},{6,5},{9,10},{10,9},{13,14},{14,13},{17,18},{18,... | collective-permute-start | bytes 1769480 | tf_op jit(solution)/shard_map/ppermute | solution.py:582
  626.1 26.5 %collective-permute-start.65 = (bf16[128,2304]{1,0:T(8,128)(2,1)S(1)}, bf16[128,2304]{1,0:T(8,128)(2,1)S(1)}, u32[]{:S(2)}, u32[]{:S(2)}) collective-permute-start(bf16[128,2304]{1,0:T(8,128)(2,1)S(1)} %reduce-precision_convert_fusion.1.refs_1_), channel_id=1, source_target_pairs={{1,0},{2,3},{5,4},{6,7},{9,8},{10,11},{13,12},{14,15},{17,16},{18,... | collective-permute-start | bytes 1769480 | tf_op jit(solution)/shard_map/ppermute | solution.py:589
  644.9 28.3 %collective-permute-start.64 = (bf16[128,2304]{1,0:T(8,128)(2,1)S(1)}, bf16[128,2304]{1,0:T(8,128)(2,1)S(1)}, u32[]{:S(2)}, u32[]{:S(2)}) collective-permute-start(bf16[128,2304]{1,0:T(8,128)(2,1)S(1)} %reduce-precision_convert_fusion.refs_1_), channel_id=1, source_target_pairs={{1,0},{2,3},{5,4},{6,7},{9,8},{10,11},{13,12},{14,15},{17,16},{18,... | collective-permute-start | bytes 1769480 | tf_op jit(solution)/shard_map/ppermute | solution.py:589
  (114 other events, 1113.2 us)
Sparse Core Ops, SparseCore 0:
  11.3 53.9 all-gather.2
  67.2 175.9 all-gather.4
  420.5 61.8 reduce-scatter.2
  485.4 125.3 reduce-scatter.4

commit v6 on v5

--- a/solution.py
+++ b/solution.py
@@ -835,7 +835,7 @@
         post_mid,
         {
             0: hold("g_down", lambda: scatter(product(down_left, held["down_right"]))),
-            1: hold("g_gate_up", lambda: scatter(product(held["mid_left"], both_right))),
+            2: hold("g_gate_up", lambda: scatter(product(held["mid_left"], both_right))),
             3: lambda: attention_back(0),
         },
     )

time: 697 us -> 708 us (1.016)
  waiting for transfers between devices: 278 us -> 297 us
  starting transfers between devices: 109 us -> 98.3 us
    ppermute x16, waiting for transfers between devices: 80.4 us -> 92.6 us  [join(): self.third[k] = lax.ppermute(total, 'tensor', [(1, 0), (2, 3)])]
    ppermute x16, starting transfers between devices: 49.6 us -> 38.4 us  [send(): self.first[k] = lax.ppermute(piece, 'tensor', [(0, 1), (3, 2)])]
  transfers between devices with their start and end apart: 72 -> 72, of which waited for: 33 -> 36; matrix products, arithmetic and copies ran while one was open for 10% -> 11% of each run, Pallas kernels for 22% -> 22%
where the time goes in v6:
time: 708 us; the launch traced here: 698 us
  waiting for transfers between devices  297 us (42%)
  Pallas kernels  181 us (26%)
  starting transfers between devices  98.3 us (14%)
  other arithmetic  48 us (7%)
  matrix products  29.9 us (4%)
  local copies, waits for them, and re-layouts  28.1 us (4%)
  between operations  16.1 us (2%)
    ppermute x16, waiting for transfers between devices, send(): self.first[k] = lax.ppermute(piece, 'tensor', [(0, 1), (3, 2)])  97 us
    ppermute x16, waiting for transfers between devices, join(): self.third[k] = lax.ppermute(total, 'tensor', [(1, 0), (2, 3)])  92.6 us
    pallas_call x16, Pallas kernels, post(): call(body, tuple(out_shapes), (steps,), specs, tuple(out_specs), flops=20...  56.2 us
    ppermute x3, waiting for transfers between devices, local(): others = [lax.ppermute(kv, 'ctx', flips[j]) for j in range(1, n_ctx)]  43.8 us
    all_gather x1, waiting for transfers between devices, local(): full_attn = lax.all_gather(pack_attn, ('dp', 'ctx'), axis=0, tiled=True)  42.2 us
    ppermute x16, starting transfers between devices, send(): self.first[k] = lax.ppermute(piece, 'tensor', [(0, 1), (3, 2)])  38.4 us
    pallas_call x1, Pallas kernels, ffn_back(): call(functools.partial(ffn_back_body, len(ys), n_out), (shape((rows, 2 *...  37.1 us
    dot_general x4, matrix products, tmm(): lax.dot_general(a, b, (((0,), (0,)), ((), ())), preferred_element_type=F32)  27.5 us
  transfers between devices with their start and end apart: 72, of which 36 were waited for; matrix products, arithmetic and copies ran while one was open for 11% of the time, Pallas kernels for 22%

profile of v6, /device:TPU:0, one launch (start us, length us, event | category | flops | bytes accessed | tf_op | source)
XLA Modules:
  0.0 697.7 jit_solution(76429349137049168)
XLA Ops:
  17.2 4.5 compare_select_fusion.1
  23.1 42.2 %all-gather.3.cloned.1.call-done.w_ref.refs_3_.refs_7_.refs_4_ = bf16[2304,1664]{1,0:T(8,128)(2,1)} async-done(((bf16[288,1664]{1,0:T(8,128)(2,1)}), bf16[2304,1664]{1,0:T(8,128)(2,1)}) %all-gather.3.cloned.1.call-update) | async-done | bytes 7667728 | tf_op jit(solution)/shard_map/all_gather | solution.py:661
  70.2 7.0 %shard_map.238.refs_0_ = bf16[512,1024]{1,0:T(8,128)(2,1)} custom-call(bf16[512,2304]{1,0:T(8,128)(2,1)} %multiply_convert_fusion.x_ref, bf16[2304,1664]{1,0:T(8,128)(2,1)} %all-gather.3.cloned.1.call-done.w_ref.refs_3_.refs_7_.refs_4_, f32[512,128]{1,0:T(8,128)} %bitcast.82, f32[512,128]{1,0:T(8,128)} %bitcast.81), custom_call_target="tpu_custom_call" | custom-call | flops 2415919104 | bytes 8126464 | tf_op jit(solution)/shard_map/pallas_call | solution.py:94
  83.3 21.8 %collective-permute-done.2.refs_7_.refs_11_ = bf16[512,512]{1,0:T(8,128)(2,1)S(1)} collective-permute-done((bf16[512,512]{1,0:T(8,128)(2,1)S(1)}, bf16[512,512]{1,0:T(8,128)(2,1)S(1)}, u32[]{:S(2)}, u32[]{:S(2)}) %collective-permute-start.2) | collective-permute-done | bytes 524320 | tf_op jit(solution)/shard_map/ppermute | solution.py:709
  105.1 11.2 %collective-permute-done.1.refs_6_.refs_10_ = bf16[512,512]{1,0:T(8,128)(2,1)S(1)} collective-permute-done((bf16[512,512]{1,0:T(8,128)(2,1)S(1)}, bf16[512,512]{1,0:T(8,128)(2,1)S(1)}, u32[]{:S(2)}, u32[]{:S(2)}) %collective-permute-start.1) | collective-permute-done | bytes 524320 | tf_op jit(solution)/shard_map/ppermute | solution.py:709
  116.3 10.9 %collective-permute-done.refs_5_.refs_9_ = bf16[512,512]{1,0:T(8,128)(2,1)S(1)} collective-permute-done((bf16[512,512]{1,0:T(8,128)(2,1)S(1)}, bf16[512,512]{1,0:T(8,128)(2,1)S(1)}, u32[]{:S(2)}, u32[]{:S(2)}) %collective-permute-start) | collective-permute-done | bytes 524320 | tf_op jit(solution)/shard_map/ppermute | solution.py:709
  127.9 4.8 shard_map.239
  137.7 4.8 shard_map.240
  145.3 4.9 collective-permute-done.3
  151.2 11.6 %collective-permute-done.5 = bf16[128,2304]{1,0:T(8,128)(2,1)S(1)} collective-permute-done((bf16[128,2304]{1,0:T(8,128)(2,1)}, bf16[128,2304]{1,0:T(8,128)(2,1)S(1)}, u32[]{:S(2)}, u32[]{:S(2)}) %collective-permute-start.5) | collective-permute-done | bytes 589856 | tf_op jit(solution)/shard_map/ppermute | solution.py:573
  165.1 21.3 %collective-permute-done.8 = bf16[128,2304]{1,0:T(8,128)(2,1)S(1)} collective-permute-done((bf16[128,2304]{1,0:T(8,128)(2,1)}, bf16[128,2304]{1,0:T(8,128)(2,1)S(1)}, u32[]{:S(2)}, u32[]{:S(2)}) %collective-permute-start.8) | collective-permute-done | bytes 589856 | tf_op jit(solution)/shard_map/ppermute | solution.py:573
  194.9 11.9 %collective-permute-done.9.third_ref = bf16[128,2304]{1,0:T(8,128)(2,1)} collective-permute-done((bf16[128,2304]{1,0:T(8,128)(2,1)S(1)}, bf16[128,2304]{1,0:T(8,128)(2,1)}, u32[]{:S(2)}, u32[]{:S(2)}) %collective-permute-start.9) | collective-permute-done | bytes 589856 | tf_op jit(solution)/shard_map/ppermute | solution.py:589
  211.2 8.1 %collective-permute-done.12.third_ref = bf16[128,2304]{1,0:T(8,128)(2,1)S(1)} collective-permute-done((bf16[128,2304]{1,0:T(8,128)(2,1)S(1)}, bf16[128,2304]{1,0:T(8,128)(2,1)S(1)}, u32[]{:S(2)}, u32[]{:S(2)}) %collective-permute-start.12) | collective-permute-done | bytes 589856 | tf_op jit(solution)/shard_map/ppermute | solution.py:589
  222.9 8.1 %collective-permute-done.14.third_ref = bf16[128,2304]{1,0:T(8,128)(2,1)S(1)} collective-permute-done((bf16[128,2304]{1,0:T(8,128)(2,1)S(1)}, bf16[128,2304]{1,0:T(8,128)(2,1)S(1)}, u32[]{:S(2)}, u32[]{:S(2)}) %collective-permute-start.14) | collective-permute-done | bytes 589856 | tf_op jit(solution)/shard_map/ppermute | solution.py:589
  243.1 25.4 %shard_map.245 = (bf16[512,2304]{1,0:T(8,128)(2,1)}, bf16[512,2304]{1,0:T(8,128)(2,1)}, bf16[512,2304]{1,0:T(8,128)(2,1)}, bf16[128,2304]{1,0:T(8,128)(2,1)}, bf...) custom-call(bf16[128,2304]{1,0:T(8,128)(2,1)} %get-tuple-element.352.refs_0_, ...), custom_call_target="tpu_custom_call" | custom-call | flops 16307453952 | bytes 43646976 | tf_op jit(solution)/shard_map/pallas_call | solution.py:440
  276.1 10.0 %collective-permute-done.16 = bf16[128,2304]{1,0:T(8,128)(2,1)S(1)} collective-permute-done((bf16[128,2304]{1,0:T(8,128)(2,1)}, bf16[128,2304]{1,0:T(8,128)(2,1)S(1)}, u32[]{:S(2)}, u32[]{:S(2)}) %collective-permute-start.16) | collective-permute-done | bytes 589856 | tf_op jit(solution)/shard_map/ppermute | solution.py:573
  288.2 10.6 %collective-permute-done.18 = bf16[128,2304]{1,0:T(8,128)(2,1)S(1)} collective-permute-done((bf16[128,2304]{1,0:T(8,128)(2,1)}, bf16[128,2304]{1,0:T(8,128)(2,1)S(1)}, u32[]{:S(2)}, u32[]{:S(2)}) %collective-permute-start.18) | collective-permute-done | bytes 589856 | tf_op jit(solution)/shard_map/ppermute | solution.py:573
  301.1 10.3 %collective-permute-done.21 = bf16[128,2304]{1,0:T(8,128)(2,1)S(1)} collective-permute-done((bf16[128,2304]{1,0:T(8,128)(2,1)}, bf16[128,2304]{1,0:T(8,128)(2,1)S(1)}, u32[]{:S(2)}, u32[]{:S(2)}) %collective-permute-start.21) | collective-permute-done | bytes 589856 | tf_op jit(solution)/shard_map/ppermute | solution.py:573
  313.7 4.7 collective-permute-done.19.third_ref
  325.6 6.5 collective-permute-done.22.third_ref
  338.9 5.8 collective-permute-done.25.third_ref
  349.5 7.8 %collective-permute-done.27.third_ref = bf16[128,2304]{1,0:T(8,128)(2,1)S(1)} collective-permute-done((bf16[128,2304]{1,0:T(8,128)(2,1)S(1)}, bf16[128,2304]{1,0:T(8,128)(2,1)S(1)}, u32[]{:S(2)}, u32[]{:S(2)}) %collective-permute-start.27) | collective-permute-done | bytes 589856 | tf_op jit(solution)/shard_map/ppermute | solution.py:589
  362.3 37.1 %shard_map.250 = (bf16[512,4608]{1,0:T(8,128)(2,1)}, bf16[128,2304]{1,0:T(8,128)(2,1)}, bf16[128,2304]{1,0:T(8,128)(2,1)}, bf16[128,2304]{1,0:T(8,128)(2,1)}, bf16[128,2304]{1,0:T(8,128)(2,1)}) custom-call(bf16[128,2304]{1,0:T(8,128)(2,1)} %get-tuple-element.337.refs_0_, bf16[128,2304]{1,0:T(8,128)(2,1)} %get-tuple-element.338.refs_1_, ...), custom_call_target="tpu_custom_call" | custom-call | flops 16307453952 | bytes 46006272 | tf_op jit(solution)/shard_map/pallas_call | solution.py:492
  404.8 7.6 %collective-permute-done.29 = bf16[128,2304]{1,0:T(8,128)(2,1)S(1)} collective-permute-done((bf16[128,2304]{1,0:T(8,128)(2,1)}, bf16[128,2304]{1,0:T(8,128)(2,1)S(1)}, u32[]{:S(2)}, u32[]{:S(2)}) %collective-permute-start.29) | collective-permute-done | bytes 589856 | tf_op jit(solution)/shard_map/ppermute | solution.py:573
  412.8 7.5 %convolution_convert_fusion.1 = bf16[1152,2304]{1,0:T(8,128)(2,1)} fusion(bf16[1024,1152]{1,0:T(8,128)(2,1)S(1)} %pad_maximum_fusion.5, bf16[1024,2304]{1,0:T(8,128)(2,1)S(1)} %pad_maximum_fusion.1), kind=kOutput, calls=%fused_computation.1 | convolution fusion | flops 5438472192 | bytes 12386304 | tf_op jit(solution)/shard_map/dot_general | solution.py:47
  423.1 4.3 collective-permute-start.31
  427.4 4.5 collective-permute-done.36
  433.5 4.3 collective-permute-start.28
  443.5 9.1 %collective-permute-done.28 = bf16[128,2304]{1,0:T(8,128)(2,1)S(1)} collective-permute-done((bf16[128,2304]{1,0:T(8,128)(2,1)S(1)}, bf16[128,2304]{1,0:T(8,128)(2,1)S(1)}, u32[]{:S(2)}, u32[]{:S(2)}) %collective-permute-start.28) | collective-permute-done | bytes 589856 | tf_op jit(solution)/shard_map/ppermute | solution.py:573
  453.0 15.8 %collective-permute-done.38.third_ref = bf16[128,2304]{1,0:T(8,128)(2,1)S(1)} collective-permute-done((bf16[128,2304]{1,0:T(8,128)(2,1)S(1)}, bf16[128,2304]{1,0:T(8,128)(2,1)S(1)}, u32[]{:S(2)}, u32[]{:S(2)}) %collective-permute-start.38) | collective-permute-done | bytes 589856 | tf_op jit(solution)/shard_map/ppermute | solution.py:589
  469.5 4.2 shard_map.251
  473.8 4.9 pad_maximum_fusion
  478.7 13.7 %convolution_convert_fusion = bf16[1152,4608]{1,0:T(8,128)(2,1)} fusion(bf16[1024,1152]{1,0:T(8,128)(2,1)S(1)} %copy-done.26, bf16[1024,4608]{1,0:T(8,128)(2,1)S(1)} %pad_maximum_fusion), kind=kOutput, calls=%fused_computation | convolution fusion | flops 10876944384 | bytes 22413312 | tf_op jit(solution)/shard_map/dot_general | solution.py:47
  496.9 9.0 %collective-permute-done.35 = bf16[128,2304]{1,0:T(8,128)(2,1)S(1)} collective-permute-done((bf16[128,2304]{1,0:T(8,128)(2,1)S(1)}, bf16[128,2304]{1,0:T(8,128)(2,1)S(1)}, u32[]{:S(2)}, u32[]{:S(2)}) %collective-permute-start.35) | collective-permute-done | bytes 589856 | tf_op jit(solution)/shard_map/ppermute | solution.py:573
  510.9 4.3 shard_map.252
  515.2 8.1 %shard_map.253 = (bf16[256,512]{1,0:T(8,128)(2,1)}, f32[256,512]{1,0:T(8,128)}, f32[256,512]{1,0:T(8,128)}, f32[256,512]{1,0:T(8,128)}, f32[256,512]{1,0:T(8,128)}) custom-call(bf16[512,1024]{1,0:T(8,128)(2,1)} %shard_map.238.refs_0_, s32[256,1]{1,0:T(8,128)} %copy.50.refs_1_, s32[1,1024]{1,0:T(1,128)} %bitcast.85, f32[256,512]{1,0:T(8,128)} %get-tuple-element.369.refs_3_, ...), custom_call_target="tpu_custom_call" | custom-call | flops 1946157056 | bytes 9961472 | tf_op jit(solution)/shard_map/pallas_call | solution.py:241
  531.0 4.5 shard_map.254
  539.1 4.2 shard_map.255
  543.3 7.8 %shard_map.256 = (bf16[256,512]{1,0:T(8,128)(2,1)}, f32[256,512]{1,0:T(8,128)}, f32[256,512]{1,0:T(8,128)}, f32[256,512]{1,0:T(8,128)}, f32[256,512]{1,0:T(8,128)}) custom-call(bf16[512,1024]{1,0:T(8,128)(2,1)} %shard_map.238.refs_0_, s32[256,1]{1,0:T(8,128)} %copy.50.refs_1_, s32[1,1024]{1,0:T(1,128)} %bitcast.86, f32[256,512]{1,0:T(8,128)} %get-tuple-element.323.refs_3_, ...), custom_call_target="tpu_custom_call" | custom-call | flops 1946157056 | bytes 9961472 | tf_op jit(solution)/shard_map/pallas_call | solution.py:241
  552.9 6.0 shard_map.257
  561.9 4.9 collective-permute-start.53
  581.5 6.2 collective-permute-done.45.refs_7_
  589.1 6.2 shard_map.259
  622.9 4.8 all-to-all-start
  638.7 12.1 %collective-permute-done.62.refs_2_ = bf16[128,2304]{1,0:T(8,128)(2,1)S(1)} collective-permute-done((bf16[128,2304]{1,0:T(8,128)(2,1)S(1)}, bf16[128,2304]{1,0:T(8,128)(2,1)S(1)}, u32[]{:S(2)}, u32[]{:S(2)}) %collective-permute-start.62) | collective-permute-done | bytes 589856 | tf_op jit(solution)/shard_map/ppermute | solution.py:589
  657.1 6.4 collective-permute-done.65.refs_2_
  667.2 4.5 shard_map.264
  677.5 5.9 all-to-all-start.1
  (417 shorter events, 219.5 us)
Async XLA Ops:
  7.2 58.1 %all-gather.3.cloned.1.call-start = ((), (), s32[]{:S(2)}) async-start(), calls=%async_computation.4 | async-start | bytes 8626176 | tf_op jit(solution)/shard_map/all_gather | solution.py:661
  11.2 231.9 %all-gather.5.cloned.1.call-start = ((), (), s32[]{:S(2)}) async-start(), calls=%async_computation.5 | async-start | bytes 35831808 | tf_op jit(solution)/shard_map/all_gather | solution.py:662
  14.4 563.6 %reduce-scatter.3.cloned.1.call-start = ((), (), s32[]{:S(2)}) async-start(), calls=%async_computation.6 | async-start | bytes 6635520 | tf_op jit(solution)/shard_map/reduce_scatter | solution.py:699
  78.3 26.7 %collective-permute-start.2 = (bf16[512,512]{1,0:T(8,128)(2,1)S(1)}, bf16[512,512]{1,0:T(8,128)(2,1)S(1)}, u32[]{:S(2)}, u32[]{:S(2)}) collective-permute-start(bf16[512,512]{1,0:T(8,128)(2,1)S(1)} %slice.95.refs_4_.refs_8_), channel_id=1, source_target_pairs={{0,12},{4,8},{8,4},{12,0},{1,13},{5,9},{9,5},{13,1},{2,14},{6,10},... | collective-permute-start | bytes 1572872 | tf_op jit(solution)/shard_map/ppermute | solution.py:709
  79.9 36.4 %collective-permute-start.1 = (bf16[512,512]{1,0:T(8,128)(2,1)S(1)}, bf16[512,512]{1,0:T(8,128)(2,1)S(1)}, u32[]{:S(2)}, u32[]{:S(2)}) collective-permute-start(bf16[512,512]{1,0:T(8,128)(2,1)S(1)} %slice.95.refs_4_.refs_8_), channel_id=1, source_target_pairs={{0,8},{4,12},{8,0},{12,4},{1,9},{5,13},{9,1},{13,5},{2,10},{6,14},... | collective-permute-start | bytes 1572872 | tf_op jit(solution)/shard_map/ppermute | solution.py:709
  81.3 45.8 %collective-permute-start = (bf16[512,512]{1,0:T(8,128)(2,1)S(1)}, bf16[512,512]{1,0:T(8,128)(2,1)S(1)}, u32[]{:S(2)}, u32[]{:S(2)}) collective-permute-start(bf16[512,512]{1,0:T(8,128)(2,1)S(1)} %slice.95.refs_4_.refs_8_), channel_id=1, source_target_pairs={{0,4},{4,0},{8,12},{12,8},{1,5},{5,1},{9,13},{13,9},{2,6},{6,2},{1... | collective-permute-start | bytes 1572872 | tf_op jit(solution)/shard_map/ppermute | solution.py:709
  132.8 17.4 %collective-permute-start.3 = (bf16[128,2304]{1,0:T(8,128)(2,1)}, bf16[128,2304]{1,0:T(8,128)(2,1)S(1)}, u32[]{:S(2)}, u32[]{:S(2)}) collective-permute-start(bf16[128,2304]{1,0:T(8,128)(2,1)} %get-tuple-element.249), channel_id=1, source_target_pairs={{0,1},{3,2},{4,5},{7,6},{8,9},{11,10},{12,13},{15,14},{16,17},{19,... | collective-permute-start | bytes 1769480 | tf_op jit(solution)/shard_map/ppermute | solution.py:573
  136.2 26.6 %collective-permute-start.5 = (bf16[128,2304]{1,0:T(8,128)(2,1)}, bf16[128,2304]{1,0:T(8,128)(2,1)S(1)}, u32[]{:S(2)}, u32[]{:S(2)}) collective-permute-start(bf16[128,2304]{1,0:T(8,128)(2,1)} %get-tuple-element.252), channel_id=1, source_target_pairs={{0,1},{3,2},{4,5},{7,6},{8,9},{11,10},{12,13},{15,14},{16,17},{19,... | collective-permute-start | bytes 1769480 | tf_op jit(solution)/shard_map/ppermute | solution.py:573
  142.5 50.0 %collective-permute-start.11 = (bf16[128,2304]{1,0:T(8,128)(2,1)}, bf16[128,2304]{1,0:T(8,128)(2,1)S(1)}, u32[]{:S(2)}, u32[]{:S(2)}) collective-permute-start(bf16[128,2304]{1,0:T(8,128)(2,1)} %get-tuple-element.264), channel_id=1, source_target_pairs={{0,1},{3,2},{4,5},{7,6},{8,9},{11,10},{12,13},{15,14},{16,17},{19,... | collective-permute-start | bytes 1769480 | tf_op jit(solution)/shard_map/ppermute | solution.py:573
  144.0 42.4 %collective-permute-start.8 = (bf16[128,2304]{1,0:T(8,128)(2,1)}, bf16[128,2304]{1,0:T(8,128)(2,1)S(1)}, u32[]{:S(2)}, u32[]{:S(2)}) collective-permute-start(bf16[128,2304]{1,0:T(8,128)(2,1)} %get-tuple-element.256), channel_id=1, source_target_pairs={{0,1},{3,2},{4,5},{7,6},{8,9},{11,10},{12,13},{15,14},{16,17},{19,... | collective-permute-start | bytes 1769480 | tf_op jit(solution)/shard_map/ppermute | solution.py:573
  163.0 24.3 %collective-permute-start.7 = (bf16[128,2304]{1,0:T(8,128)(2,1)S(1)}, bf16[128,2304]{1,0:T(8,128)(2,1)S(1)}, u32[]{:S(2)}, u32[]{:S(2)}) collective-permute-start(bf16[128,2304]{1,0:T(8,128)(2,1)S(1)} %reduce-precision_convert_fusion.30), channel_id=1, source_target_pairs={{1,2},{2,1},{5,6},{6,5},{9,10},{10,9},{13,14},{14,13},{17,18},{18,... | collective-permute-start | bytes 1769480 | tf_op jit(solution)/shard_map/ppermute | solution.py:582
  163.8 25.0 %collective-permute-start.6 = (bf16[128,2304]{1,0:T(8,128)(2,1)S(1)}, bf16[128,2304]{1,0:T(8,128)(2,1)S(1)}, u32[]{:S(2)}, u32[]{:S(2)}) collective-permute-start(bf16[128,2304]{1,0:T(8,128)(2,1)S(1)} %reduce-precision_convert_fusion.29.total_ref), channel_id=1, source_target_pairs={{1,0},{2,3},{5,4},{6,7},{9,8},{10,11},{13,12},{14,15},{17,16},{18,... | collective-permute-start | bytes 1769480 | tf_op jit(solution)/shard_map/ppermute | solution.py:589
  187.4 19.3 %collective-permute-start.9 = (bf16[128,2304]{1,0:T(8,128)(2,1)S(1)}, bf16[128,2304]{1,0:T(8,128)(2,1)}, u32[]{:S(2)}, u32[]{:S(2)}) collective-permute-start(bf16[128,2304]{1,0:T(8,128)(2,1)S(1)} %reduce-precision_convert_fusion.27.total_ref), channel_id=1, source_target_pairs={{1,0},{2,3},{5,4},{6,7},{9,8},{10,11},{13,12},{14,15},{17,16},{18,... | collective-permute-start | bytes 1769480 | tf_op jit(solution)/shard_map/ppermute | solution.py:589
  192.7 16.8 %collective-permute-start.13 = (bf16[128,2304]{1,0:T(8,128)(2,1)S(1)}, bf16[128,2304]{1,0:T(8,128)(2,1)S(1)}, u32[]{:S(2)}, u32[]{:S(2)}) collective-permute-start(bf16[128,2304]{1,0:T(8,128)(2,1)S(1)} %reduce-precision_convert_fusion.26), channel_id=1, source_target_pairs={{1,2},{2,1},{5,6},{6,5},{9,10},{10,9},{13,14},{14,13},{17,18},{18,... | collective-permute-start | bytes 1769480 | tf_op jit(solution)/shard_map/ppermute | solution.py:582
  193.6 25.7 %collective-permute-start.12 = (bf16[128,2304]{1,0:T(8,128)(2,1)S(1)}, bf16[128,2304]{1,0:T(8,128)(2,1)S(1)}, u32[]{:S(2)}, u32[]{:S(2)}) collective-permute-start(bf16[128,2304]{1,0:T(8,128)(2,1)S(1)} %reduce-precision_convert_fusion.25.total_ref), channel_id=1, source_target_pairs={{1,0},{2,3},{5,4},{6,7},{9,8},{10,11},{13,12},{14,15},{17,16},{18,... | collective-permute-start | bytes 1769480 | tf_op jit(solution)/shard_map/ppermute | solution.py:589
  209.7 21.3 %collective-permute-start.14 = (bf16[128,2304]{1,0:T(8,128)(2,1)S(1)}, bf16[128,2304]{1,0:T(8,128)(2,1)S(1)}, u32[]{:S(2)}, u32[]{:S(2)}) collective-permute-start(bf16[128,2304]{1,0:T(8,128)(2,1)S(1)} %reduce-precision_convert_fusion.24.total_ref), channel_id=1, source_target_pairs={{1,0},{2,3},{5,4},{6,7},{9,8},{10,11},{13,12},{14,15},{17,16},{18,... | collective-permute-start | bytes 1769480 | tf_op jit(solution)/shard_map/ppermute | solution.py:589
  268.6 17.5 %collective-permute-start.16 = (bf16[128,2304]{1,0:T(8,128)(2,1)}, bf16[128,2304]{1,0:T(8,128)(2,1)S(1)}, u32[]{:S(2)}, u32[]{:S(2)}) collective-permute-start(bf16[128,2304]{1,0:T(8,128)(2,1)} %get-tuple-element.285), channel_id=1, source_target_pairs={{0,1},{3,2},{4,5},{7,6},{8,9},{11,10},{12,13},{15,14},{16,17},{19,... | collective-permute-start | bytes 1769480 | tf_op jit(solution)/shard_map/ppermute | solution.py:573
  272.1 26.6 %collective-permute-start.18 = (bf16[128,2304]{1,0:T(8,128)(2,1)}, bf16[128,2304]{1,0:T(8,128)(2,1)S(1)}, u32[]{:S(2)}, u32[]{:S(2)}) collective-permute-start(bf16[128,2304]{1,0:T(8,128)(2,1)} %get-tuple-element.288), channel_id=1, source_target_pairs={{0,1},{3,2},{4,5},{7,6},{8,9},{11,10},{12,13},{15,14},{16,17},{19,... | collective-permute-start | bytes 1769480 | tf_op jit(solution)/shard_map/ppermute | solution.py:573
  273.5 37.9 %collective-permute-start.21 = (bf16[128,2304]{1,0:T(8,128)(2,1)}, bf16[128,2304]{1,0:T(8,128)(2,1)S(1)}, u32[]{:S(2)}, u32[]{:S(2)}) collective-permute-start(bf16[128,2304]{1,0:T(8,128)(2,1)} %get-tuple-element.293), channel_id=1, source_target_pairs={{0,1},{3,2},{4,5},{7,6},{8,9},{11,10},{12,13},{15,14},{16,17},{19,... | collective-permute-start | bytes 1769480 | tf_op jit(solution)/shard_map/ppermute | solution.py:573
  274.8 48.5 %collective-permute-start.24 = (bf16[128,2304]{1,0:T(8,128)(2,1)}, bf16[128,2304]{1,0:T(8,128)(2,1)S(1)}, u32[]{:S(2)}, u32[]{:S(2)}) collective-permute-start(bf16[128,2304]{1,0:T(8,128)(2,1)} %get-tuple-element.303), channel_id=1, source_target_pairs={{0,1},{3,2},{4,5},{7,6},{8,9},{11,10},{12,13},{15,14},{16,17},{19,... | collective-permute-start | bytes 1769480 | tf_op jit(solution)/shard_map/ppermute | solution.py:573
  299.8 18.6 %collective-permute-start.19 = (bf16[128,2304]{1,0:T(8,128)(2,1)S(1)}, bf16[128,2304]{1,0:T(8,128)(2,1)S(1)}, u32[]{:S(2)}, u32[]{:S(2)}) collective-permute-start(bf16[128,2304]{1,0:T(8,128)(2,1)S(1)} %reduce-precision_convert_fusion.21.total_ref), channel_id=1, source_target_pairs={{1,0},{2,3},{5,4},{6,7},{9,8},{10,11},{13,12},{14,15},{17,16},{18,... | collective-permute-start | bytes 1769480 | tf_op jit(solution)/shard_map/ppermute | solution.py:589
  312.4 19.7 %collective-permute-start.22 = (bf16[128,2304]{1,0:T(8,128)(2,1)S(1)}, bf16[128,2304]{1,0:T(8,128)(2,1)S(1)}, u32[]{:S(2)}, u32[]{:S(2)}) collective-permute-start(bf16[128,2304]{1,0:T(8,128)(2,1)S(1)} %reduce-precision_convert_fusion.19.total_ref), channel_id=1, source_target_pairs={{1,0},{2,3},{5,4},{6,7},{9,8},{10,11},{13,12},{14,15},{17,16},{18,... | collective-permute-start | bytes 1769480 | tf_op jit(solution)/shard_map/ppermute | solution.py:589
  324.3 20.4 %collective-permute-start.25 = (bf16[128,2304]{1,0:T(8,128)(2,1)S(1)}, bf16[128,2304]{1,0:T(8,128)(2,1)S(1)}, u32[]{:S(2)}, u32[]{:S(2)}) collective-permute-start(bf16[128,2304]{1,0:T(8,128)(2,1)S(1)} %reduce-precision_convert_fusion.17.total_ref), channel_id=1, source_target_pairs={{1,0},{2,3},{5,4},{6,7},{9,8},{10,11},{13,12},{14,15},{17,16},{18,... | collective-permute-start | bytes 1769480 | tf_op jit(solution)/shard_map/ppermute | solution.py:589
  337.1 20.3 %collective-permute-start.27 = (bf16[128,2304]{1,0:T(8,128)(2,1)S(1)}, bf16[128,2304]{1,0:T(8,128)(2,1)S(1)}, u32[]{:S(2)}, u32[]{:S(2)}) collective-permute-start(bf16[128,2304]{1,0:T(8,128)(2,1)S(1)} %reduce-precision_convert_fusion.16.total_ref), channel_id=1, source_target_pairs={{1,0},{2,3},{5,4},{6,7},{9,8},{10,11},{13,12},{14,15},{17,16},{18,... | collective-permute-start | bytes 1769480 | tf_op jit(solution)/shard_map/ppermute | solution.py:589
  338.8 62.8 %collective-permute-start.33 = (bf16[512,2304]{1,0:T(8,128)(2,1)}, bf16[512,2304]{1,0:T(8,128)(2,1)}, u32[]{:S(2)}, u32[]{:S(2)}) collective-permute-start(bf16[512,2304]{1,0:T(8,128)(2,1)} %get-tuple-element.342), channel_id=1, source_target_pairs={{0,16},{16,0},{1,17},{17,1},{2,18},{18,2},{3,19},{19,3},{4,20},{20... | collective-permute-start | bytes 7077896 | tf_op jit(solution)/shard_map/ppermute | solution.py:676
  420.4 246.8 %reduce-scatter.5.cloned.1.call-start = ((), (), s32[]{:S(2)}) async-start(), calls=%async_computation.7 | async-start | bytes 13271040 | tf_op jit(solution)/shard_map/reduce_scatter | solution.py:699
  422.0 51.8 %collective-permute-start.37 = (bf16[512,4608]{1,0:T(8,128)(2,1)}, bf16[512,4608]{1,0:T(8,128)(2,1)}, u32[]{:S(2)}, u32[]{:S(2)}) collective-permute-start(bf16[512,4608]{1,0:T(8,128)(2,1)} %get-tuple-element.357), channel_id=1, source_target_pairs={{0,16},{16,0},{1,17},{17,1},{2,18},{18,2},{3,19},{19,3},{4,20},{20... | collective-permute-start | bytes 14155784 | tf_op jit(solution)/shard_map/ppermute | solution.py:676
  423.1 18.0 %collective-permute-start.31 = (bf16[128,2304]{1,0:T(8,128)(2,1)S(1)}, bf16[128,2304]{1,0:T(8,128)(2,1)S(1)}, u32[]{:S(2)}, u32[]{:S(2)}) collective-permute-start(bf16[128,2304]{1,0:T(8,128)(2,1)S(1)} %copy-done.57), channel_id=1, source_target_pairs={{0,1},{3,2},{4,5},{7,6},{8,9},{11,10},{12,13},{15,14},{16,17},{19,... | collective-permute-start | bytes 1769480 | tf_op jit(solution)/shard_map/ppermute | solution.py:573
  433.5 19.2 %collective-permute-start.28 = (bf16[128,2304]{1,0:T(8,128)(2,1)S(1)}, bf16[128,2304]{1,0:T(8,128)(2,1)S(1)}, u32[]{:S(2)}, u32[]{:S(2)}) collective-permute-start(bf16[128,2304]{1,0:T(8,128)(2,1)S(1)} %copy-done.56), channel_id=1, source_target_pairs={{0,1},{3,2},{4,5},{7,6},{8,9},{11,10},{12,13},{15,14},{16,17},{19,... | collective-permute-start | bytes 1769480 | tf_op jit(solution)/shard_map/ppermute | solution.py:573
  442.1 26.7 %collective-permute-start.38 = (bf16[128,2304]{1,0:T(8,128)(2,1)S(1)}, bf16[128,2304]{1,0:T(8,128)(2,1)S(1)}, u32[]{:S(2)}, u32[]{:S(2)}) collective-permute-start(bf16[128,2304]{1,0:T(8,128)(2,1)S(1)} %reduce-precision_convert_fusion.13.total_ref), channel_id=1, source_target_pairs={{1,0},{2,3},{5,4},{6,7},{9,8},{10,11},{13,12},{14,15},{17,16},{18,... | collective-permute-start | bytes 1769480 | tf_op jit(solution)/shard_map/ppermute | solution.py:589
  506.0 17.3 %collective-permute-start.41 = (bf16[128,2304]{1,0:T(8,128)(2,1)S(1)}, bf16[128,2304]{1,0:T(8,128)(2,1)S(1)}, u32[]{:S(2)}, u32[]{:S(2)}) collective-permute-start(bf16[128,2304]{1,0:T(8,128)(2,1)S(1)} %reduce-precision_convert_fusion.10), channel_id=1, source_target_pairs={{1,2},{2,1},{5,6},{6,5},{9,10},{10,9},{13,14},{14,13},{17,18},{18,... | collective-permute-start | bytes 1769480 | tf_op jit(solution)/shard_map/ppermute | solution.py:582
  506.9 23.3 %collective-permute-start.40 = (bf16[128,2304]{1,0:T(8,128)(2,1)S(1)}, bf16[128,2304]{1,0:T(8,128)(2,1)S(1)}, u32[]{:S(2)}, u32[]{:S(2)}) collective-permute-start(bf16[128,2304]{1,0:T(8,128)(2,1)S(1)} %reduce-precision_convert_fusion.9.total_ref), channel_id=1, source_target_pairs={{1,0},{2,3},{5,4},{6,7},{9,8},{10,11},{13,12},{14,15},{17,16},{18,... | collective-permute-start | bytes 1769480 | tf_op jit(solution)/shard_map/ppermute | solution.py:589
  526.7 24.4 %collective-permute-start.49 = (bf16[256,512]{1,0:T(8,128)(2,1)}, bf16[256,512]{1,0:T(8,128)(2,1)S(1)}, u32[]{:S(2)}, u32[]{:S(2)}) collective-permute-start(bf16[256,512]{1,0:T(8,128)(2,1)} %convert_element_type.422), channel_id=1, source_target_pairs={{0,12},{4,8},{8,4},{12,0},{1,13},{5,9},{9,5},{13,1},{2,14},{6,10},... | collective-permute-start | bytes 786440 | tf_op jit(solution)/shard_map/ppermute | solution.py:828
  528.5 22.7 %collective-permute-start.48 = (bf16[256,512]{1,0:T(8,128)(2,1)}, bf16[256,512]{1,0:T(8,128)(2,1)S(1)}, u32[]{:S(2)}, u32[]{:S(2)}) collective-permute-start(bf16[256,512]{1,0:T(8,128)(2,1)} %convert_element_type.421), channel_id=1, source_target_pairs={{0,8},{4,12},{8,0},{12,4},{1,9},{5,13},{9,1},{13,5},{2,10},{6,14},... | collective-permute-start | bytes 786440 | tf_op jit(solution)/shard_map/ppermute | solution.py:828
  529.7 22.5 %collective-permute-start.47 = (bf16[256,512]{1,0:T(8,128)(2,1)S(1)}, bf16[256,512]{1,0:T(8,128)(2,1)S(1)}, u32[]{:S(2)}, u32[]{:S(2)}) collective-permute-start(bf16[256,512]{1,0:T(8,128)(2,1)S(1)} %convert_element_type.420), channel_id=1, source_target_pairs={{0,4},{4,0},{8,12},{12,8},{1,5},{5,1},{9,13},{13,9},{2,6},{6,2},{1... | collective-permute-start | bytes 786440 | tf_op jit(solution)/shard_map/ppermute | solution.py:828
  561.9 35.6 %collective-permute-start.53 = (bf16[128,2304]{1,0:T(8,128)(2,1)S(1)}, bf16[128,2304]{1,0:T(8,128)(2,1)S(1)}, u32[]{:S(2)}, u32[]{:S(2)}) collective-permute-start(bf16[128,2304]{1,0:T(8,128)(2,1)S(1)} %copy-done.55), channel_id=1, source_target_pairs={{0,1},{3,2},{4,5},{7,6},{8,9},{11,10},{12,13},{15,14},{16,17},{19,... | collective-permute-start | bytes 1769480 | tf_op jit(solution)/shard_map/ppermute | solution.py:573
  569.7 17.9 %collective-permute-start.45 = (bf16[256,512]{1,0:T(8,128)(2,1)S(1)}, bf16[256,512]{1,0:T(8,128)(2,1)S(1)}, u32[]{:S(2)}, u32[]{:S(2)}) collective-permute-start(bf16[256,512]{1,0:T(8,128)(2,1)S(1)} %convert_element_type.418), channel_id=1, source_target_pairs={{0,8},{4,12},{8,0},{12,4},{1,9},{5,13},{9,1},{13,5},{2,10},{6,14},... | collective-permute-start | bytes 786440 | tf_op jit(solution)/shard_map/ppermute | solution.py:828
  572.7 15.7 %collective-permute-start.44 = (bf16[256,512]{1,0:T(8,128)(2,1)S(1)}, bf16[256,512]{1,0:T(8,128)(2,1)S(1)}, u32[]{:S(2)}, u32[]{:S(2)}) collective-permute-start(bf16[256,512]{1,0:T(8,128)(2,1)S(1)} %convert_element_type.417), channel_id=1, source_target_pairs={{0,4},{4,0},{8,12},{12,8},{1,5},{5,1},{9,13},{13,9},{2,6},{6,2},{1... | collective-permute-start | bytes 786440 | tf_op jit(solution)/shard_map/ppermute | solution.py:828
  573.3 26.2 %collective-permute-start.55 = (bf16[128,2304]{1,0:T(8,128)(2,1)S(1)}, bf16[128,2304]{1,0:T(8,128)(2,1)}, u32[]{:S(2)}, u32[]{:S(2)}) collective-permute-start(bf16[128,2304]{1,0:T(8,128)(2,1)S(1)} %copy-done.54), channel_id=1, source_target_pairs={{0,1},{3,2},{4,5},{7,6},{8,9},{11,10},{12,13},{15,14},{16,17},{19,... | collective-permute-start | bytes 1769480 | tf_op jit(solution)/shard_map/ppermute | solution.py:573
  595.3 24.9 %collective-permute-start.58 = (bf16[128,2304]{1,0:T(8,128)(2,1)}, bf16[128,2304]{1,0:T(8,128)(2,1)}, u32[]{:S(2)}, u32[]{:S(2)}) collective-permute-start(bf16[128,2304]{1,0:T(8,128)(2,1)} %get-tuple-element.442), channel_id=1, source_target_pairs={{0,1},{3,2},{4,5},{7,6},{8,9},{11,10},{12,13},{15,14},{16,17},{19,... | collective-permute-start | bytes 1769480 | tf_op jit(solution)/shard_map/ppermute | solution.py:573
  603.6 19.3 %collective-permute-start.57 = (bf16[128,2304]{1,0:T(8,128)(2,1)S(1)}, bf16[128,2304]{1,0:T(8,128)(2,1)}, u32[]{:S(2)}, u32[]{:S(2)}) collective-permute-start(bf16[128,2304]{1,0:T(8,128)(2,1)S(1)} %reduce-precision_convert_fusion.6), channel_id=1, source_target_pairs={{1,2},{2,1},{5,6},{6,5},{9,10},{10,9},{13,14},{14,13},{17,18},{18,... | collective-permute-start | bytes 1769480 | tf_op jit(solution)/shard_map/ppermute | solution.py:582
  605.0 28.2 %collective-permute-start.52 = (bf16[128,2304]{1,0:T(8,128)(2,1)}, bf16[128,2304]{1,0:T(8,128)(2,1)}, u32[]{:S(2)}, u32[]{:S(2)}) collective-permute-start(bf16[128,2304]{1,0:T(8,128)(2,1)} %get-tuple-element.449), channel_id=1, source_target_pairs={{0,1},{3,2},{4,5},{7,6},{8,9},{11,10},{12,13},{15,14},{16,17},{19,... | collective-permute-start | bytes 1769480 | tf_op jit(solution)/shard_map/ppermute | solution.py:573
  609.8 20.5 %collective-permute-start.56 = (bf16[128,2304]{1,0:T(8,128)(2,1)S(1)}, bf16[128,2304]{1,0:T(8,128)(2,1)}, u32[]{:S(2)}, u32[]{:S(2)}) collective-permute-start(bf16[128,2304]{1,0:T(8,128)(2,1)S(1)} %reduce-precision_convert_fusion.5.total_ref), channel_id=1, source_target_pairs={{1,0},{2,3},{5,4},{6,7},{9,8},{10,11},{13,12},{14,15},{17,16},{18,... | collective-permute-start | bytes 1769480 | tf_op jit(solution)/shard_map/ppermute | solution.py:589
  622.9 49.3 %all-to-all-start = ((bf16[4,288,1664]{2,1,0:T(8,128)(2,1)}), bf16[4,288,1664]{2,1,0:T(8,128)(2,1)}, u32[]{:S(2)}, u32[]{:S(2)}) async-start(bf16[4,288,1664]{2,1,0:T(8,128)(2,1)} %bitcast.77), calls=%async_computation.1 | async-start | bytes 7667712 | tf_op jit(solution)/shard_map/all_to_all | solution.py:690
  628.9 21.9 %collective-permute-start.62 = (bf16[128,2304]{1,0:T(8,128)(2,1)S(1)}, bf16[128,2304]{1,0:T(8,128)(2,1)S(1)}, u32[]{:S(2)}, u32[]{:S(2)}) collective-permute-start(bf16[128,2304]{1,0:T(8,128)(2,1)S(1)} %reduce-precision_convert_fusion.3.refs_1_), channel_id=1, source_target_pairs={{1,0},{2,3},{5,4},{6,7},{9,8},{10,11},{13,12},{14,15},{17,16},{18,... | collective-permute-start | bytes 1769480 | tf_op jit(solution)/shard_map/ppermute | solution.py:589
  634.7 19.9 %collective-permute-start.61 = (bf16[128,2304]{1,0:T(8,128)(2,1)S(1)}, bf16[128,2304]{1,0:T(8,128)(2,1)}, u32[]{:S(2)}, u32[]{:S(2)}) collective-permute-start(bf16[128,2304]{1,0:T(8,128)(2,1)S(1)} %reduce-precision_convert_fusion.2), channel_id=1, source_target_pairs={{1,2},{2,1},{5,6},{6,5},{9,10},{10,9},{13,14},{14,13},{17,18},{18,... | collective-permute-start | bytes 1769480 | tf_op jit(solution)/shard_map/ppermute | solution.py:582
  637.4 26.1 %collective-permute-start.65 = (bf16[128,2304]{1,0:T(8,128)(2,1)S(1)}, bf16[128,2304]{1,0:T(8,128)(2,1)S(1)}, u32[]{:S(2)}, u32[]{:S(2)}) collective-permute-start(bf16[128,2304]{1,0:T(8,128)(2,1)S(1)} %reduce-precision_convert_fusion.1.refs_1_), channel_id=1, source_target_pairs={{1,0},{2,3},{5,4},{6,7},{9,8},{10,11},{13,12},{14,15},{17,16},{18,... | collective-permute-start | bytes 1769480 | tf_op jit(solution)/shard_map/ppermute | solution.py:589
  655.8 29.2 %collective-permute-start.64 = (bf16[128,2304]{1,0:T(8,128)(2,1)S(1)}, bf16[128,2304]{1,0:T(8,128)(2,1)S(1)}, u32[]{:S(2)}, u32[]{:S(2)}) collective-permute-start(bf16[128,2304]{1,0:T(8,128)(2,1)S(1)} %reduce-precision_convert_fusion.refs_1_), channel_id=1, source_target_pairs={{1,0},{2,3},{5,4},{6,7},{9,8},{10,11},{13,12},{14,15},{17,16},{18,... | collective-permute-start | bytes 1769480 | tf_op jit(solution)/shard_map/ppermute | solution.py:589
  (114 other events, 1104.0 us)
Sparse Core Ops, SparseCore 0:
  11.3 53.9 all-gather.2
  67.2 175.9 all-gather.4
  420.5 61.8 reduce-scatter.2
  492.5 120.1 reduce-scatter.4
